TPU v7x, 512 devices: a whole 4x4x16 slice. The times are simulated.
512 devices in a mesh: patch: 128 (over y, z, core), trial: 4 (over x).
Axes of the slice: x: 4, y: 4, z: 16, core: 2. Of those that a mesh axis runs over, the one named last changes fastest.
Arguments:
- activity: float32 [32, 524288], P('trial', 'patch'), may hold values from 0 to 1
- history: bfloat16 [7, 32, 524288], P(None, 'trial', 'patch'), may hold values from 0 to 1
- drive: float32 [524288], P('patch'), may hold values from -6 to 6
- slope: float32 [32], P('trial'), may hold values from 0.5 to 2
- strength: float32 [32], P('trial'), may hold values from 0.1 to 1
- kernel: bfloat16 [4096, 4, 128, 128], P('patch', 'trial'), may hold values from -0.25 to 0.25
- kernel_index: int32 [4096, 4], P('patch'), may hold values from 0 to 33, as said below
- tract_source: int32 [16384], P('patch'), may hold values from 0 to 31
- tract_delay: int32 [16384], P('patch'), may hold values from 4 to 7
- tract_target: int32 [16384, 1], P('patch'), may hold values from 0 to 127; in each aligned block of 128 rows (0 to 127, 128 to 255, ...) at most 2 rows name the same one
- tract_block: int32 [16384], P('patch'), may hold values from 0 to 31
- tract_weight: float32 [16384], P('patch'), may hold values from 0.25 to 2
- voxel_owner: int32 [524288], P('patch'), may hold values from 0 to 16351, as said below
- vaso_signal: float32 [32, 16384], P('trial', 'patch'), may hold values from -3 to 3
- blood_flow: float32 [32, 16384], P('trial', 'patch'), may hold values from 0.5 to 1.5
Outputs:
- activity_out: float32 [32, 524288], P('trial', 'patch')
- vaso_out: float32 [32, 16384], P('trial', 'patch')
- flow_out: float32 [32, 16384], P('trial', 'patch')
Inputs may be any that keep to these rules, and one draw needn't show every extreme that they name: `kernel_index`: block b of a patch lists itself (entry b + 1) first; its other entries name b, b + 1 or b + 2; block 0's second entry is 0 and the last block's third entry is 33. `tract_target`: among the 128 tracts of one patch no target patch is named more than 2 times. `voxel_owner`: A vertex of patch p lies in a voxel owned by patch p - 1, p or p + 1, where patch p owns voxels p * 128 to (p + 1) * 128 - 1; the last quarter of each patch's voxels hold no vertex.
All inputs are finite; a program needn't handle non-finite values.
Results may differ from a plain program's by a relative error of at most 0.00037.
Values may be sent and summed in bfloat16 or wider, within the bound.
No kernel may reach another device: no remote copies, remote signals or barrier semaphores. Data moves between devices by JAX's collectives and lax.ppermute only.
A program may use at most 64 MiB of HBM per device.

v0:
```python
import jax
import jax.numpy as jnp
from jax import lax
from jax.sharding import PartitionSpec as P

BLOCK = 128
STEPS = 4
HIST = 7


def extended_2(array, sides, width):
    for axis, dim in sides:
        peers, length = (lax.axis_size(axis), array.shape[dim])
        up = [(i, (i + 1) % peers) for i in range(peers - 1)]
        down = [(j, i) for i, j in up]
        last = lax.slice_in_dim(array, length - width, length, axis=dim)
        leading = lax.slice_in_dim(array, 0, width, axis=dim)
        before = lax.ppermute(last, axis, up)
        after = lax.ppermute(leading, axis, down)
        array = jnp.concatenate([before, array, after], axis=dim)
    return array


def shards(
    activity,
    history,
    drive,
    slope,
    strength,
    kernel,
    kernel_index,
    tract_source,
    tract_delay,
    tract_target,
    tract_block,
    tract_weight,
    voxel_owner,
    vaso_signal,
    blood_flow,
):
    trials_here = activity.shape[0]
    verts = activity.shape[1]
    nblk = verts // BLOCK
    patches = lax.axis_size("patch")
    tracts_here = tract_source.shape[0]
    capacity = max(2, tracts_here // patches + 1)
    slots = patches * capacity
    voxels_here = vaso_signal.shape[1]
    hist_blocks = history.reshape(HIST, trials_here, nblk, BLOCK)
    lag = tract_delay[:, None] - jnp.arange(STEPS, dtype=jnp.int32)[None, :] - 1
    rows = hist_blocks[lag, :, tract_source[:, None], :]
    weighted = (rows.astype(jnp.float32) * tract_weight[:, None, None, None]).astype(jnp.bfloat16)
    target = tract_target[:, 0]
    order = jnp.arange(tracts_here, dtype=jnp.int32)
    same = (target[:, None] == target[None, :]) & (order[None, :] < order[:, None])
    rank = jnp.sum(same.astype(jnp.int32), axis=1)
    slot = target * capacity + rank
    send_rates = jnp.zeros((slots, STEPS, trials_here, BLOCK), jnp.bfloat16).at[slot].set(weighted)
    send_blocks = jnp.full((slots,), -1, jnp.int32).at[slot].set(tract_block)
    got_rates, got_blocks = (
        lax.all_to_all(send_rates, "patch", split_axis=0, concat_axis=0, tiled=True),
        lax.all_to_all(send_blocks, "patch", split_axis=0, concat_axis=0, tiled=True),
    )
    onehot = (got_blocks[None, :] == jnp.arange(nblk, dtype=jnp.int32)[:, None]).astype(
        jnp.bfloat16
    )
    coupling = jnp.einsum("bs,sxtj->xtbj", onehot, got_rates, preferred_element_type=jnp.float32)
    coupling = coupling.reshape(STEPS, trials_here, verts)
    tiles = lax.all_gather(kernel, "trial", axis=1, tiled=True)
    rate = activity
    recorded = []
    for step in range(STEPS):
        rate_b = rate.astype(jnp.bfloat16)
        extended = extended_2(rate_b, (("patch", 1),), BLOCK)
        extended = extended.reshape(trials_here, nblk + 2, BLOCK)
        picked = extended[:, kernel_index]
        local = jnp.einsum("tbki,bkij->tbj", picked, tiles, preferred_element_type=jnp.float32)
        local = local.reshape(trials_here, verts)
        pre = slope[:, None] * (local + strength[:, None] * coupling[step] + drive[None, :])
        rate = rate + 0.5 * (jax.nn.sigmoid(pre) - rate)
        recorded.append(rate)
    values = jnp.concatenate(
        [
            jnp.stack(recorded).reshape(STEPS * trials_here, verts),
            jnp.ones((1, verts), jnp.float32),
        ],
        axis=0,
    )
    offset = (lax.axis_index("patch") - 1) * voxels_here
    partial_value = (
        jnp.zeros((values.shape[0], 3 * voxels_here), jnp.float32)
        .at[:, voxel_owner - offset]
        .add(values)
    )
    widened = extended_2(partial_value, (("patch", 1),), voxels_here)
    mine = (
        widened[:, :voxels_here]
        + widened[:, 2 * voxels_here : 3 * voxels_here]
        + widened[:, 4 * voxels_here :]
    )
    floor = jnp.maximum(mine[-1], 1.0)
    levels = mine[:-1].reshape(STEPS, trials_here, voxels_here) / floor[None, None, :]
    vaso = vaso_signal
    flow = blood_flow
    for step in range(STEPS):
        vaso = vaso + 0.5 * (levels[step] - 0.65 * vaso - 0.41 * (flow - 1.0))
        flow = flow + 0.5 * vaso
    return (rate, vaso, flow)


def solution(mesh):
    placed = (
        P("trial", "patch"),
        P(None, "trial", "patch"),
        P("patch"),
        P("trial"),
        P("trial"),
        P("patch", "trial", None, None),
        P("patch", None),
        P("patch"),
        P("patch"),
        P("patch", None),
        P("patch"),
        P("patch"),
        P("patch"),
        P("trial", "patch"),
        P("trial", "patch"),
    )
    return jax.shard_map(
        shards,
        mesh=mesh,
        in_specs=placed,
        out_specs=(P("trial", "patch"), P("trial", "patch"), P("trial", "patch")),
        check_vma=False,
    )
```

profile of v0, /device:TPU:24, one launch (start us, length us, event | category | flops | bytes accessed | tf_op | source)
XLA Modules:
  0.0 245.7 jit_solution(5393697009876018720)
XLA Ops:
  10.6 19.8 %all-to-all-start.1 = ((s32[128,2,1]{1,2,0:T(1,128)}), s32[128,2,1]{1,2,0:T(1,128)S(1)}, u32[]{:S(2)}, u32[]{:S(2)}) async-start(s32[128,2,1]{1,2,0:T(1,128)} %bitcast.12), calls=%async_computation.1 | async-start | bytes 131072 | tf_op jit(solution)/shard_map/all_to_all | solution.py:62
  32.0 2.3 gather_fusion.1
  36.2 13.7 %scatter_fusion = bf16[256,4,8,128]{3,2,1,0:T(8,128)(2,1)} fusion(bf16[256,4,8,128]{3,2,1,0:T(8,128)(2,1)} %broadcast_in_dim.13, s32[128]{0:T(128)S(1)} %fusion.75, bf16[128,4,8,128]{3,2,1,0:T(8,128)(2,1)S(1)} %fusion.40), kind=kCustom, calls=%fused_computation.5 | custom fusion | bytes 3146240 | tf_op jit(solution)/shard_map/scatter | solution.py:58
  49.9 16.3 %all-to-all-start = ((bf16[256,4,8,128]{3,2,1,0:T(8,128)(2,1)}), bf16[256,4,8,128]{3,2,1,0:T(8,128)(2,1)S(1)}, u32[]{:S(2)}, u32[]{:S(2)}) async-start(bf16[256,4,8,128]{3,2,1,0:T(8,128)(2,1)} %scatter_fusion), calls=%async_computation | async-start | bytes 4194304 | tf_op jit(solution)/shard_map/all_to_all | solution.py:61
  67.0 4.6 %collective-permute-start.1 = (bf16[8,128]{1,0:T(8,128)(2,1)S(1)}, bf16[8,128]{1,0:T(8,128)(2,1)S(1)}, u32[]{:S(2)}, u32[]{:S(2)}) collective-permute-start(bf16[8,128]{1,0:T(8,128)(2,1)S(1)} %get-tuple-element.18), channel_id=1, source_target_pairs={{4,0},{8,4},{12,8},{16,12},{20,16},{24,20},{28,24},{32,28},{36,32}... | collective-permute-start | bytes 6152 | tf_op jit(solution)/shard_map/ppermute | solution.py:19
  71.7 1.9 collective-permute-start
  73.8 78.1 %collective-permute-done.1 = bf16[8,128]{1,0:T(8,128)(2,1)S(1)} collective-permute-done((bf16[8,128]{1,0:T(8,128)(2,1)S(1)}, bf16[8,128]{1,0:T(8,128)(2,1)S(1)}, u32[]{:S(2)}, u32[]{:S(2)}) %collective-permute-start.1) | collective-permute-done | bytes 2080 | tf_op jit(solution)/shard_map/ppermute | solution.py:19
  151.9 3.3 %collective-permute-done = bf16[8,128]{1,0:T(8,128)(2,1)S(1)} collective-permute-done((bf16[8,128]{1,0:T(8,128)(2,1)S(1)}, bf16[8,128]{1,0:T(8,128)(2,1)S(1)}, u32[]{:S(2)}, u32[]{:S(2)}) %collective-permute-start) | collective-permute-done | bytes 2080 | tf_op jit(solution)/shard_map/ppermute | solution.py:18
  157.4 6.4 %all-to-all-done = bf16[256,4,8,128]{3,2,1,0:T(8,128)(2,1)S(1)} async-done(((bf16[256,4,8,128]{3,2,1,0:T(8,128)(2,1)}), bf16[256,4,8,128]{3,2,1,0:T(8,128)(2,1)S(1)}, u32[]{:S(2)}, u32[]{:S(2)}) %all-to-all-start) | async-done | bytes 2097184 | tf_op jit(solution)/shard_map/all_to_all | solution.py:61
  164.6 2.9 %fusion.86 = (bf16[8,4096]{1,0:T(8,128)(2,1)S(1)}, f32[8,4096]{1,0:T(8,128)S(1)}) fusion(f32[8,4096]{1,0:T(8,128)S(1)} %copy-done.1, f32[4096]{0:T(1024)S(1)} %copy-done.3, f32[1,8,32,128]{3,2,1,0:T(8,128)S(1)} %get-tuple-element.8, f32[8]{0:T(128)S(1)} %copy-done.5, bf16[8,32,4,128]{3,0,2,1:T(8,128)(2,1)S(1)} %bitcast.266, ...), kind=kOutput, calls=%fused_computation.129 | convolution fusion | flops 33914880 | bytes 4931648 | tf_op jit(solution)/shard_map/tbki,bkij->tbj/dot_general | solution.py:77
  167.5 1.9 collective-permute-start.3
  169.4 2.4 collective-permute-start.2
  171.8 4.6 %collective-permute-done.2 = bf16[8,128]{1,0:T(8,128)(2,1)S(1)} collective-permute-done((bf16[8,128]{1,0:T(8,128)(2,1)S(1)}, bf16[8,128]{1,0:T(8,128)(2,1)S(1)}, u32[]{:S(2)}, u32[]{:S(2)}) %collective-permute-start.2) | collective-permute-done | bytes 2080 | tf_op jit(solution)/shard_map/ppermute | solution.py:18
  177.1 2.9 %fusion.87 = (bf16[8,4096]{1,0:T(8,128)(2,1)S(1)}, f32[8,4096]{1,0:T(8,128)S(1)}) fusion(f32[8,4096]{1,0:T(8,128)S(1)} %get-tuple-element.20, f32[4096]{0:T(1024)S(1)} %copy-done.3, f32[1,8,32,128]{3,2,1,0:T(8,128)S(1)} %get-tuple-element.7, f32[8]{0:T(128)S(1)} %copy-done.5, bf16[8,32,4,128]{3,0,2,1:T(8,128)(2,1)S(1)} %bitcast.268, ...), kind=kOutput, calls=%fused_computation.130 | convolution fusion | flops 33914880 | bytes 4931648 | tf_op jit(solution)/shard_map/tbki,bkij->tbj/dot_general | solution.py:77
  180.0 1.9 collective-permute-start.5
  182.0 2.4 collective-permute-start.4
  184.4 4.6 %collective-permute-done.4 = bf16[8,128]{1,0:T(8,128)(2,1)S(1)} collective-permute-done((bf16[8,128]{1,0:T(8,128)(2,1)S(1)}, bf16[8,128]{1,0:T(8,128)(2,1)S(1)}, u32[]{:S(2)}, u32[]{:S(2)}) %collective-permute-start.4) | collective-permute-done | bytes 2080 | tf_op jit(solution)/shard_map/ppermute | solution.py:18
  189.7 2.9 %fusion.88 = (bf16[8,4096]{1,0:T(8,128)(2,1)S(1)}, f32[8,4096]{1,0:T(8,128)S(1)}) fusion(f32[8,4096]{1,0:T(8,128)S(1)} %get-tuple-element.22, f32[4096]{0:T(1024)S(1)} %copy-done.3, f32[1,8,32,128]{3,2,1,0:T(8,128)S(1)} %get-tuple-element.6, f32[8]{0:T(128)S(1)} %copy-done.5, bf16[8,32,4,128]{3,0,2,1:T(8,128)(2,1)S(1)} %bitcast.269, ...), kind=kOutput, calls=%fused_computation.131 | convolution fusion | flops 33914880 | bytes 4931648 | tf_op jit(solution)/shard_map/tbki,bkij->tbj/dot_general | solution.py:77
  194.5 2.6 %collective-permute-start.6 = (bf16[8,128]{1,0:T(8,128)(2,1)S(1)}, bf16[8,128]{1,0:T(8,128)(2,1)S(1)}, u32[]{:S(2)}, u32[]{:S(2)}) collective-permute-start(bf16[8,128]{1,0:T(8,128)(2,1)S(1)} %get-tuple-element.11), channel_id=1, source_target_pairs={{0,4},{4,8},{8,12},{12,16},{16,20},{20,24},{24,28},{28,32},{32,36}... | collective-permute-start | bytes 6152 | tf_op jit(solution)/shard_map/ppermute | solution.py:18
  197.2 4.4 %collective-permute-done.6 = bf16[8,128]{1,0:T(8,128)(2,1)S(1)} collective-permute-done((bf16[8,128]{1,0:T(8,128)(2,1)S(1)}, bf16[8,128]{1,0:T(8,128)(2,1)S(1)}, u32[]{:S(2)}, u32[]{:S(2)}) %collective-permute-start.6) | collective-permute-done | bytes 2080 | tf_op jit(solution)/shard_map/ppermute | solution.py:18
  202.3 2.9 %fusion.9 = f32[8,4096]{1,0:T(8,128)S(1)} fusion(f32[8,4096]{1,0:T(8,128)S(1)} %get-tuple-element.24, bf16[8,32,4,128]{3,0,2,1:T(8,128)(2,1)S(1)} %bitcast.267, bf16[32,4,128,128]{3,2,1,0:T(8,128)(2,1)} %all-gather.2.cloned.1.call-done, f32[1,8,32,128]{3,2,1,0:T(8,128)S(1)} %get-tuple-element.5, f32[4096]{0:T(1024)S(1)} %copy-done.3, f32[8]{0:T(128)S(1)} %copy-done.5, ...), kind=kOutput, calls=%fused_computation.18 | convolution fusion | flops 33882112 | bytes 4866112 | tf_op jit(solution)/shard_map/tbki,bkij->tbj/dot_general | solution.py:77
  205.8 22.5 %scatter_custom_fusion.2 = f32[33,384]{0,1:T(8,128)S(1)} fusion(s32[4096]{0:T(1024)S(1)} %compare_select_fusion.1, f32[32,4096]{0,1:T(8,128)S(1)} %copy.33, f32[]{:T(128)} %constant.18.clone.1, f32[]{:T(128)} %constant.9.clone.1), kind=kCustom, calls=%fused_computation.54 | custom fusion | flops 135168 | bytes 2147848 | tf_op jit(solution)/shard_map/scatter-add | solution.py:93
  230.3 2.4 collective-permute-start.8
  232.7 5.3 %collective-permute-done.8 = f32[33,128]{0,1:T(8,128)S(1)} collective-permute-done((f32[33,128]{0,1:T(8,128)S(1)}, f32[33,128]{0,1:T(8,128)S(1)}, u32[]{:S(2)}, u32[]{:S(2)}) %collective-permute-start.8) | collective-permute-done | bytes 16928 | tf_op jit(solution)/shard_map/ppermute | solution.py:18
  (72 shorter events, 18.3 us)
Async XLA Ops:
  7.2 24.8 %copy-start = (bf16[7,8,4096]{2,1,0:T(8,128)(2,1)S(1)}, bf16[7,8,4096]{2,1,0:T(8,128)(2,1)}, u32[]{:S(2)}) copy-start(bf16[7,8,4096]{2,1,0:T(8,128)(2,1)} %param.16) | copy-start | bytes 1376260
  7.2 27.1 %copy-start.10 = (f32[128]{0:T(128)S(1)}, f32[128]{0:T(128)}, u32[]{:S(2)}) copy-start(f32[128]{0:T(128)} %param.26) | copy-start | bytes 1540
  10.6 39.3 %all-to-all-start.1 = ((s32[128,2,1]{1,2,0:T(1,128)}), s32[128,2,1]{1,2,0:T(1,128)S(1)}, u32[]{:S(2)}, u32[]{:S(2)}) async-start(s32[128,2,1]{1,2,0:T(1,128)} %bitcast.12), calls=%async_computation.1 | async-start | bytes 131072 | tf_op jit(solution)/shard_map/all_to_all | solution.py:62
  49.9 17.1 %copy-start.1 = (f32[8,4096]{1,0:T(8,128)S(1)}, f32[8,4096]{1,0:T(8,128)}, u32[]{:S(2)}) copy-start(f32[8,4096]{1,0:T(8,128)} %param.15) | copy-start | bytes 393220
  49.9 23.7 %copy-start.9 = (s32[32,4]{0,1:T(4,128)S(1)}, s32[32,4]{0,1:T(4,128)}, u32[]{:S(2)}) copy-start(s32[32,4]{0,1:T(4,128)} %param.21) | copy-start | bytes 1540
  49.9 113.8 %all-to-all-start = ((bf16[256,4,8,128]{3,2,1,0:T(8,128)(2,1)}), bf16[256,4,8,128]{3,2,1,0:T(8,128)(2,1)S(1)}, u32[]{:S(2)}, u32[]{:S(2)}) async-start(bf16[256,4,8,128]{3,2,1,0:T(8,128)(2,1)} %scatter_fusion), calls=%async_computation | async-start | bytes 4194304 | tf_op jit(solution)/shard_map/all_to_all | solution.py:61
  66.3 98.3 %all-gather.2.cloned.1.call-start = ((), (), s32[]{:S(2)}) async-start(), calls=%async_computation.2 | async-start | bytes 5242880 | tf_op jit(solution)/shard_map/all_gather | solution.py:69
  67.0 84.9 %collective-permute-start.1 = (bf16[8,128]{1,0:T(8,128)(2,1)S(1)}, bf16[8,128]{1,0:T(8,128)(2,1)S(1)}, u32[]{:S(2)}, u32[]{:S(2)}) collective-permute-start(bf16[8,128]{1,0:T(8,128)(2,1)S(1)} %get-tuple-element.18), channel_id=1, source_target_pairs={{4,0},{8,4},{12,8},{16,12},{20,16},{24,20},{28,24},{32,28},{36,32}... | collective-permute-start | bytes 6152 | tf_op jit(solution)/shard_map/ppermute | solution.py:19
  71.7 83.5 %collective-permute-start = (bf16[8,128]{1,0:T(8,128)(2,1)S(1)}, bf16[8,128]{1,0:T(8,128)(2,1)S(1)}, u32[]{:S(2)}, u32[]{:S(2)}) collective-permute-start(bf16[8,128]{1,0:T(8,128)(2,1)S(1)} %get-tuple-element.17), channel_id=1, source_target_pairs={{0,4},{4,8},{8,12},{12,16},{16,20},{20,24},{24,28},{28,32},{32,36}... | collective-permute-start | bytes 6152 | tf_op jit(solution)/shard_map/ppermute | solution.py:18
  155.2 9.3 %copy-start.3 = (f32[4096]{0:T(1024)S(1)}, f32[4096]{0:T(1024)}, u32[]{:S(2)}) copy-start(f32[4096]{0:T(1024)} %param.17) | copy-start | bytes 49156
  155.2 9.3 %copy-start.5 = (f32[8]{0:T(128)S(1)}, f32[8]{0:T(128)}, u32[]{:S(2)}) copy-start(f32[8]{0:T(128)} %param.19) | copy-start | bytes 100
  155.2 9.3 %copy-start.6 = (f32[8]{0:T(128)S(1)}, f32[8]{0:T(128)}, u32[]{:S(2)}) copy-start(f32[8]{0:T(128)} %param.18) | copy-start | bytes 100
  167.5 4.3 %collective-permute-start.3 = (bf16[8,128]{1,0:T(8,128)(2,1)S(1)}, bf16[8,128]{1,0:T(8,128)(2,1)S(1)}, u32[]{:S(2)}, u32[]{:S(2)}) collective-permute-start(bf16[8,128]{1,0:T(8,128)(2,1)S(1)} %get-tuple-element.16), channel_id=1, source_target_pairs={{4,0},{8,4},{12,8},{16,12},{20,16},{24,20},{28,24},{32,28},{36,32}... | collective-permute-start | bytes 6152 | tf_op jit(solution)/shard_map/ppermute | solution.py:19
  169.4 7.0 %collective-permute-start.2 = (bf16[8,128]{1,0:T(8,128)(2,1)S(1)}, bf16[8,128]{1,0:T(8,128)(2,1)S(1)}, u32[]{:S(2)}, u32[]{:S(2)}) collective-permute-start(bf16[8,128]{1,0:T(8,128)(2,1)S(1)} %get-tuple-element.15), channel_id=1, source_target_pairs={{0,4},{4,8},{8,12},{12,16},{16,20},{20,24},{24,28},{28,32},{32,36}... | collective-permute-start | bytes 6152 | tf_op jit(solution)/shard_map/ppermute | solution.py:18
  180.0 4.4 %collective-permute-start.5 = (bf16[8,128]{1,0:T(8,128)(2,1)S(1)}, bf16[8,128]{1,0:T(8,128)(2,1)S(1)}, u32[]{:S(2)}, u32[]{:S(2)}) collective-permute-start(bf16[8,128]{1,0:T(8,128)(2,1)S(1)} %get-tuple-element.14), channel_id=1, source_target_pairs={{4,0},{8,4},{12,8},{16,12},{20,16},{24,20},{28,24},{32,28},{36,32}... | collective-permute-start | bytes 6152 | tf_op jit(solution)/shard_map/ppermute | solution.py:19
  182.0 7.0 %collective-permute-start.4 = (bf16[8,128]{1,0:T(8,128)(2,1)S(1)}, bf16[8,128]{1,0:T(8,128)(2,1)S(1)}, u32[]{:S(2)}, u32[]{:S(2)}) collective-permute-start(bf16[8,128]{1,0:T(8,128)(2,1)S(1)} %get-tuple-element.13), channel_id=1, source_target_pairs={{0,4},{4,8},{8,12},{12,16},{16,20},{20,24},{24,28},{28,32},{32,36}... | collective-permute-start | bytes 6152 | tf_op jit(solution)/shard_map/ppermute | solution.py:18
  189.7 7.5 %copy-start.4 = (s32[4096]{0:T(1024)S(1)}, s32[4096]{0:T(1024)}, u32[]{:S(2)}) copy-start(s32[4096]{0:T(1024)} %param.27) | copy-start | bytes 49156
  192.6 4.6 %collective-permute-start.7 = (bf16[8,128]{1,0:T(8,128)(2,1)S(1)}, bf16[8,128]{1,0:T(8,128)(2,1)S(1)}, u32[]{:S(2)}, u32[]{:S(2)}) collective-permute-start(bf16[8,128]{1,0:T(8,128)(2,1)S(1)} %get-tuple-element.12), channel_id=1, source_target_pairs={{4,0},{8,4},{12,8},{16,12},{20,16},{24,20},{28,24},{32,28},{36,32}... | collective-permute-start | bytes 6152 | tf_op jit(solution)/shard_map/ppermute | solution.py:19
  194.5 7.0 %collective-permute-start.6 = (bf16[8,128]{1,0:T(8,128)(2,1)S(1)}, bf16[8,128]{1,0:T(8,128)(2,1)S(1)}, u32[]{:S(2)}, u32[]{:S(2)}) collective-permute-start(bf16[8,128]{1,0:T(8,128)(2,1)S(1)} %get-tuple-element.11), channel_id=1, source_target_pairs={{0,4},{4,8},{8,12},{12,16},{16,20},{20,24},{24,28},{28,32},{32,36}... | collective-permute-start | bytes 6152 | tf_op jit(solution)/shard_map/ppermute | solution.py:18
  205.2 23.1 %copy-start.2 = (f32[8,4096]{1,0:T(8,128)}, f32[8,4096]{1,0:T(8,128)S(1)}, u32[]{:S(2)}) copy-start(f32[8,4096]{1,0:T(8,128)S(1)} %fusion.9) | copy-start | bytes 393220
  205.8 32.4 %copy-start.7 = (f32[8,128]{1,0:T(8,128)S(1)}, f32[8,128]{1,0:T(8,128)}, u32[]{:S(2)}) copy-start(f32[8,128]{1,0:T(8,128)} %param.29) | copy-start | bytes 12292
  205.8 32.4 %copy-start.8 = (f32[8,128]{1,0:T(8,128)S(1)}, f32[8,128]{1,0:T(8,128)}, u32[]{:S(2)}) copy-start(f32[8,128]{1,0:T(8,128)} %param.28) | copy-start | bytes 12292
  228.3 4.3 %collective-permute-start.9 = (f32[33,128]{0,1:T(8,128)S(1)}, f32[33,128]{0,1:T(8,128)S(1)}, u32[]{:S(2)}, u32[]{:S(2)}) collective-permute-start(f32[33,128]{0,1:T(8,128)S(1)} %get-tuple-element.10), channel_id=1, source_target_pairs={{4,0},{8,4},{12,8},{16,12},{20,16},{24,20},{28,24},{32,28},{36,32}... | collective-permute-start | bytes 50696 | tf_op jit(solution)/shard_map/ppermute | solution.py:19
  230.3 7.7 %collective-permute-start.8 = (f32[33,128]{0,1:T(8,128)S(1)}, f32[33,128]{0,1:T(8,128)S(1)}, u32[]{:S(2)}, u32[]{:S(2)}) collective-permute-start(f32[33,128]{0,1:T(8,128)S(1)} %get-tuple-element.9), channel_id=1, source_target_pairs={{0,4},{4,8},{8,12},{12,16},{16,20},{20,24},{24,28},{28,32},{32,36}... | collective-permute-start | bytes 50696 | tf_op jit(solution)/shard_map/ppermute | solution.py:18
Sparse Core Ops, SparseCore 0:
  69.2 56.4 all-gather.1
where the time goes:
time: 248 us; the launch traced here: 246 us
  waiting for transfers between devices  107 us (43%)
  starting transfers between devices  60.2 us (24%)
  other arithmetic  27.4 us (11%)
  local copies, waits for them, and re-layouts  24 us (10%)
  between operations  14.5 us (6%)
  matrix products  12.3 us (5%)
    ppermute x5, waiting for transfers between devices, extended_2(): after = lax.ppermute(leading, axis, down)  78.1 us
    scatter-add x1, other arithmetic, shards(): partial_value = jnp.zeros((values.shape[0], 3 * voxels_here), jnp.float32...  22.5 us
    ppermute x5, waiting for transfers between devices, extended_2(): before = lax.ppermute(last, axis, up)  22.1 us
    all_to_all x1, starting transfers between devices, shards(): lax.all_to_all(send_blocks, 'patch', split_axis=0, concat_axis=0, tiled=T...  19.8 us
    all_to_all x1, starting transfers between devices, shards(): lax.all_to_all(send_rates, 'patch', split_axis=0, concat_axis=0, tiled=True)  16.3 us
    scatter x1, local copies, waits for them, and re-layouts, shards(): jnp.zeros((slots, STEPS, trials_here, BLOCK), jnp.bfloat16).at[slot]  13.7 us
    ppermute x5, starting transfers between devices, extended_2(): after = lax.ppermute(leading, axis, down)  12.3 us
    ppermute x5, starting transfers between devices, extended_2(): before = lax.ppermute(last, axis, up)  11.7 us
  transfers between devices with their start and end apart: 13, of which 7 were waited for; matrix products, arithmetic and copies ran while one was open for 9% of the time, Pallas kernels for 0%

commit v1 on v0

v1 whole, which is shorter than its diff:
```python
import jax
import jax.numpy as jnp
from jax import lax
from jax.experimental import pallas as pl
from jax.experimental.pallas import tpu as pltpu
from jax.sharding import PartitionSpec as P

BLOCK = 128
STEPS = 4
TR = 8
EDGE = STEPS - 1
PAIRS = [(s, i) for s in range(EDGE) for i in range(EDGE - s)]
F32 = jnp.float32
BF16 = jnp.bfloat16

SMEM = pl.BlockSpec(memory_space=pltpu.SMEM)
VMEM = pl.BlockSpec(memory_space=pltpu.VMEM)
PARAMS = pltpu.CompilerParams(vmem_limit_bytes=48 * 1024 * 1024)


def pack_kernel(target, source, delay, block, weight, history, out, count):
    patches = out.shape[0]
    out[...] = jnp.zeros_like(out)

    def clear(i, carry):
        count[i] = 0
        return carry

    lax.fori_loop(0, patches, clear, 0, unroll=8)
    row = lax.broadcasted_iota(jnp.int32, (TR, BLOCK), 0)

    def tract(i, carry):
        to = target[i]
        rank = count[to]
        count[to] = rank + 1
        lanes = pl.ds(pl.multiple_of(source[i] * BLOCK, BLOCK), BLOCK)
        for step in range(STEPS):
            rates = history[delay[i] - step - 1, :, lanes].astype(F32)
            out[to, 2 * step + rank] = (rates * weight[i]).astype(BF16)
        ids = out[to, 2 * STEPS].astype(F32)
        name = (block[i] + 1).astype(F32)
        out[to, 2 * STEPS] = jnp.where(row == rank, name, ids).astype(BF16)
        return carry

    lax.fori_loop(0, target.shape[0], tract, 0, unroll=4)


def pack(target, source, delay, block, weight, history, patches):
    return pl.pallas_call(
        pack_kernel,
        out_shape=jax.ShapeDtypeStruct((patches, 2 * STEPS + 1, TR, BLOCK), BF16),
        in_specs=[SMEM] * 5 + [VMEM],
        out_specs=VMEM,
        scratch_shapes=[pltpu.SMEM((patches,), jnp.int32)],
        compiler_params=PARAMS,
        name="pack",
    )(target, source, delay, block, weight, history)


def coupling_kernel(got, spread, coupling, first, last, names, picks):
    patches = got.shape[0]
    nblk = coupling.shape[1]
    width = 2 * TR
    ids = got[:, STEPS * width : STEPS * width + TR, :].astype(F32)
    names[...] = ids.reshape(patches * TR, BLOCK)
    lane = lax.broadcasted_iota(jnp.int32, (TR, BLOCK), 1)
    one = jnp.where(lane == 0, 1.0, 0.0).astype(BF16)
    flat = [
        lax.dot_general(
            one,
            names[pl.ds(r, patches, stride=TR), :].astype(BF16),
            (((1,), (1,)), ((), ())),
            preferred_element_type=F32,
        )
        for r in range(2)
    ]
    flat = jnp.concatenate(flat, axis=1).astype(BF16)
    spot = jnp.dot(flat, spread[...], preferred_element_type=F32)[0:1]
    trial = lax.broadcasted_iota(jnp.int32, (1, patches * width), 1) % TR
    spot = (spot.astype(jnp.int32) - 1) * TR + trial
    line = lax.broadcasted_iota(jnp.int32, (nblk * TR, patches * width), 0)
    picks[...] = jnp.where(line == spot, 1.0, 0.0).astype(BF16)
    for s in range(STEPS):
        sent = got[:, s * width : (s + 1) * width, :].reshape(patches * width, BLOCK)
        total = jnp.dot(picks[...], sent, preferred_element_type=F32)
        coupling[s] = total.reshape(nblk, TR, BLOCK)
    for n, (s, i) in enumerate(PAIRS):
        first[n] = coupling[s, i]
        last[n] = coupling[s, nblk - EDGE + s + i]


def tract_sums(got, nblk):
    patches = got.shape[0]
    width = 2 * TR
    column = jnp.arange(patches * width, dtype=jnp.int32)[None, :]
    line = jnp.arange(2 * patches, dtype=jnp.int32)[:, None]
    spread = (column // TR == (line % patches) * 2 + line // patches).astype(BF16)
    return pl.pallas_call(
        coupling_kernel,
        out_shape=[
            jax.ShapeDtypeStruct((STEPS, nblk, TR, BLOCK), F32),
            jax.ShapeDtypeStruct((len(PAIRS), TR, BLOCK), F32),
            jax.ShapeDtypeStruct((len(PAIRS), TR, BLOCK), F32),
        ],
        in_specs=[VMEM] * 2,
        out_specs=[VMEM] * 3,
        scratch_shapes=[
            pltpu.VMEM((patches * TR, BLOCK), F32),
            pltpu.VMEM((nblk * TR, patches * width), BF16),
        ],
        compiler_params=PARAMS,
        name="tracts",
    )(got, spread)


def local_block(j, place, index, frame, own, left, right, far0, far1):
    rows = [frame[index[4 * j + place[shift]]] for shift in (0, 3, 1, 2)]
    rows = jnp.concatenate(rows, axis=1).astype(BF16)
    half = far0.shape[0]
    distant = far0[j] if j < half else far1[j - half]
    tiles = jnp.concatenate([own[j], left[j], right[j], distant], axis=0)
    return jnp.dot(rows, tiles, preferred_element_type=F32)


def start_kernel(place, index, frame, own, left, right, far0, far1, out):
    for j in range(own.shape[0]):
        out[j] = local_block(j, place, index, frame, own, left, right, far0, far1)


def start_local(place, index, frame, tiles):
    return pl.pallas_call(
        start_kernel,
        out_shape=jax.ShapeDtypeStruct((tiles[0].shape[0], TR, BLOCK), F32),
        in_specs=[SMEM] * 2 + [VMEM] * 6,
        out_specs=VMEM,
        compiler_params=PARAMS,
        name="start",
    )(place, index, frame, *tiles)


CHUNK = 512


def window_kernel(
    place, index, flags, offset, begin, local, coupling, below, above,
    own, left, right, far0, far1, drive, slope, strength, owner,
    rate, mine, to_left, to_right, frame, sums, parts,
):
    ext = own.shape[0]
    nblk = ext - 2 * EDGE
    tiles = (own, left, right, far0, far1)
    frame[...] = begin[...]
    steep = jnp.broadcast_to(slope[...], (TR, BLOCK))
    strong = jnp.broadcast_to(strength[...], (TR, BLOCK))
    for step in range(STEPS):
        blocks = range(step, ext - step)
        if step > 0:
            for j in blocks:
                sums[j] = local_block(j, place, index, frame, *tiles)
        for j in blocks:
            if j < EDGE:
                tracts = below[PAIRS.index((step, j - step))]
            elif j >= nblk + EDGE:
                tracts = above[PAIRS.index((step, j - nblk - EDGE))]
            else:
                tracts = coupling[step, j - EDGE]
            near = local[j] if step == 0 else sums[j]
            pre = steep * (near + strong * tracts + drive[j])
            old = frame[j + 1]
            fresh = old + 0.5 * (jax.nn.sigmoid(pre) - old)
            if j < EDGE:
                fresh = fresh * flags[0]
            elif j >= nblk + EDGE:
                fresh = fresh * flags[1]
            frame[j + 1] = fresh
            if EDGE <= j < nblk + EDGE:
                at = slice((j - EDGE) * BLOCK, (j - EDGE + 1) * BLOCK)
                top = fresh.astype(BF16).astype(F32)
                pair = jnp.concatenate([top, fresh - top], axis=0)
                parts[2 * TR * step : 2 * TR * (step + 1), at] = pair.astype(BF16)
                if step == STEPS - 1:
                    rate[:, at] = fresh
    voxels = 3 * mine.shape[1]
    rows = 2 * TR * STEPS
    parts[rows:] = jnp.ones_like(parts[rows:])
    total = jnp.zeros((rows + 2 * TR, voxels), F32)
    for c in range(0, nblk * BLOCK, CHUNK):
        name = owner[:, c : c + CHUNK] - offset[0]
        hit = lax.broadcasted_iota(jnp.int32, (voxels, CHUNK), 0) == name
        hit = jnp.where(hit, 1.0, 0.0).astype(BF16)
        total = total + lax.dot_general(
            parts[:, c : c + CHUNK], hit, (((1,), (1,)), ((), ())), preferred_element_type=F32
        )
    for n, out in enumerate((to_left, mine, to_right)):
        at = slice(n * mine.shape[1], (n + 1) * mine.shape[1])
        for step in range(STEPS):
            high = total[2 * TR * step : 2 * TR * step + TR, at]
            low = total[2 * TR * step + TR : 2 * TR * (step + 1), at]
            out[TR * step : TR * (step + 1)] = high + low
        out[TR * STEPS :] = total[rows : rows + TR, at]


def window(
    place, index, flags, offset, begin, local, coupling, below, above, tiles,
    drive, slope, strength, owner, voxels,
):
    ext = tiles[0].shape[0]
    nblk = ext - 2 * EDGE
    return pl.pallas_call(
        window_kernel,
        out_shape=[
            jax.ShapeDtypeStruct((TR, nblk * BLOCK), F32),
            *[jax.ShapeDtypeStruct(((STEPS + 1) * TR, voxels), F32)] * 3,
        ],
        in_specs=[SMEM] * 4 + [VMEM] * 14,
        out_specs=[VMEM] * 4,
        scratch_shapes=[
            pltpu.VMEM((ext + 2, TR, BLOCK), F32),
            pltpu.VMEM((ext, TR, BLOCK), F32),
            pltpu.VMEM((2 * TR * (STEPS + 1), nblk * BLOCK), BF16),
        ],
        compiler_params=PARAMS,
        name="window",
    )(
        place, index, flags, offset, begin, local, coupling, below, above, *tiles,
        drive, slope, strength, owner,
    )


def flow_kernel(mine, below, above, vaso, flow, vaso_out, flow_out):
    total = mine[...] + below[...] + above[...]
    floor = jnp.maximum(total[STEPS * TR :], 1.0)
    signal, inflow = vaso[...], flow[...]
    for step in range(STEPS):
        level = total[step * TR : (step + 1) * TR] / floor
        signal = signal + 0.5 * (level - 0.65 * signal - 0.41 * (inflow - 1.0))
        inflow = inflow + 0.5 * signal
    vaso_out[...] = signal
    flow_out[...] = inflow


def shards(
    activity,
    history,
    drive,
    slope,
    strength,
    kernel,
    kernel_index,
    tract_source,
    tract_delay,
    tract_target,
    tract_block,
    tract_weight,
    voxel_owner,
    vaso_signal,
    blood_flow,
):
    verts = activity.shape[1]
    nblk = verts // BLOCK
    patches = lax.axis_size("patch")
    group = lax.axis_size("trial")
    voxels_here = vaso_signal.shape[1]
    up = [(i, i + 1) for i in range(patches - 1)]
    down = [(j, i) for i, j in up]
    clock = [(i, (i + 1) % group) for i in range(group)]
    counter = [(j, i) for i, j in clock]
    patch = lax.axis_index("patch").astype(jnp.int32)

    def sides(low, high):
        return lax.ppermute(high, "patch", up), lax.ppermute(low, "patch", down)

    raw = kernel.reshape(nblk, BLOCK, BLOCK)
    before, after = sides(raw[:EDGE], raw[nblk - EDGE :])
    send = pack(
        tract_target[:, 0], tract_source, tract_delay, tract_block, tract_weight, history, patches
    )
    send, before, after = lax.optimization_barrier((send, before, after))
    got = lax.all_to_all(send, "patch", split_axis=0, concat_axis=0, tiled=True)

    own = jnp.concatenate([before, raw, after], axis=0)
    half = own.shape[0] // 2
    left = lax.ppermute(own, "trial", clock)
    right = lax.ppermute(own, "trial", counter)
    far0 = lax.ppermute(left[:half], "trial", clock)
    far1 = lax.ppermute(right[half:], "trial", counter)
    tiles = (own, left, right, far0, far1)

    near = EDGE + 1
    blocks = activity.reshape(TR, nblk, BLOCK)
    extra = jnp.concatenate([drive.reshape(nblk, BLOCK)[:, None, :]] * TR, axis=1)
    names = jnp.zeros((nblk, TR, BLOCK), F32)
    names = names + jnp.pad(kernel_index.astype(F32), ((0, 0), (0, BLOCK - 4)))[:, None, :]

    def edge(at, inner):
        rates = blocks[:, at].transpose(1, 0, 2)
        return jnp.concatenate([rates, extra[inner], names[inner]], axis=0)

    before, after = sides(
        edge(slice(0, near), slice(0, EDGE)),
        edge(slice(nblk - near, nblk), slice(nblk - EDGE, nblk)),
    )
    begin = jnp.concatenate([before[:near], blocks.transpose(1, 0, 2), after[:near]], axis=0)
    drive_ext = jnp.concatenate([before[near : near + EDGE], extra, after[near : near + EDGE]])
    index = jnp.concatenate(
        [
            before[near + EDGE :, 0, :4].astype(jnp.int32) - (nblk - near + 1),
            kernel_index + EDGE,
            after[near + EDGE :, 0, :4].astype(jnp.int32) + (nblk + EDGE),
        ]
    )
    index = jnp.clip(index, 0, nblk + 2 * near - 1).reshape(-1)
    here = lax.axis_index("trial").astype(jnp.int32)
    place = (here + jnp.arange(group, dtype=jnp.int32)) % group
    flags = jnp.stack([patch > 0, patch < patches - 1]).astype(F32)
    offset = ((patch - 1) * voxels_here).reshape(1)
    local = start_local(place, index, begin, tiles)

    rows = (2 * STEPS + 1) * TR
    coupling, first, last = tract_sums(got.reshape(patches, rows, BLOCK), nblk)
    below, above = sides(first, last)
    rate, mine, to_left, to_right = window(
        place,
        index,
        flags,
        offset,
        begin,
        local,
        coupling,
        below,
        above,
        tiles,
        drive_ext,
        slope[:, None],
        strength[:, None],
        voxel_owner.reshape(1, verts),
        voxels_here,
    )
    below, above = sides(to_left, to_right)
    vaso, flow = pl.pallas_call(
        flow_kernel,
        out_shape=[jax.ShapeDtypeStruct(vaso_signal.shape, F32)] * 2,
        in_specs=[VMEM] * 5,
        out_specs=[VMEM] * 2,
        name="flow",
    )(mine, below, above, vaso_signal, blood_flow)
    return (rate, vaso, flow)


def solution(mesh):
    placed = (
        P("trial", "patch"),
        P(None, "trial", "patch"),
        P("patch"),
        P("trial"),
        P("trial"),
        P("patch", "trial", None, None),
        P("patch", None),
        P("patch"),
        P("patch"),
        P("patch", None),
        P("patch"),
        P("patch"),
        P("patch"),
        P("trial", "patch"),
        P("trial", "patch"),
    )
    return jax.shard_map(
        shards,
        mesh=mesh,
        in_specs=placed,
        out_specs=(P("trial", "patch"), P("trial", "patch"), P("trial", "patch")),
        check_vma=False,
    )
```

time: 248 us -> 183 us (0.74)
  waiting for transfers between devices: 107 us -> 73.6 us
  other arithmetic: 27.4 us -> 7.25 us
  Pallas kernels: 0 us -> 17.1 us
  between operations: 14.5 us -> 0.95 us
  matrix products: 12.3 us -> 0 us
  local copies, waits for them, and re-layouts: 24 us -> 20.7 us
    ppermute x10 -> x12, waiting for transfers between devices: 100 us -> 73.6 us  [the longest x8 59.6 us: sides(): return (lax.ppermute(high, 'patch', up), lax.ppermute(low, 'patch', down))]
    ppermute x10 -> x12, starting transfers between devices: 24 us -> 50 us  [the longest x8 35.9 us: sides(): return (lax.ppermute(high, 'patch', up), lax.ppermute(low, 'patch', down))]
    all_to_all x2 -> x1, starting transfers between devices: 36.2 us -> 12.4 us  [shards(): got = lax.all_to_all(send, 'patch', split_axis=0, concat_axis=0, tiled=True)]
    scatter-add x1 -> x0, other arithmetic: 22.5 us -> none  [shards(): partial_value = jnp.zeros((values.shape[0], 3 * voxels_here), jnp.float32...]
    pallas_call x0 -> x5, Pallas kernels: none -> 17.1 us  [the longest x1 5.32 us: window(): pl.pallas_call(window_kernel, out_shape=[jax.ShapeDtypeStruct((TR, nblk *...]
    scatter x2 -> x0, local copies, waits for them, and re-layouts: 14.8 us -> none  [the longest x1 13.7 us: shards(): jnp.zeros((slots, STEPS, trials_here, BLOCK), jnp.bfloat16).at[slot]]
    dot_general x5 -> x0, matrix products: 12.3 us -> none  [the longest x4 11.6 us: shards(): jnp.einsum('tbki,bkij->tbj', picked, tiles, preferred_element_type=jnp.fl...]
    slice x6 -> x11, local copies, waits for them, and re-layouts: 0.08 us -> 7.64 us  [the longest x1 2 us: shards(): far0 = lax.ppermute(left[:half], 'trial', clock)]
  transfers between devices with their start and end apart: 13 -> 13, of which waited for: 7 -> 3; matrix products, arithmetic and copies ran while one was open for 9% -> 11% of each run, Pallas kernels for 0% -> 6%
where the time goes in v1:
time: 183 us; the launch traced here: 182 us
  waiting for transfers between devices  73.6 us (40%)
  starting transfers between devices  62.4 us (34%)
  local copies, waits for them, and re-layouts  20.7 us (11%)
  Pallas kernels  17.1 us (9%)
  other arithmetic  7.25 us (4%)
    ppermute x8, waiting for transfers between devices, sides(): return (lax.ppermute(high, 'patch', up), lax.ppermute(low, 'patch', down))  59.6 us
    ppermute x8, starting transfers between devices, sides(): return (lax.ppermute(high, 'patch', up), lax.ppermute(low, 'patch', down))  35.9 us
    ppermute x1, waiting for transfers between devices, shards(): right = lax.ppermute(own, 'trial', counter)  14 us
    all_to_all x1, starting transfers between devices, shards(): got = lax.all_to_all(send, 'patch', split_axis=0, concat_axis=0, tiled=True)  12.4 us
    unnamed x38, local copies, waits for them, and re-layouts  7.22 us
    ppermute x1, starting transfers between devices, shards(): far1 = lax.ppermute(right[half:], 'trial', counter)  5.59 us
    pallas_call x1, Pallas kernels, window(): pl.pallas_call(window_kernel, out_shape=[jax.ShapeDtypeStruct((TR, nblk *...  5.32 us
    ppermute x1, starting transfers between devices, shards(): right = lax.ppermute(own, 'trial', counter)  4.67 us
  transfers between devices with their start and end apart: 13, of which 3 were waited for; matrix products, arithmetic and copies ran while one was open for 11% of the time, Pallas kernels for 6%

profile of v1, /device:TPU:24, one launch (start us, length us, event | category | flops | bytes accessed | tf_op | source)
XLA Modules:
  0.0 182.0 jit_solution(2433223549185076213)
XLA Ops:
  1.6 11.0 %collective-permute-start.3 = (bf16[3,128,128]{2,1,0:T(8,128)(2,1)S(1)}, bf16[3,128,128]{2,1,0:T(8,128)(2,1)S(1)}, u32[]{:S(2)}, u32[]{:S(2)}) collective-permute-start(bf16[3,128,128]{2,1,0:T(8,128)(2,1)S(1)} %get-tuple-element.27), channel_id=1, source_target_pairs={{4,0},{8,4},{12,8},{16,12},{20,16},{24,20},{28,24},{32,28},{36,32}... | collective-permute-start | bytes 294920 | tf_op jit(solution)/shard_map/ppermute | solution.py:271
  12.6 1.9 %collective-permute-start.2 = (bf16[3,128,128]{2,1,0:T(8,128)(2,1)S(1)}, bf16[3,128,128]{2,1,0:T(8,128)(2,1)S(1)}, u32[]{:S(2)}, u32[]{:S(2)}) collective-permute-start(bf16[3,128,128]{2,1,0:T(8,128)(2,1)S(1)} %get-tuple-element.28), channel_id=1, source_target_pairs={{0,4},{4,8},{8,12},{12,16},{16,20},{20,24},{24,28},{28,32},{32,36}... | collective-permute-start | bytes 294920 | tf_op jit(solution)/shard_map/ppermute | solution.py:271
  18.8 4.4 %pack.1 = bf16[128,9,8,128]{3,2,1,0:T(8,128)(2,1)} custom-call(s32[128]{0:T(128)S(1)} %bitcast.29, s32[128]{0:T(128)S(1)} %copy-done.8, s32[128]{0:T(128)S(1)} %copy-done.9, s32[128]{0:T(128)S(1)} %copy-done.10, f32[128]{0:T(128)S(1)} %copy-done.11, bf16[7,8,4096]{2,1,0:T(8,128)(2,1)S(1)} %copy-done.4), custom_call_target="tpu_custom_call" | custom-call | tf_op jit(solution)/shard_map/pack/pallas_call | solution.py:49
  23.2 12.4 %all-to-all-start = ((bf16[128,9,8,128]{3,2,1,0:T(8,128)(2,1)}), bf16[128,9,8,128]{3,2,1,0:T(8,128)(2,1)}, u32[]{:S(2)}, u32[]{:S(2)}) async-start(bf16[128,9,8,128]{3,2,1,0:T(8,128)(2,1)} %pack.1), calls=%async_computation | async-start | bytes 4718592 | tf_op jit(solution)/shard_map/all_to_all | solution.py:279
  37.9 4.7 %collective-permute-start.5 = (bf16[38,128,128]{2,1,0:T(8,128)(2,1)S(1)}, bf16[38,128,128]{2,1,0:T(8,128)(2,1)S(1)}, u32[]{:S(2)}, u32[]{:S(2)}) collective-permute-start(bf16[38,128,128]{2,1,0:T(8,128)(2,1)S(1)} %pad_maximum_fusion.own), channel_id=1, source_target_pairs={{1,0},{2,1},{3,2},{0,3},{5,4},{6,5},{7,6},{4,7},{9,8},{10,9},{11,1... | collective-permute-start | bytes 3735560 | tf_op jit(solution)/shard_map/ppermute | solution.py:284
  42.5 1.9 %collective-permute-start.4 = (bf16[38,128,128]{2,1,0:T(8,128)(2,1)S(1)}, bf16[38,128,128]{2,1,0:T(8,128)(2,1)}, u32[]{:S(2)}, u32[]{:S(2)}) collective-permute-start(bf16[38,128,128]{2,1,0:T(8,128)(2,1)S(1)} %pad_maximum_fusion.own), channel_id=1, source_target_pairs={{0,1},{1,2},{2,3},{3,0},{4,5},{5,6},{6,7},{7,4},{8,9},{9,10},{10,1... | collective-permute-start | bytes 3735560 | tf_op jit(solution)/shard_map/ppermute | solution.py:283
  45.3 1.9 %collective-permute-start = (f32[10,8,128]{2,1,0:T(8,128)}, f32[10,8,128]{2,1,0:T(8,128)}, u32[]{:S(2)}, u32[]{:S(2)}) collective-permute-start(f32[10,8,128]{2,1,0:T(8,128)} %pad_maximum_fusion.3), channel_id=1, source_target_pairs={{0,4},{4,8},{8,12},{12,16},{16,20},{20,24},{24,28},{28,32},{32,36}... | collective-permute-start | bytes 122888 | tf_op jit(solution)/shard_map/ppermute | solution.py:271
  47.9 5.7 %collective-permute-start.1 = (f32[10,8,128]{2,1,0:T(8,128)}, f32[10,8,128]{2,1,0:T(8,128)}, u32[]{:S(2)}, u32[]{:S(2)}) collective-permute-start(f32[10,8,128]{2,1,0:T(8,128)} %pad_maximum_fusion.4), channel_id=1, source_target_pairs={{4,0},{8,4},{12,8},{16,12},{20,16},{24,20},{28,24},{32,28},{36,32}... | collective-permute-start | bytes 122888 | tf_op jit(solution)/shard_map/ppermute | solution.py:271
  55.5 14.0 %collective-permute-done.5.right = bf16[38,128,128]{2,1,0:T(8,128)(2,1)S(1)} collective-permute-done((bf16[38,128,128]{2,1,0:T(8,128)(2,1)S(1)}, bf16[38,128,128]{2,1,0:T(8,128)(2,1)S(1)}, u32[]{:S(2)}, u32[]{:S(2)}) %collective-permute-start.5) | collective-permute-done | bytes 1245216 | tf_op jit(solution)/shard_map/ppermute | solution.py:284
  70.4 5.6 %collective-permute-start.7 = (bf16[19,128,128]{2,1,0:T(8,128)(2,1)}, bf16[19,128,128]{2,1,0:T(8,128)(2,1)}, u32[]{:S(2)}, u32[]{:S(2)}) collective-permute-start(bf16[19,128,128]{2,1,0:T(8,128)(2,1)} %slice.106), channel_id=1, source_target_pairs={{1,0},{2,1},{3,2},{0,3},{5,4},{6,5},{7,6},{4,7},{9,8},{10,9},{11,1... | collective-permute-start | bytes 1867784 | tf_op jit(solution)/shard_map/ppermute | solution.py:286
  76.0 2.0 %slice.105 = bf16[19,128,128]{2,1,0:T(8,128)(2,1)} slice(bf16[38,128,128]{2,1,0:T(8,128)(2,1)} %collective-permute-done.4.left), slice={[0:19], [0:128], [0:128]} | slice | bytes 1245184 | tf_op jit(solution)/shard_map/slice | solution.py:285
  78.0 1.9 %collective-permute-start.6 = (bf16[19,128,128]{2,1,0:T(8,128)(2,1)}, bf16[19,128,128]{2,1,0:T(8,128)(2,1)}, u32[]{:S(2)}, u32[]{:S(2)}) collective-permute-start(bf16[19,128,128]{2,1,0:T(8,128)(2,1)} %slice.105), channel_id=1, source_target_pairs={{0,1},{1,2},{2,3},{3,0},{4,5},{5,6},{6,7},{7,4},{8,9},{9,10},{10,1... | collective-permute-start | bytes 1867784 | tf_op jit(solution)/shard_map/ppermute | solution.py:285
  79.9 58.1 %collective-permute-done = f32[10,8,128]{2,1,0:T(8,128)} collective-permute-done((f32[10,8,128]{2,1,0:T(8,128)}, f32[10,8,128]{2,1,0:T(8,128)}, u32[]{:S(2)}, u32[]{:S(2)}) %collective-permute-start) | collective-permute-done | bytes 40992 | tf_op jit(solution)/shard_map/ppermute | solution.py:271
  139.3 1.3 copy.35
  147.5 1.6 pad_maximum_fusion.1.frame.begin
  149.1 3.6 %tracts.1 = (f32[4,32,8,128]{3,2,1,0:T(8,128)S(1)}, f32[6,8,128]{2,1,0:T(8,128)}, f32[6,8,128]{2,1,0:T(8,128)}) custom-call(bf16[128,72,128]{2,1,0:T(8,128)(2,1)} %bitcast.16.got, bf16[256,2048]{1,0:T(8,128)(2,1)S(1)} %compare_convert_fusion.spread), custom_call_target="tpu_custom_call" | custom-call | tf_op jit(solution)/shard_map/tracts/pallas_call | solution.py:98
  153.5 1.9 %collective-permute-start.8 = (f32[6,8,128]{2,1,0:T(8,128)}, f32[6,8,128]{2,1,0:T(8,128)S(1)}, u32[]{:S(2)}, u32[]{:S(2)}) collective-permute-start(f32[6,8,128]{2,1,0:T(8,128)} %get-tuple-element.19), channel_id=1, source_target_pairs={{0,4},{4,8},{8,12},{12,16},{16,20},{20,24},{24,28},{28,32},{32,36}... | collective-permute-start | bytes 73736 | tf_op jit(solution)/shard_map/ppermute | solution.py:271
  155.4 5.8 %collective-permute-start.9 = (f32[6,8,128]{2,1,0:T(8,128)}, f32[6,8,128]{2,1,0:T(8,128)S(1)}, u32[]{:S(2)}, u32[]{:S(2)}) collective-permute-start(f32[6,8,128]{2,1,0:T(8,128)} %get-tuple-element.20), channel_id=1, source_target_pairs={{4,0},{8,4},{12,8},{16,12},{20,16},{24,20},{28,24},{32,28},{36,32}... | collective-permute-start | bytes 73736 | tf_op jit(solution)/shard_map/ppermute | solution.py:271
  162.4 2.5 %start.1.local = f32[38,8,128]{2,1,0:T(8,128)S(1)} custom-call(s32[4]{0:T(128)S(1)} %and_select_fusion.2.place, s32[152]{0:T(256)S(1)} %min.12.index, f32[40,8,128]{2,1,0:T(8,128)S(1)} %copy-done, bf16[38,128,128]{2,1,0:T(8,128)(2,1)S(1)} %pad_maximum_fusion.own, bf16[38,128,128]{2,1,0:T(8,128)(2,1)} %collective-permute-done.4.left, ...), custom_call_target="tpu_custom_call" | custom-call | tf_op jit(solution)/shard_map/start/pallas_call | solution.py:131
  165.0 5.3 %window.1 = (f32[8,4096]{1,0:T(8,128)}, f32[40,128]{1,0:T(8,128)S(1)}, f32[40,128]{1,0:T(8,128)S(1)}, f32[40,128]{1,0:T(8,128)S(1)}) custom-call(s32[4]{0:T(128)S(1)} %and_select_fusion.2.place, s32[152]{0:T(256)S(1)} %min.12.index, f32[2]{0:T(128)S(1)} %add_convert_fusion.flags, s32[1]{0:T(128)} %bitcast.9.offset, f32[40,8,128]{2,1,0:T(8,128)S(1)} %copy-done, ...), custom_call_target="tpu_custom_call" | custom-call | tf_op jit(solution)/shard_map/window/pallas_call | solution.py:209
  170.9 1.9 %collective-permute-start.10 = (f32[40,128]{1,0:T(8,128)S(1)}, f32[40,128]{1,0:T(8,128)S(1)}, u32[]{:S(2)}, u32[]{:S(2)}) collective-permute-start(f32[40,128]{1,0:T(8,128)S(1)} %get-tuple-element.23), channel_id=1, source_target_pairs={{0,4},{4,8},{8,12},{12,16},{16,20},{20,24},{24,28},{28,32},{32,36}... | collective-permute-start | bytes 61448 | tf_op jit(solution)/shard_map/ppermute | solution.py:271
  172.8 5.8 %collective-permute-start.11 = (f32[40,128]{1,0:T(8,128)S(1)}, f32[40,128]{1,0:T(8,128)S(1)}, u32[]{:S(2)}, u32[]{:S(2)}) collective-permute-start(f32[40,128]{1,0:T(8,128)S(1)} %get-tuple-element.24), channel_id=1, source_target_pairs={{4,0},{8,4},{12,8},{16,12},{20,16},{24,20},{28,24},{32,28},{36,32}... | collective-permute-start | bytes 61448 | tf_op jit(solution)/shard_map/ppermute | solution.py:271
  178.6 1.4 collective-permute-done.11.above
  180.6 1.4 flow.2
  (82 shorter events, 23.0 us)
Async XLA Ops:
  1.6 21.6 %collective-permute-start.3 = (bf16[3,128,128]{2,1,0:T(8,128)(2,1)S(1)}, bf16[3,128,128]{2,1,0:T(8,128)(2,1)S(1)}, u32[]{:S(2)}, u32[]{:S(2)}) collective-permute-start(bf16[3,128,128]{2,1,0:T(8,128)(2,1)S(1)} %get-tuple-element.27), channel_id=1, source_target_pairs={{4,0},{8,4},{12,8},{16,12},{20,16},{24,20},{28,24},{32,28},{36,32}... | collective-permute-start | bytes 294920 | tf_op jit(solution)/shard_map/ppermute | solution.py:271
  12.6 10.6 %collective-permute-start.2 = (bf16[3,128,128]{2,1,0:T(8,128)(2,1)S(1)}, bf16[3,128,128]{2,1,0:T(8,128)(2,1)S(1)}, u32[]{:S(2)}, u32[]{:S(2)}) collective-permute-start(bf16[3,128,128]{2,1,0:T(8,128)(2,1)S(1)} %get-tuple-element.28), channel_id=1, source_target_pairs={{0,4},{4,8},{8,12},{12,16},{16,20},{20,24},{24,28},{28,32},{32,36}... | collective-permute-start | bytes 294920 | tf_op jit(solution)/shard_map/ppermute | solution.py:271
  14.5 1.0 copy-start.4
  23.2 12.5 %copy-start.18 = (s32[32,4]{0,1:T(4,128)S(1)}, s32[32,4]{0,1:T(4,128)}, u32[]{:S(2)}) copy-start(s32[32,4]{0,1:T(4,128)} %param.21) | copy-start | bytes 1540
  23.2 14.5 %copy-start.12 = (bf16[32,1,128,128]{3,2,1,0:T(8,128)(2,1)S(1)}, bf16[32,1,128,128]{3,2,1,0:T(8,128)(2,1)}, u32[]{:S(2)}) copy-start(bf16[32,1,128,128]{3,2,1,0:T(8,128)(2,1)} %param.20) | copy-start | bytes 3145732
  23.2 125.9 %all-to-all-start = ((bf16[128,9,8,128]{3,2,1,0:T(8,128)(2,1)}), bf16[128,9,8,128]{3,2,1,0:T(8,128)(2,1)}, u32[]{:S(2)}, u32[]{:S(2)}) async-start(bf16[128,9,8,128]{3,2,1,0:T(8,128)(2,1)} %pack.1), calls=%async_computation | async-start | bytes 4718592 | tf_op jit(solution)/shard_map/all_to_all | solution.py:279
  37.9 31.6 %collective-permute-start.5 = (bf16[38,128,128]{2,1,0:T(8,128)(2,1)S(1)}, bf16[38,128,128]{2,1,0:T(8,128)(2,1)S(1)}, u32[]{:S(2)}, u32[]{:S(2)}) collective-permute-start(bf16[38,128,128]{2,1,0:T(8,128)(2,1)S(1)} %pad_maximum_fusion.own), channel_id=1, source_target_pairs={{1,0},{2,1},{3,2},{0,3},{5,4},{6,5},{7,6},{4,7},{9,8},{10,9},{11,1... | collective-permute-start | bytes 3735560 | tf_op jit(solution)/shard_map/ppermute | solution.py:284
  42.5 33.5 %collective-permute-start.4 = (bf16[38,128,128]{2,1,0:T(8,128)(2,1)S(1)}, bf16[38,128,128]{2,1,0:T(8,128)(2,1)}, u32[]{:S(2)}, u32[]{:S(2)}) collective-permute-start(bf16[38,128,128]{2,1,0:T(8,128)(2,1)S(1)} %pad_maximum_fusion.own), channel_id=1, source_target_pairs={{0,1},{1,2},{2,3},{3,0},{4,5},{5,6},{6,7},{7,4},{8,9},{9,10},{10,1... | collective-permute-start | bytes 3735560 | tf_op jit(solution)/shard_map/ppermute | solution.py:283
  45.3 92.8 %collective-permute-start = (f32[10,8,128]{2,1,0:T(8,128)}, f32[10,8,128]{2,1,0:T(8,128)}, u32[]{:S(2)}, u32[]{:S(2)}) collective-permute-start(f32[10,8,128]{2,1,0:T(8,128)} %pad_maximum_fusion.3), channel_id=1, source_target_pairs={{0,4},{4,8},{8,12},{12,16},{16,20},{20,24},{24,28},{28,32},{32,36}... | collective-permute-start | bytes 122888 | tf_op jit(solution)/shard_map/ppermute | solution.py:271
  47.9 92.8 %collective-permute-start.1 = (f32[10,8,128]{2,1,0:T(8,128)}, f32[10,8,128]{2,1,0:T(8,128)}, u32[]{:S(2)}, u32[]{:S(2)}) collective-permute-start(f32[10,8,128]{2,1,0:T(8,128)} %pad_maximum_fusion.4), channel_id=1, source_target_pairs={{4,0},{8,4},{12,8},{16,12},{20,16},{24,20},{28,24},{32,28},{36,32}... | collective-permute-start | bytes 122888 | tf_op jit(solution)/shard_map/ppermute | solution.py:271
  70.4 91.1 %collective-permute-start.7 = (bf16[19,128,128]{2,1,0:T(8,128)(2,1)}, bf16[19,128,128]{2,1,0:T(8,128)(2,1)}, u32[]{:S(2)}, u32[]{:S(2)}) collective-permute-start(bf16[19,128,128]{2,1,0:T(8,128)(2,1)} %slice.106), channel_id=1, source_target_pairs={{1,0},{2,1},{3,2},{0,3},{5,4},{6,5},{7,6},{4,7},{9,8},{10,9},{11,1... | collective-permute-start | bytes 1867784 | tf_op jit(solution)/shard_map/ppermute | solution.py:286
  78.0 83.5 %collective-permute-start.6 = (bf16[19,128,128]{2,1,0:T(8,128)(2,1)}, bf16[19,128,128]{2,1,0:T(8,128)(2,1)}, u32[]{:S(2)}, u32[]{:S(2)}) collective-permute-start(bf16[19,128,128]{2,1,0:T(8,128)(2,1)} %slice.105), channel_id=1, source_target_pairs={{0,1},{1,2},{2,3},{3,0},{4,5},{5,6},{6,7},{7,4},{8,9},{9,10},{10,1... | collective-permute-start | bytes 1867784 | tf_op jit(solution)/shard_map/ppermute | solution.py:285
  149.1 12.0 %copy-start.15 = (s32[32,4]{0,1:T(4,128)S(1)}, s32[32,4]{0,1:T(4,128)}, u32[]{:S(2)}) copy-start(s32[32,4]{0,1:T(4,128)} %get-tuple-element.35) | copy-start | bytes 1540
  149.1 12.1 %copy-start.16 = (s32[3,1,4]{0,2,1:T(4,128)S(1)}, s32[3,1,4]{0,2,1:T(4,128)}, u32[]{:S(2)}) copy-start(s32[3,1,4]{0,2,1:T(4,128)} %copy.35) | copy-start | bytes 148
  149.1 12.1 %copy-start.17 = (s32[3,1,4]{0,2,1:T(4,128)S(1)}, s32[3,1,4]{0,2,1:T(4,128)}, u32[]{:S(2)}) copy-start(s32[3,1,4]{0,2,1:T(4,128)} %copy.36) | copy-start | bytes 148
  153.5 11.4 %collective-permute-start.8 = (f32[6,8,128]{2,1,0:T(8,128)}, f32[6,8,128]{2,1,0:T(8,128)S(1)}, u32[]{:S(2)}, u32[]{:S(2)}) collective-permute-start(f32[6,8,128]{2,1,0:T(8,128)} %get-tuple-element.19), channel_id=1, source_target_pairs={{0,4},{4,8},{8,12},{12,16},{16,20},{20,24},{24,28},{28,32},{32,36}... | collective-permute-start | bytes 73736 | tf_op jit(solution)/shard_map/ppermute | solution.py:271
  155.4 9.5 %collective-permute-start.9 = (f32[6,8,128]{2,1,0:T(8,128)}, f32[6,8,128]{2,1,0:T(8,128)S(1)}, u32[]{:S(2)}, u32[]{:S(2)}) collective-permute-start(f32[6,8,128]{2,1,0:T(8,128)} %get-tuple-element.20), channel_id=1, source_target_pairs={{4,0},{8,4},{12,8},{16,12},{20,16},{24,20},{28,24},{32,28},{36,32}... | collective-permute-start | bytes 73736 | tf_op jit(solution)/shard_map/ppermute | solution.py:271
  161.4 3.6 %copy-start.6 = (s32[4096]{0:T(1024)S(1)}, s32[4096]{0:T(1024)}, u32[]{:S(2)}) copy-start(s32[4096]{0:T(1024)} %param.27) | copy-start | bytes 49156
  161.5 0.9 copy-start
  162.4 2.5 %copy-start.1 = (f32[38,8,128]{2,1,0:T(8,128)S(1)}, f32[38,8,128]{2,1,0:T(8,128)}, u32[]{:S(2)}) copy-start(f32[38,8,128]{2,1,0:T(8,128)} %pad_maximum_fusion.2.drive) | copy-start | bytes 466948
  162.4 2.5 %copy-start.3 = (f32[4,32,8,128]{3,2,1,0:T(8,128)S(1)}, f32[4,32,8,128]{3,2,1,0:T(8,128)}, u32[]{:S(2)}) copy-start(f32[4,32,8,128]{3,2,1,0:T(8,128)} %copy-done.2) | copy-start | bytes 1572868
  170.9 7.7 %collective-permute-start.10 = (f32[40,128]{1,0:T(8,128)S(1)}, f32[40,128]{1,0:T(8,128)S(1)}, u32[]{:S(2)}, u32[]{:S(2)}) collective-permute-start(f32[40,128]{1,0:T(8,128)S(1)} %get-tuple-element.23), channel_id=1, source_target_pairs={{0,4},{4,8},{8,12},{12,16},{16,20},{20,24},{24,28},{28,32},{32,36}... | collective-permute-start | bytes 61448 | tf_op jit(solution)/shard_map/ppermute | solution.py:271
  172.8 7.2 %collective-permute-start.11 = (f32[40,128]{1,0:T(8,128)S(1)}, f32[40,128]{1,0:T(8,128)S(1)}, u32[]{:S(2)}, u32[]{:S(2)}) collective-permute-start(f32[40,128]{1,0:T(8,128)S(1)} %get-tuple-element.24), channel_id=1, source_target_pairs={{4,0},{8,4},{12,8},{16,12},{20,16},{24,20},{28,24},{32,28},{36,32}... | collective-permute-start | bytes 61448 | tf_op jit(solution)/shard_map/ppermute | solution.py:271
  178.6 1.5 copy-start.13
  (8 other events, 5.3 us)

commit v2 on v1

--- a/solution.py
+++ b/solution.py
@@ -18,49 +18,103 @@
 PARAMS = pltpu.CompilerParams(vmem_limit_bytes=48 * 1024 * 1024)
 
 
-def pack_kernel(target, source, delay, block, weight, history, out, count):
+def pack_kernel(
+    target, source, delay, block, weight, history, out,
+    to_s, source_s, delay_s, block_s, weight_s, rates, tiles, names, count, rank_s, sems,
+):
     patches = out.shape[0]
-    out[...] = jnp.zeros_like(out)
+    moves = [
+        pltpu.make_async_copy(a, b, sems.at[n])
+        for n, (a, b) in enumerate(
+            (
+                (target, to_s),
+                (block, block_s),
+                (source, source_s),
+                (delay, delay_s),
+                (weight, weight_s),
+                (history, rates),
+            )
+        )
+    ]
+    for move in moves:
+        move.start()
+    tiles[...] = jnp.zeros_like(tiles)
+    names[...] = jnp.zeros_like(names)
 
     def clear(i, carry):
         count[i] = 0
         return carry
 
-    lax.fori_loop(0, patches, clear, 0, unroll=8)
-    row = lax.broadcasted_iota(jnp.int32, (TR, BLOCK), 0)
-
-    def tract(i, carry):
-        to = target[i]
+    lax.fori_loop(0, patches, clear, 0, unroll=16)
+    moves[0].wait()
+    moves[1].wait()
+
+    def place(i, carry):
+        to = to_s[i]
         rank = count[to]
         count[to] = rank + 1
-        lanes = pl.ds(pl.multiple_of(source[i] * BLOCK, BLOCK), BLOCK)
-        for step in range(STEPS):
-            rates = history[delay[i] - step - 1, :, lanes].astype(F32)
-            out[to, 2 * step + rank] = (rates * weight[i]).astype(BF16)
-        ids = out[to, 2 * STEPS].astype(F32)
-        name = (block[i] + 1).astype(F32)
-        out[to, 2 * STEPS] = jnp.where(row == rank, name, ids).astype(BF16)
+        rank_s[i] = rank
+        name = (block_s[i] + 1).astype(F32)
+        names[to, pl.ds(rank, 1), :] = jnp.full((1, BLOCK), name)
         return carry
 
-    lax.fori_loop(0, target.shape[0], tract, 0, unroll=4)
+    lax.fori_loop(0, to_s.shape[0], place, 0, unroll=8)
+    for move in moves[2:]:
+        move.wait()
+    done = []
+    for step in range(STEPS):
+
+        def tract(i, carry):
+            lanes = pl.ds(pl.multiple_of(source_s[i] * BLOCK, BLOCK), BLOCK)
+            rows = rates[delay_s[i] - step - 1, :, lanes].astype(F32)
+            tiles[to_s[i], 2 * step + rank_s[i]] = (rows * weight_s[i]).astype(BF16)
+            return carry
+
+        lax.fori_loop(0, to_s.shape[0], tract, 0, unroll=8)
+        at = pl.ds(2 * step, 2)
+        done.append(pltpu.make_async_copy(tiles.at[:, at], out.at[:, at], sems.at[6 + step]))
+        done[-1].start()
+    tiles[:, 2 * STEPS] = names[...].astype(BF16)
+    at = pl.ds(2 * STEPS, 1)
+    done.append(pltpu.make_async_copy(tiles.at[:, at], out.at[:, at], sems.at[6 + STEPS]))
+    done[-1].start()
+    for move in done:
+        move.wait()
 
 
 def pack(target, source, delay, block, weight, history, patches):
+    count = target.shape[0]
+    shape = (patches, 2 * STEPS + 1, TR, BLOCK)
     return pl.pallas_call(
         pack_kernel,
-        out_shape=jax.ShapeDtypeStruct((patches, 2 * STEPS + 1, TR, BLOCK), BF16),
-        in_specs=[SMEM] * 5 + [VMEM],
-        out_specs=VMEM,
-        scratch_shapes=[pltpu.SMEM((patches,), jnp.int32)],
+        out_shape=jax.ShapeDtypeStruct(shape, BF16),
+        in_specs=[pl.BlockSpec(memory_space=pl.ANY)] * 6,
+        out_specs=pl.BlockSpec(memory_space=pl.ANY),
+        scratch_shapes=[pltpu.SMEM((count,), jnp.int32)] * 4
+        + [
+            pltpu.SMEM((count,), F32),
+            pltpu.VMEM(history.shape, BF16),
+            pltpu.VMEM(shape, BF16),
+            pltpu.VMEM((patches, TR, BLOCK), F32),
+            pltpu.SMEM((patches,), jnp.int32),
+            pltpu.SMEM((count,), jnp.int32),
+            pltpu.SemaphoreType.DMA((7 + STEPS,)),
+        ],
         compiler_params=PARAMS,
         name="pack",
     )(target, source, delay, block, weight, history)
 
 
-def coupling_kernel(got, spread, coupling, first, last, names, picks):
+def coupling_kernel(here, spread, coupling, first, last, got, names, picks, sems):
     patches = got.shape[0]
     nblk = coupling.shape[1]
     width = 2 * TR
+    moves = []
+    for n in range(STEPS + 1):
+        at = pl.ds((n - 1) * width if n else STEPS * width, width if n else TR)
+        moves.append(pltpu.make_async_copy(here.at[:, at], got.at[:, at], sems.at[n]))
+        moves[-1].start()
+    moves[0].wait()
     ids = got[:, STEPS * width : STEPS * width + TR, :].astype(F32)
     names[...] = ids.reshape(patches * TR, BLOCK)
     lane = lax.broadcasted_iota(jnp.int32, (TR, BLOCK), 1)
@@ -81,6 +135,7 @@
     line = lax.broadcasted_iota(jnp.int32, (nblk * TR, patches * width), 0)
     picks[...] = jnp.where(line == spot, 1.0, 0.0).astype(BF16)
     for s in range(STEPS):
+        moves[s + 1].wait()
         sent = got[:, s * width : (s + 1) * width, :].reshape(patches * width, BLOCK)
         total = jnp.dot(picks[...], sent, preferred_element_type=F32)
         coupling[s] = total.reshape(nblk, TR, BLOCK)
@@ -102,11 +157,13 @@
             jax.ShapeDtypeStruct((len(PAIRS), TR, BLOCK), F32),
             jax.ShapeDtypeStruct((len(PAIRS), TR, BLOCK), F32),
         ],
-        in_specs=[VMEM] * 2,
+        in_specs=[pl.BlockSpec(memory_space=pl.ANY), VMEM],
         out_specs=[VMEM] * 3,
         scratch_shapes=[
+            pltpu.VMEM(got.shape, BF16),
             pltpu.VMEM((patches * TR, BLOCK), F32),
             pltpu.VMEM((nblk * TR, patches * width), BF16),
+            pltpu.SemaphoreType.DMA((STEPS + 1,)),
         ],
         compiler_params=PARAMS,
         name="tracts",
@@ -227,18 +284,6 @@
     )
 
 
-def flow_kernel(mine, below, above, vaso, flow, vaso_out, flow_out):
-    total = mine[...] + below[...] + above[...]
-    floor = jnp.maximum(total[STEPS * TR :], 1.0)
-    signal, inflow = vaso[...], flow[...]
-    for step in range(STEPS):
-        level = total[step * TR : (step + 1) * TR] / floor
-        signal = signal + 0.5 * (level - 0.65 * signal - 0.41 * (inflow - 1.0))
-        inflow = inflow + 0.5 * signal
-    vaso_out[...] = signal
-    flow_out[...] = inflow
-
-
 def shards(
     activity,
     history,
@@ -337,13 +382,13 @@
         voxels_here,
     )
     below, above = sides(to_left, to_right)
-    vaso, flow = pl.pallas_call(
-        flow_kernel,
-        out_shape=[jax.ShapeDtypeStruct(vaso_signal.shape, F32)] * 2,
-        in_specs=[VMEM] * 5,
-        out_specs=[VMEM] * 2,
-        name="flow",
-    )(mine, below, above, vaso_signal, blood_flow)
+    total = mine + below + above
+    floor = jnp.maximum(total[STEPS * TR :], 1.0)
+    vaso, flow = vaso_signal, blood_flow
+    for step in range(STEPS):
+        level = total[step * TR : (step + 1) * TR] / floor
+        vaso = vaso + 0.5 * (level - 0.65 * vaso - 0.41 * (flow - 1.0))
+        flow = flow + 0.5 * vaso
     return (rate, vaso, flow)
 
 

time: 183 us -> 183 us (level)
    unnamed x38 -> x36, local copies, waits for them, and re-layouts: 7.22 us -> 6.03 us
    pallas_call x2 -> x1, Pallas kernels: 5.79 us -> 5.1 us  [pack(): pl.pallas_call(pack_kernel, out_shape=jax.ShapeDtypeStruct(shape, BF16),...]
where the time goes in v2:
time: 183 us; the launch traced here: 181 us
  waiting for transfers between devices  73.6 us (40%)
  starting transfers between devices  62.4 us (34%)
  local copies, waits for them, and re-layouts  19.5 us (11%)
  Pallas kernels  16.7 us (9%)
  other arithmetic  7.89 us (4%)
    ppermute x8, waiting for transfers between devices, sides(): return (lax.ppermute(high, 'patch', up), lax.ppermute(low, 'patch', down))  59.6 us
    ppermute x8, starting transfers between devices, sides(): return (lax.ppermute(high, 'patch', up), lax.ppermute(low, 'patch', down))  35.9 us
    ppermute x1, waiting for transfers between devices, shards(): right = lax.ppermute(own, 'trial', counter)  14 us
    all_to_all x1, starting transfers between devices, shards(): got = lax.all_to_all(send, 'patch', split_axis=0, concat_axis=0, tiled=True)  12.4 us
    unnamed x36, local copies, waits for them, and re-layouts  6.03 us
    ppermute x1, starting transfers between devices, shards(): far1 = lax.ppermute(right[half:], 'trial', counter)  5.59 us
    pallas_call x1, Pallas kernels, window(): pl.pallas_call(window_kernel, out_shape=[jax.ShapeDtypeStruct((TR, nblk *...  5.32 us
    pallas_call x1, Pallas kernels, pack(): pl.pallas_call(pack_kernel, out_shape=jax.ShapeDtypeStruct(shape, BF16),...  5.1 us
  transfers between devices with their start and end apart: 13, of which 3 were waited for; matrix products, arithmetic and copies ran while one was open for 11% of the time, Pallas kernels for 6%

profile of v2, /device:TPU:24, one launch (start us, length us, event | category | flops | bytes accessed | tf_op | source)
XLA Modules:
  0.0 181.1 jit_solution(3241831008458804022)
XLA Ops:
  1.6 11.0 %collective-permute-start.3 = (bf16[3,128,128]{2,1,0:T(8,128)(2,1)S(1)}, bf16[3,128,128]{2,1,0:T(8,128)(2,1)S(1)}, u32[]{:S(2)}, u32[]{:S(2)}) collective-permute-start(bf16[3,128,128]{2,1,0:T(8,128)(2,1)S(1)} %get-tuple-element.25), channel_id=1, source_target_pairs={{4,0},{8,4},{12,8},{16,12},{20,16},{24,20},{28,24},{32,28},{36,32}... | collective-permute-start | bytes 294920 | tf_op jit(solution)/shard_map/ppermute | solution.py:316
  12.6 1.9 %collective-permute-start.2 = (bf16[3,128,128]{2,1,0:T(8,128)(2,1)S(1)}, bf16[3,128,128]{2,1,0:T(8,128)(2,1)S(1)}, u32[]{:S(2)}, u32[]{:S(2)}) collective-permute-start(bf16[3,128,128]{2,1,0:T(8,128)(2,1)S(1)} %get-tuple-element.26), channel_id=1, source_target_pairs={{0,4},{4,8},{8,12},{12,16},{16,20},{20,24},{24,28},{28,32},{32,36}... | collective-permute-start | bytes 294920 | tf_op jit(solution)/shard_map/ppermute | solution.py:316
  18.8 5.1 %pack.1 = bf16[128,9,8,128]{3,2,1,0:T(8,128)(2,1)} custom-call(s32[128]{0:T(128)S(1)} %bitcast.29, s32[128]{0:T(128)S(1)} %copy-done.7, s32[128]{0:T(128)S(1)} %copy-done.8, s32[128]{0:T(128)S(1)} %copy-done.9, f32[128]{0:T(128)S(1)} %copy-done.10, bf16[7,8,4096]{2,1,0:T(8,128)(2,1)S(1)} %copy-done.4), custom_call_target="tpu_custom_call" | custom-call | tf_op jit(solution)/shard_map/pack/pallas_call | solution.py:88
  24.0 12.4 %all-to-all-start = ((bf16[128,9,8,128]{3,2,1,0:T(8,128)(2,1)}), bf16[128,9,8,128]{3,2,1,0:T(8,128)(2,1)}, u32[]{:S(2)}, u32[]{:S(2)}) async-start(bf16[128,9,8,128]{3,2,1,0:T(8,128)(2,1)} %pack.1), calls=%async_computation | async-start | bytes 4718592 | tf_op jit(solution)/shard_map/all_to_all | solution.py:324
  38.6 4.7 %collective-permute-start.5 = (bf16[38,128,128]{2,1,0:T(8,128)(2,1)S(1)}, bf16[38,128,128]{2,1,0:T(8,128)(2,1)S(1)}, u32[]{:S(2)}, u32[]{:S(2)}) collective-permute-start(bf16[38,128,128]{2,1,0:T(8,128)(2,1)S(1)} %pad_maximum_fusion.own), channel_id=1, source_target_pairs={{1,0},{2,1},{3,2},{0,3},{5,4},{6,5},{7,6},{4,7},{9,8},{10,9},{11,1... | collective-permute-start | bytes 3735560 | tf_op jit(solution)/shard_map/ppermute | solution.py:329
  43.3 1.9 %collective-permute-start.4 = (bf16[38,128,128]{2,1,0:T(8,128)(2,1)S(1)}, bf16[38,128,128]{2,1,0:T(8,128)(2,1)}, u32[]{:S(2)}, u32[]{:S(2)}) collective-permute-start(bf16[38,128,128]{2,1,0:T(8,128)(2,1)S(1)} %pad_maximum_fusion.own), channel_id=1, source_target_pairs={{0,1},{1,2},{2,3},{3,0},{4,5},{5,6},{6,7},{7,4},{8,9},{9,10},{10,1... | collective-permute-start | bytes 3735560 | tf_op jit(solution)/shard_map/ppermute | solution.py:328
  46.0 1.9 %collective-permute-start = (f32[10,8,128]{2,1,0:T(8,128)}, f32[10,8,128]{2,1,0:T(8,128)}, u32[]{:S(2)}, u32[]{:S(2)}) collective-permute-start(f32[10,8,128]{2,1,0:T(8,128)} %pad_maximum_fusion.3), channel_id=1, source_target_pairs={{0,4},{4,8},{8,12},{12,16},{16,20},{20,24},{24,28},{28,32},{32,36}... | collective-permute-start | bytes 122888 | tf_op jit(solution)/shard_map/ppermute | solution.py:316
  48.7 5.7 %collective-permute-start.1 = (f32[10,8,128]{2,1,0:T(8,128)}, f32[10,8,128]{2,1,0:T(8,128)}, u32[]{:S(2)}, u32[]{:S(2)}) collective-permute-start(f32[10,8,128]{2,1,0:T(8,128)} %pad_maximum_fusion.4), channel_id=1, source_target_pairs={{4,0},{8,4},{12,8},{16,12},{20,16},{24,20},{28,24},{32,28},{36,32}... | collective-permute-start | bytes 122888 | tf_op jit(solution)/shard_map/ppermute | solution.py:316
  56.2 14.0 %collective-permute-done.5.right = bf16[38,128,128]{2,1,0:T(8,128)(2,1)S(1)} collective-permute-done((bf16[38,128,128]{2,1,0:T(8,128)(2,1)S(1)}, bf16[38,128,128]{2,1,0:T(8,128)(2,1)S(1)}, u32[]{:S(2)}, u32[]{:S(2)}) %collective-permute-start.5) | collective-permute-done | bytes 1245216 | tf_op jit(solution)/shard_map/ppermute | solution.py:329
  71.2 5.6 %collective-permute-start.7 = (bf16[19,128,128]{2,1,0:T(8,128)(2,1)}, bf16[19,128,128]{2,1,0:T(8,128)(2,1)}, u32[]{:S(2)}, u32[]{:S(2)}) collective-permute-start(bf16[19,128,128]{2,1,0:T(8,128)(2,1)} %slice.126), channel_id=1, source_target_pairs={{1,0},{2,1},{3,2},{0,3},{5,4},{6,5},{7,6},{4,7},{9,8},{10,9},{11,1... | collective-permute-start | bytes 1867784 | tf_op jit(solution)/shard_map/ppermute | solution.py:331
  76.8 2.0 %slice.125 = bf16[19,128,128]{2,1,0:T(8,128)(2,1)} slice(bf16[38,128,128]{2,1,0:T(8,128)(2,1)} %collective-permute-done.4.left), slice={[0:19], [0:128], [0:128]} | slice | bytes 1245184 | tf_op jit(solution)/shard_map/slice | solution.py:330
  78.8 1.9 %collective-permute-start.6 = (bf16[19,128,128]{2,1,0:T(8,128)(2,1)}, bf16[19,128,128]{2,1,0:T(8,128)(2,1)}, u32[]{:S(2)}, u32[]{:S(2)}) collective-permute-start(bf16[19,128,128]{2,1,0:T(8,128)(2,1)} %slice.125), channel_id=1, source_target_pairs={{0,1},{1,2},{2,3},{3,0},{4,5},{5,6},{6,7},{7,4},{8,9},{9,10},{10,1... | collective-permute-start | bytes 1867784 | tf_op jit(solution)/shard_map/ppermute | solution.py:330
  80.7 58.1 %collective-permute-done = f32[10,8,128]{2,1,0:T(8,128)} collective-permute-done((f32[10,8,128]{2,1,0:T(8,128)}, f32[10,8,128]{2,1,0:T(8,128)}, u32[]{:S(2)}, u32[]{:S(2)}) %collective-permute-start) | collective-permute-done | bytes 40992 | tf_op jit(solution)/shard_map/ppermute | solution.py:316
  140.1 1.4 copy.35
  142.7 1.3 copy.36
  148.3 1.6 pad_maximum_fusion.1.frame.begin
  149.9 3.8 %tracts.1 = (f32[4,32,8,128]{3,2,1,0:T(8,128)S(1)}, f32[6,8,128]{2,1,0:T(8,128)}, f32[6,8,128]{2,1,0:T(8,128)}) custom-call(bf16[128,72,128]{2,1,0:T(8,128)(2,1)} %bitcast.16.here, bf16[256,2048]{1,0:T(8,128)(2,1)S(1)} %compare_convert_fusion.spread), custom_call_target="tpu_custom_call" | custom-call | tf_op jit(solution)/shard_map/tracts/pallas_call | solution.py:153
  154.5 1.9 %collective-permute-start.8 = (f32[6,8,128]{2,1,0:T(8,128)}, f32[6,8,128]{2,1,0:T(8,128)S(1)}, u32[]{:S(2)}, u32[]{:S(2)}) collective-permute-start(f32[6,8,128]{2,1,0:T(8,128)} %get-tuple-element.17), channel_id=1, source_target_pairs={{0,4},{4,8},{8,12},{12,16},{16,20},{20,24},{24,28},{28,32},{32,36}... | collective-permute-start | bytes 73736 | tf_op jit(solution)/shard_map/ppermute | solution.py:316
  156.4 5.8 %collective-permute-start.9 = (f32[6,8,128]{2,1,0:T(8,128)}, f32[6,8,128]{2,1,0:T(8,128)S(1)}, u32[]{:S(2)}, u32[]{:S(2)}) collective-permute-start(f32[6,8,128]{2,1,0:T(8,128)} %get-tuple-element.18), channel_id=1, source_target_pairs={{4,0},{8,4},{12,8},{16,12},{20,16},{24,20},{28,24},{32,28},{36,32}... | collective-permute-start | bytes 73736 | tf_op jit(solution)/shard_map/ppermute | solution.py:316
  163.5 2.5 %start.1.local = f32[38,8,128]{2,1,0:T(8,128)S(1)} custom-call(s32[4]{0:T(128)S(1)} %and_select_fusion.2.place, s32[152]{0:T(256)S(1)} %min.12.index, f32[40,8,128]{2,1,0:T(8,128)S(1)} %copy-done, bf16[38,128,128]{2,1,0:T(8,128)(2,1)S(1)} %pad_maximum_fusion.own, bf16[38,128,128]{2,1,0:T(8,128)(2,1)} %collective-permute-done.4.left, ...), custom_call_target="tpu_custom_call" | custom-call | tf_op jit(solution)/shard_map/start/pallas_call | solution.py:188
  166.0 5.3 %window.1 = (f32[8,4096]{1,0:T(8,128)}, f32[40,128]{1,0:T(8,128)S(1)}, f32[40,128]{1,0:T(8,128)S(1)}, f32[40,128]{1,0:T(8,128)S(1)}) custom-call(s32[4]{0:T(128)S(1)} %and_select_fusion.2.place, s32[152]{0:T(256)S(1)} %min.12.index, f32[2]{0:T(128)S(1)} %add_convert_fusion.flags, s32[1]{0:T(128)} %bitcast.9.offset, f32[40,8,128]{2,1,0:T(8,128)S(1)} %copy-done, ...), custom_call_target="tpu_custom_call" | custom-call | tf_op jit(solution)/shard_map/window/pallas_call | solution.py:266
  171.3 1.9 %collective-permute-start.10 = (f32[40,128]{1,0:T(8,128)S(1)}, f32[40,128]{1,0:T(8,128)S(1)}, u32[]{:S(2)}, u32[]{:S(2)}) collective-permute-start(f32[40,128]{1,0:T(8,128)S(1)} %get-tuple-element.21), channel_id=1, source_target_pairs={{0,4},{4,8},{8,12},{12,16},{16,20},{20,24},{24,28},{28,32},{32,36}... | collective-permute-start | bytes 61448 | tf_op jit(solution)/shard_map/ppermute | solution.py:316
  173.3 5.8 %collective-permute-start.11 = (f32[40,128]{1,0:T(8,128)S(1)}, f32[40,128]{1,0:T(8,128)S(1)}, u32[]{:S(2)}, u32[]{:S(2)}) collective-permute-start(f32[40,128]{1,0:T(8,128)S(1)} %get-tuple-element.22), channel_id=1, source_target_pairs={{4,0},{8,4},{12,8},{16,12},{20,16},{24,20},{28,24},{32,28},{36,32}... | collective-permute-start | bytes 61448 | tf_op jit(solution)/shard_map/ppermute | solution.py:316
  179.0 1.4 collective-permute-done.11
  (81 shorter events, 21.1 us)
Async XLA Ops:
  1.6 22.4 %collective-permute-start.3 = (bf16[3,128,128]{2,1,0:T(8,128)(2,1)S(1)}, bf16[3,128,128]{2,1,0:T(8,128)(2,1)S(1)}, u32[]{:S(2)}, u32[]{:S(2)}) collective-permute-start(bf16[3,128,128]{2,1,0:T(8,128)(2,1)S(1)} %get-tuple-element.25), channel_id=1, source_target_pairs={{4,0},{8,4},{12,8},{16,12},{20,16},{24,20},{28,24},{32,28},{36,32}... | collective-permute-start | bytes 294920 | tf_op jit(solution)/shard_map/ppermute | solution.py:316
  12.6 11.4 %collective-permute-start.2 = (bf16[3,128,128]{2,1,0:T(8,128)(2,1)S(1)}, bf16[3,128,128]{2,1,0:T(8,128)(2,1)S(1)}, u32[]{:S(2)}, u32[]{:S(2)}) collective-permute-start(bf16[3,128,128]{2,1,0:T(8,128)(2,1)S(1)} %get-tuple-element.26), channel_id=1, source_target_pairs={{0,4},{4,8},{8,12},{12,16},{16,20},{20,24},{24,28},{28,32},{32,36}... | collective-permute-start | bytes 294920 | tf_op jit(solution)/shard_map/ppermute | solution.py:316
  14.5 1.0 copy-start.4
  24.0 12.5 %copy-start.17 = (s32[32,4]{0,1:T(4,128)S(1)}, s32[32,4]{0,1:T(4,128)}, u32[]{:S(2)}) copy-start(s32[32,4]{0,1:T(4,128)} %param.21) | copy-start | bytes 1540
  24.0 14.5 %copy-start.11 = (bf16[32,1,128,128]{3,2,1,0:T(8,128)(2,1)S(1)}, bf16[32,1,128,128]{3,2,1,0:T(8,128)(2,1)}, u32[]{:S(2)}) copy-start(bf16[32,1,128,128]{3,2,1,0:T(8,128)(2,1)} %param.20) | copy-start | bytes 3145732
  24.0 125.9 %all-to-all-start = ((bf16[128,9,8,128]{3,2,1,0:T(8,128)(2,1)}), bf16[128,9,8,128]{3,2,1,0:T(8,128)(2,1)}, u32[]{:S(2)}, u32[]{:S(2)}) async-start(bf16[128,9,8,128]{3,2,1,0:T(8,128)(2,1)} %pack.1), calls=%async_computation | async-start | bytes 4718592 | tf_op jit(solution)/shard_map/all_to_all | solution.py:324
  38.6 31.6 %collective-permute-start.5 = (bf16[38,128,128]{2,1,0:T(8,128)(2,1)S(1)}, bf16[38,128,128]{2,1,0:T(8,128)(2,1)S(1)}, u32[]{:S(2)}, u32[]{:S(2)}) collective-permute-start(bf16[38,128,128]{2,1,0:T(8,128)(2,1)S(1)} %pad_maximum_fusion.own), channel_id=1, source_target_pairs={{1,0},{2,1},{3,2},{0,3},{5,4},{6,5},{7,6},{4,7},{9,8},{10,9},{11,1... | collective-permute-start | bytes 3735560 | tf_op jit(solution)/shard_map/ppermute | solution.py:329
  43.3 33.5 %collective-permute-start.4 = (bf16[38,128,128]{2,1,0:T(8,128)(2,1)S(1)}, bf16[38,128,128]{2,1,0:T(8,128)(2,1)}, u32[]{:S(2)}, u32[]{:S(2)}) collective-permute-start(bf16[38,128,128]{2,1,0:T(8,128)(2,1)S(1)} %pad_maximum_fusion.own), channel_id=1, source_target_pairs={{0,1},{1,2},{2,3},{3,0},{4,5},{5,6},{6,7},{7,4},{8,9},{9,10},{10,1... | collective-permute-start | bytes 3735560 | tf_op jit(solution)/shard_map/ppermute | solution.py:328
  46.0 92.8 %collective-permute-start = (f32[10,8,128]{2,1,0:T(8,128)}, f32[10,8,128]{2,1,0:T(8,128)}, u32[]{:S(2)}, u32[]{:S(2)}) collective-permute-start(f32[10,8,128]{2,1,0:T(8,128)} %pad_maximum_fusion.3), channel_id=1, source_target_pairs={{0,4},{4,8},{8,12},{12,16},{16,20},{20,24},{24,28},{28,32},{32,36}... | collective-permute-start | bytes 122888 | tf_op jit(solution)/shard_map/ppermute | solution.py:316
  48.7 92.8 %collective-permute-start.1 = (f32[10,8,128]{2,1,0:T(8,128)}, f32[10,8,128]{2,1,0:T(8,128)}, u32[]{:S(2)}, u32[]{:S(2)}) collective-permute-start(f32[10,8,128]{2,1,0:T(8,128)} %pad_maximum_fusion.4), channel_id=1, source_target_pairs={{4,0},{8,4},{12,8},{16,12},{20,16},{24,20},{28,24},{32,28},{36,32}... | collective-permute-start | bytes 122888 | tf_op jit(solution)/shard_map/ppermute | solution.py:316
  71.2 91.4 %collective-permute-start.7 = (bf16[19,128,128]{2,1,0:T(8,128)(2,1)}, bf16[19,128,128]{2,1,0:T(8,128)(2,1)}, u32[]{:S(2)}, u32[]{:S(2)}) collective-permute-start(bf16[19,128,128]{2,1,0:T(8,128)(2,1)} %slice.126), channel_id=1, source_target_pairs={{1,0},{2,1},{3,2},{0,3},{5,4},{6,5},{7,6},{4,7},{9,8},{10,9},{11,1... | collective-permute-start | bytes 1867784 | tf_op jit(solution)/shard_map/ppermute | solution.py:331
  78.8 83.8 %collective-permute-start.6 = (bf16[19,128,128]{2,1,0:T(8,128)(2,1)}, bf16[19,128,128]{2,1,0:T(8,128)(2,1)}, u32[]{:S(2)}, u32[]{:S(2)}) collective-permute-start(bf16[19,128,128]{2,1,0:T(8,128)(2,1)} %slice.125), channel_id=1, source_target_pairs={{0,1},{1,2},{2,3},{3,0},{4,5},{5,6},{6,7},{7,4},{8,9},{9,10},{10,1... | collective-permute-start | bytes 1867784 | tf_op jit(solution)/shard_map/ppermute | solution.py:330
  149.9 12.3 %copy-start.12 = (s32[32,4]{0,1:T(4,128)S(1)}, s32[32,4]{0,1:T(4,128)}, u32[]{:S(2)}) copy-start(s32[32,4]{0,1:T(4,128)} %get-tuple-element.33) | copy-start | bytes 1540
  149.9 12.3 %copy-start.13 = (s32[3,1,4]{0,2,1:T(4,128)S(1)}, s32[3,1,4]{0,2,1:T(4,128)}, u32[]{:S(2)}) copy-start(s32[3,1,4]{0,2,1:T(4,128)} %copy.35) | copy-start | bytes 148
  149.9 12.3 %copy-start.14 = (s32[3,1,4]{0,2,1:T(4,128)S(1)}, s32[3,1,4]{0,2,1:T(4,128)}, u32[]{:S(2)}) copy-start(s32[3,1,4]{0,2,1:T(4,128)} %copy.36) | copy-start | bytes 148
  154.5 11.4 %collective-permute-start.8 = (f32[6,8,128]{2,1,0:T(8,128)}, f32[6,8,128]{2,1,0:T(8,128)S(1)}, u32[]{:S(2)}, u32[]{:S(2)}) collective-permute-start(f32[6,8,128]{2,1,0:T(8,128)} %get-tuple-element.17), channel_id=1, source_target_pairs={{0,4},{4,8},{8,12},{12,16},{16,20},{20,24},{24,28},{28,32},{32,36}... | collective-permute-start | bytes 73736 | tf_op jit(solution)/shard_map/ppermute | solution.py:316
  156.4 9.5 %collective-permute-start.9 = (f32[6,8,128]{2,1,0:T(8,128)}, f32[6,8,128]{2,1,0:T(8,128)S(1)}, u32[]{:S(2)}, u32[]{:S(2)}) collective-permute-start(f32[6,8,128]{2,1,0:T(8,128)} %get-tuple-element.18), channel_id=1, source_target_pairs={{4,0},{8,4},{12,8},{16,12},{20,16},{24,20},{28,24},{32,28},{36,32}... | collective-permute-start | bytes 73736 | tf_op jit(solution)/shard_map/ppermute | solution.py:316
  162.4 3.6 %copy-start.5 = (s32[4096]{0:T(1024)S(1)}, s32[4096]{0:T(1024)}, u32[]{:S(2)}) copy-start(s32[4096]{0:T(1024)} %param.27) | copy-start | bytes 49156
  163.5 2.5 %copy-start.1 = (f32[38,8,128]{2,1,0:T(8,128)S(1)}, f32[38,8,128]{2,1,0:T(8,128)}, u32[]{:S(2)}) copy-start(f32[38,8,128]{2,1,0:T(8,128)} %pad_maximum_fusion.2.drive) | copy-start | bytes 466948
  163.5 2.5 %copy-start.3 = (f32[4,32,8,128]{3,2,1,0:T(8,128)S(1)}, f32[4,32,8,128]{3,2,1,0:T(8,128)}, u32[]{:S(2)}) copy-start(f32[4,32,8,128]{3,2,1,0:T(8,128)} %copy-done.2) | copy-start | bytes 1572868
  166.0 14.5 %copy-start.15 = (f32[8,128]{1,0:T(8,128)S(1)}, f32[8,128]{1,0:T(8,128)}, u32[]{:S(2)}) copy-start(f32[8,128]{1,0:T(8,128)} %param.29) | copy-start | bytes 12292
  166.0 14.5 %copy-start.16 = (f32[8,128]{1,0:T(8,128)S(1)}, f32[8,128]{1,0:T(8,128)}, u32[]{:S(2)}) copy-start(f32[8,128]{1,0:T(8,128)} %param.28) | copy-start | bytes 12292
  171.3 7.7 %collective-permute-start.10 = (f32[40,128]{1,0:T(8,128)S(1)}, f32[40,128]{1,0:T(8,128)S(1)}, u32[]{:S(2)}, u32[]{:S(2)}) collective-permute-start(f32[40,128]{1,0:T(8,128)S(1)} %get-tuple-element.21), channel_id=1, source_target_pairs={{0,4},{4,8},{8,12},{12,16},{16,20},{20,24},{24,28},{28,32},{32,36}... | collective-permute-start | bytes 61448 | tf_op jit(solution)/shard_map/ppermute | solution.py:316
  173.3 7.2 %collective-permute-start.11 = (f32[40,128]{1,0:T(8,128)S(1)}, f32[40,128]{1,0:T(8,128)S(1)}, u32[]{:S(2)}, u32[]{:S(2)}) collective-permute-start(f32[40,128]{1,0:T(8,128)S(1)} %get-tuple-element.22), channel_id=1, source_target_pairs={{4,0},{8,4},{12,8},{16,12},{20,16},{24,20},{28,24},{32,28},{36,32}... | collective-permute-start | bytes 61448 | tf_op jit(solution)/shard_map/ppermute | solution.py:316
  (7 other events, 5.0 us)

commit v3 on v2

--- a/solution.py
+++ b/solution.py
@@ -15,27 +15,26 @@
 
 SMEM = pl.BlockSpec(memory_space=pltpu.SMEM)
 VMEM = pl.BlockSpec(memory_space=pltpu.VMEM)
+HBM = pl.BlockSpec(memory_space=pltpu.HBM)
 PARAMS = pltpu.CompilerParams(vmem_limit_bytes=48 * 1024 * 1024)
 
 
 def pack_kernel(
     target, source, delay, block, weight, history, out,
-    to_s, source_s, delay_s, block_s, weight_s, rates, tiles, names, count, rank_s, sems,
+    to_s, source_s, delay_s, block_s, weight_s, rates, tiles, names, count, from_s, sems,
 ):
-    patches = out.shape[0]
-    moves = [
-        pltpu.make_async_copy(a, b, sems.at[n])
-        for n, (a, b) in enumerate(
-            (
-                (target, to_s),
-                (block, block_s),
-                (source, source_s),
-                (delay, delay_s),
-                (weight, weight_s),
-                (history, rates),
-            )
-        )
-    ]
+    patches = names.shape[0]
+    per = 2 * STEPS + 1
+    nblk = rates.shape[0] // 7
+    pairs = (
+        (target, to_s),
+        (block, block_s),
+        (source, source_s),
+        (delay, delay_s),
+        (weight, weight_s),
+        (history, rates),
+    )
+    moves = [pltpu.make_async_copy(a, b, sems.at[n]) for n, (a, b) in enumerate(pairs)]
     for move in moves:
         move.start()
     tiles[...] = jnp.zeros_like(tiles)
@@ -46,50 +45,53 @@
         return carry
 
     lax.fori_loop(0, patches, clear, 0, unroll=16)
-    moves[0].wait()
-    moves[1].wait()
+    for move in moves[:4]:
+        move.wait()
 
     def place(i, carry):
         to = to_s[i]
         rank = count[to]
         count[to] = rank + 1
-        rank_s[i] = rank
         name = (block_s[i] + 1).astype(F32)
         names[to, pl.ds(rank, 1), :] = jnp.full((1, BLOCK), name)
+        from_s[i] = (delay_s[i] - 1) * nblk + source_s[i]
+        to_s[i] = to * per + rank
         return carry
 
     lax.fori_loop(0, to_s.shape[0], place, 0, unroll=8)
-    for move in moves[2:]:
+    for move in moves[4:]:
         move.wait()
-    done = []
-    for step in range(STEPS):
+    out_moves = []
+    for part in range(2):
+        steps = (2 * part, 2 * part + 1)
 
         def tract(i, carry):
-            lanes = pl.ds(pl.multiple_of(source_s[i] * BLOCK, BLOCK), BLOCK)
-            rows = rates[delay_s[i] - step - 1, :, lanes].astype(F32)
-            tiles[to_s[i], 2 * step + rank_s[i]] = (rows * weight_s[i]).astype(BF16)
+            start, slot, scale = from_s[i], to_s[i], weight_s[i]
+            for step in steps:
+                rows = rates[start - step * nblk].astype(F32)
+                tiles[slot + 2 * step] = (rows * scale).astype(BF16)
             return carry
 
         lax.fori_loop(0, to_s.shape[0], tract, 0, unroll=8)
-        at = pl.ds(2 * step, 2)
-        done.append(pltpu.make_async_copy(tiles.at[:, at], out.at[:, at], sems.at[6 + step]))
-        done[-1].start()
-    tiles[:, 2 * STEPS] = names[...].astype(BF16)
-    at = pl.ds(2 * STEPS, 1)
-    done.append(pltpu.make_async_copy(tiles.at[:, at], out.at[:, at], sems.at[6 + STEPS]))
-    done[-1].start()
-    for move in done:
-        move.wait()
+        if part:
+            for p in range(patches):
+                tiles[p * per + per - 1] = names[p].astype(BF16)
+    move = pltpu.make_async_copy(tiles, out, sems.at[6])
+    move.start()
+    move.wait()
 
 
 def pack(target, source, delay, block, weight, history, patches):
     count = target.shape[0]
-    shape = (patches, 2 * STEPS + 1, TR, BLOCK)
+    lags, trials, verts = history.shape
+    history = history.reshape(lags, trials, verts // BLOCK, BLOCK).transpose(0, 2, 1, 3)
+    history = history.reshape(-1, trials, BLOCK)
+    shape = (patches * (2 * STEPS + 1), TR, BLOCK)
     return pl.pallas_call(
         pack_kernel,
         out_shape=jax.ShapeDtypeStruct(shape, BF16),
-        in_specs=[pl.BlockSpec(memory_space=pl.ANY)] * 6,
-        out_specs=pl.BlockSpec(memory_space=pl.ANY),
+        in_specs=[HBM] * 6,
+        out_specs=HBM,
         scratch_shapes=[pltpu.SMEM((count,), jnp.int32)] * 4
         + [
             pltpu.SMEM((count,), F32),
@@ -98,25 +100,15 @@
             pltpu.VMEM((patches, TR, BLOCK), F32),
             pltpu.SMEM((patches,), jnp.int32),
             pltpu.SMEM((count,), jnp.int32),
-            pltpu.SemaphoreType.DMA((7 + STEPS,)),
+            pltpu.SemaphoreType.DMA((7,)),
         ],
         compiler_params=PARAMS,
         name="pack",
     )(target, source, delay, block, weight, history)
 
 
-def coupling_kernel(here, spread, coupling, first, last, got, names, picks, sems):
-    patches = got.shape[0]
-    nblk = coupling.shape[1]
+def find_spots(names, spread, patches):
     width = 2 * TR
-    moves = []
-    for n in range(STEPS + 1):
-        at = pl.ds((n - 1) * width if n else STEPS * width, width if n else TR)
-        moves.append(pltpu.make_async_copy(here.at[:, at], got.at[:, at], sems.at[n]))
-        moves[-1].start()
-    moves[0].wait()
-    ids = got[:, STEPS * width : STEPS * width + TR, :].astype(F32)
-    names[...] = ids.reshape(patches * TR, BLOCK)
     lane = lax.broadcasted_iota(jnp.int32, (TR, BLOCK), 1)
     one = jnp.where(lane == 0, 1.0, 0.0).astype(BF16)
     flat = [
@@ -131,42 +123,65 @@
     flat = jnp.concatenate(flat, axis=1).astype(BF16)
     spot = jnp.dot(flat, spread[...], preferred_element_type=F32)[0:1]
     trial = lax.broadcasted_iota(jnp.int32, (1, patches * width), 1) % TR
-    spot = (spot.astype(jnp.int32) - 1) * TR + trial
-    line = lax.broadcasted_iota(jnp.int32, (nblk * TR, patches * width), 0)
+    return (spot.astype(jnp.int32) - 1) * TR + trial
+
+
+def tract_kernel(nblk, here, spread, *rest):
+    outs, (got, names, picks, sems) = rest[:-4], rest[-4:]
+    edges = len(outs) == 2
+    steps = EDGE if edges else STEPS
+    patches = got.shape[0]
+    width = 2 * TR
+    moves = []
+    for n in range(steps + 1):
+        at = pl.ds((n - 1) * width if n else STEPS * width, width if n else TR)
+        moves.append(pltpu.make_async_copy(here.at[:, at], got.at[:, at], sems.at[n]))
+        moves[-1].start()
+    moves[0].wait()
+    ids = got[:, STEPS * width : STEPS * width + TR, :].astype(F32)
+    names[...] = ids.reshape(patches * TR, BLOCK)
+    spot = find_spots(names, spread, patches)
+    line = lax.broadcasted_iota(jnp.int32, picks.shape, 0)
+    if edges:
+        line = jnp.where(line < EDGE * TR, line, line + (nblk - 2 * EDGE) * TR)
     picks[...] = jnp.where(line == spot, 1.0, 0.0).astype(BF16)
-    for s in range(STEPS):
+    for s in range(steps):
         moves[s + 1].wait()
         sent = got[:, s * width : (s + 1) * width, :].reshape(patches * width, BLOCK)
         total = jnp.dot(picks[...], sent, preferred_element_type=F32)
-        coupling[s] = total.reshape(nblk, TR, BLOCK)
-    for n, (s, i) in enumerate(PAIRS):
-        first[n] = coupling[s, i]
-        last[n] = coupling[s, nblk - EDGE + s + i]
-
-
-def tract_sums(got, nblk):
+        if not edges:
+            outs[0][s] = total.reshape(nblk, TR, BLOCK)
+            continue
+        for i in range(EDGE - s):
+            n = PAIRS.index((s, i))
+            outs[0][n] = total[i * TR : (i + 1) * TR]
+            outs[1][n] = total[(EDGE + s + i) * TR : (EDGE + s + i + 1) * TR]
+
+
+def tract_sums(got, nblk, edges):
     patches = got.shape[0]
     width = 2 * TR
     column = jnp.arange(patches * width, dtype=jnp.int32)[None, :]
     line = jnp.arange(2 * patches, dtype=jnp.int32)[:, None]
     spread = (column // TR == (line % patches) * 2 + line // patches).astype(BF16)
+
+    def kernel(*refs):
+        tract_kernel(nblk, *refs)
+
+    shapes = [(len(PAIRS), TR, BLOCK)] * 2 if edges else [(STEPS, nblk, TR, BLOCK)]
     return pl.pallas_call(
-        coupling_kernel,
-        out_shape=[
-            jax.ShapeDtypeStruct((STEPS, nblk, TR, BLOCK), F32),
-            jax.ShapeDtypeStruct((len(PAIRS), TR, BLOCK), F32),
-            jax.ShapeDtypeStruct((len(PAIRS), TR, BLOCK), F32),
-        ],
-        in_specs=[pl.BlockSpec(memory_space=pl.ANY), VMEM],
-        out_specs=[VMEM] * 3,
+        kernel,
+        out_shape=[jax.ShapeDtypeStruct(shape, F32) for shape in shapes],
+        in_specs=[HBM, VMEM],
+        out_specs=[VMEM] * len(shapes),
         scratch_shapes=[
             pltpu.VMEM(got.shape, BF16),
             pltpu.VMEM((patches * TR, BLOCK), F32),
-            pltpu.VMEM((nblk * TR, patches * width), BF16),
+            pltpu.VMEM(((2 * EDGE if edges else nblk) * TR, patches * width), BF16),
             pltpu.SemaphoreType.DMA((STEPS + 1,)),
         ],
         compiler_params=PARAMS,
-        name="tracts",
+        name="edges" if edges else "tracts",
     )(got, spread)
 
 
@@ -321,6 +336,8 @@
         tract_target[:, 0], tract_source, tract_delay, tract_block, tract_weight, history, patches
     )
     send, before, after = lax.optimization_barrier((send, before, after))
+    rows = (2 * STEPS + 1) * TR
+    send = send.reshape(patches, rows, BLOCK)
     got = lax.all_to_all(send, "patch", split_axis=0, concat_axis=0, tiled=True)
 
     own = jnp.concatenate([before, raw, after], axis=0)
@@ -361,9 +378,10 @@
     offset = ((patch - 1) * voxels_here).reshape(1)
     local = start_local(place, index, begin, tiles)
 
-    rows = (2 * STEPS + 1) * TR
-    coupling, first, last = tract_sums(got.reshape(patches, rows, BLOCK), nblk)
+    got, local = lax.optimization_barrier((got, local))
+    first, last = tract_sums(got, nblk, True)
     below, above = sides(first, last)
+    [coupling] = tract_sums(got, nblk, False)
     rate, mine, to_left, to_right = window(
         place,
         index,

time: 183 us -> 179 us (0.978)
  waiting for transfers between devices: 73.6 us -> 76.2 us
  local copies, waits for them, and re-layouts: 19.5 us -> 16.9 us
    ppermute x1, waiting for transfers between devices: 0.01 us -> 16.4 us  [shards(): left = lax.ppermute(own, 'trial', clock)]
    ppermute x1, waiting for transfers between devices: 14 us -> 0.01 us  [shards(): right = lax.ppermute(own, 'trial', counter)]
    ppermute x8, starting transfers between devices: 35.9 us -> 33.1 us  [sides(): return (lax.ppermute(high, 'patch', up), lax.ppermute(low, 'patch', down))]
    pallas_call x1, Pallas kernels: 5.1 us -> 3.07 us  [pack(): pl.pallas_call(pack_kernel, out_shape=jax.ShapeDtypeStruct(shape, BF16),...]
    concatenate x1, other arithmetic: 0.16 us -> 2.1 us  [shards(): own = jnp.concatenate([before, raw, after], axis=0)]
    unnamed x36 -> x46, local copies, waits for them, and re-layouts: 6.03 us -> 7.75 us
    pallas_call x1 -> x2, Pallas kernels: 3.81 us -> 3.74 us  [tract_sums(): pl.pallas_call(kernel, out_shape=[jax.ShapeDtypeStruct(shape, F32) for sh...]
  transfers between devices with their start and end apart: 13 -> 13, of which waited for: 3 -> 4; matrix products, arithmetic and copies ran while one was open for 11% -> 8% of each run, Pallas kernels for 6% -> 5%
where the time goes in v3:
time: 179 us; the launch traced here: 178 us
  waiting for transfers between devices  76.2 us (43%)
  starting transfers between devices  61.1 us (34%)
  local copies, waits for them, and re-layouts  16.9 us (9%)
  Pallas kernels  16 us (9%)
  other arithmetic  6.5 us (4%)
    ppermute x8, waiting for transfers between devices, sides(): return (lax.ppermute(high, 'patch', up), lax.ppermute(low, 'patch', down))  59.8 us
    ppermute x8, starting transfers between devices, sides(): return (lax.ppermute(high, 'patch', up), lax.ppermute(low, 'patch', down))  33.1 us
    ppermute x1, waiting for transfers between devices, shards(): left = lax.ppermute(own, 'trial', clock)  16.4 us
    all_to_all x1, starting transfers between devices, shards(): got = lax.all_to_all(send, 'patch', split_axis=0, concat_axis=0, tiled=True)  13.8 us
    unnamed x46, local copies, waits for them, and re-layouts  7.75 us
    pallas_call x1, Pallas kernels, window(): pl.pallas_call(window_kernel, out_shape=[jax.ShapeDtypeStruct((TR, nblk *...  6.05 us
    ppermute x1, starting transfers between devices, shards(): far1 = lax.ppermute(right[half:], 'trial', counter)  4.85 us
    pallas_call x2, Pallas kernels, tract_sums(): pl.pallas_call(kernel, out_shape=[jax.ShapeDtypeStruct(shape, F32) for sh...  3.74 us
  transfers between devices with their start and end apart: 13, of which 4 were waited for; matrix products, arithmetic and copies ran while one was open for 8% of the time, Pallas kernels for 5%

profile of v3, /device:TPU:24, one launch (start us, length us, event | category | flops | bytes accessed | tf_op | source)
XLA Modules:
  0.0 177.8 jit_solution(12061851492010199396)
XLA Ops:
  1.6 1.9 %collective-permute-start.2 = (bf16[3,128,128]{2,1,0:T(8,128)(2,1)S(1)}, bf16[3,128,128]{2,1,0:T(8,128)(2,1)S(1)}, u32[]{:S(2)}, u32[]{:S(2)}) collective-permute-start(bf16[3,128,128]{2,1,0:T(8,128)(2,1)S(1)} %get-tuple-element.28), channel_id=1, source_target_pairs={{0,4},{4,8},{8,12},{12,16},{16,20},{20,24},{24,28},{28,32},{32,36}... | collective-permute-start | bytes 294920 | tf_op jit(solution)/shard_map/ppermute | solution.py:331
  3.5 11.0 %collective-permute-start.3 = (bf16[3,128,128]{2,1,0:T(8,128)(2,1)S(1)}, bf16[3,128,128]{2,1,0:T(8,128)(2,1)S(1)}, u32[]{:S(2)}, u32[]{:S(2)}) collective-permute-start(bf16[3,128,128]{2,1,0:T(8,128)(2,1)S(1)} %get-tuple-element.27), channel_id=1, source_target_pairs={{4,0},{8,4},{12,8},{16,12},{20,16},{24,20},{28,24},{32,28},{36,32}... | collective-permute-start | bytes 294920 | tf_op jit(solution)/shard_map/ppermute | solution.py:331
  18.8 3.1 %pack.1 = bf16[1152,8,128]{2,1,0:T(8,128)(2,1)S(1)} custom-call(s32[128]{0:T(128)S(1)} %bitcast.36, s32[128]{0:T(128)S(1)} %copy-done.8, s32[128]{0:T(128)S(1)} %copy-done.9, s32[128]{0:T(128)S(1)} %copy-done.10, f32[128]{0:T(128)S(1)} %copy-done.11, bf16[224,8,128]{2,1,0:T(8,128)(2,1)S(1)} %bitcast.34), custom_call_target="tpu_custom_call" | custom-call | tf_op jit(solution)/shard_map/pack/pallas_call | solution.py:90
  24.0 13.8 %all-to-all-start = ((bf16[128,72,128]{2,1,0:T(8,128)(2,1)}), bf16[128,72,128]{2,1,0:T(8,128)(2,1)S(1)}, u32[]{:S(2)}, u32[]{:S(2)}) async-start(bf16[128,72,128]{2,1,0:T(8,128)(2,1)} %bitcast.33), calls=%async_computation | async-start | bytes 4718592 | tf_op jit(solution)/shard_map/all_to_all | solution.py:341
  39.7 2.1 %pad_maximum_fusion.own = bf16[38,128,128]{2,1,0:T(8,128)(2,1)} fusion(bf16[3,128,128]{2,1,0:T(8,128)(2,1)} %copy-done.13, bf16[32,128,128]{2,1,0:T(8,128)(2,1)S(1)} %bitcast.38, bf16[3,128,128]{2,1,0:T(8,128)(2,1)S(1)} %collective-permute-done.2), kind=kLoop, calls=%fused_computation.1 | loop fusion | flops 1245184 | bytes 2490368 | tf_op jit(solution)/shard_map/concatenate | solution.py:343
  41.8 3.5 %collective-permute-start.4 = (bf16[38,128,128]{2,1,0:T(8,128)(2,1)}, bf16[38,128,128]{2,1,0:T(8,128)(2,1)}, u32[]{:S(2)}, u32[]{:S(2)}) collective-permute-start(bf16[38,128,128]{2,1,0:T(8,128)(2,1)} %pad_maximum_fusion.own), channel_id=1, source_target_pairs={{0,1},{1,2},{2,3},{3,0},{4,5},{5,6},{6,7},{7,4},{8,9},{9,10},{10,1... | collective-permute-start | bytes 3735560 | tf_op jit(solution)/shard_map/ppermute | solution.py:345
  45.4 3.7 %collective-permute-start.5 = (bf16[38,128,128]{2,1,0:T(8,128)(2,1)}, bf16[38,128,128]{2,1,0:T(8,128)(2,1)}, u32[]{:S(2)}, u32[]{:S(2)}) collective-permute-start(bf16[38,128,128]{2,1,0:T(8,128)(2,1)} %pad_maximum_fusion.own), channel_id=1, source_target_pairs={{1,0},{2,1},{3,2},{0,3},{5,4},{6,5},{7,6},{4,7},{9,8},{10,9},{11,1... | collective-permute-start | bytes 3735560 | tf_op jit(solution)/shard_map/ppermute | solution.py:346
  50.5 4.0 %collective-permute-start.1 = (f32[10,8,128]{2,1,0:T(8,128)}, f32[10,8,128]{2,1,0:T(8,128)S(1)}, u32[]{:S(2)}, u32[]{:S(2)}) collective-permute-start(f32[10,8,128]{2,1,0:T(8,128)} %pad_maximum_fusion.4), channel_id=1, source_target_pairs={{4,0},{8,4},{12,8},{16,12},{20,16},{24,20},{28,24},{32,28},{36,32}... | collective-permute-start | bytes 122888 | tf_op jit(solution)/shard_map/ppermute | solution.py:331
  55.9 1.9 %collective-permute-start = (f32[10,8,128]{2,1,0:T(8,128)}, f32[10,8,128]{2,1,0:T(8,128)S(1)}, u32[]{:S(2)}, u32[]{:S(2)}) collective-permute-start(f32[10,8,128]{2,1,0:T(8,128)} %pad_maximum_fusion.3), channel_id=1, source_target_pairs={{0,4},{4,8},{8,12},{12,16},{16,20},{20,24},{24,28},{28,32},{32,36}... | collective-permute-start | bytes 122888 | tf_op jit(solution)/shard_map/ppermute | solution.py:331
  58.4 16.4 %collective-permute-done.4.left = bf16[38,128,128]{2,1,0:T(8,128)(2,1)} collective-permute-done((bf16[38,128,128]{2,1,0:T(8,128)(2,1)}, bf16[38,128,128]{2,1,0:T(8,128)(2,1)}, u32[]{:S(2)}, u32[]{:S(2)}) %collective-permute-start.4) | collective-permute-done | bytes 1245216 | tf_op jit(solution)/shard_map/ppermute | solution.py:345
  74.8 2.0 %slice.125 = bf16[19,128,128]{2,1,0:T(8,128)(2,1)} slice(bf16[38,128,128]{2,1,0:T(8,128)(2,1)} %collective-permute-done.4.left), slice={[0:19], [0:128], [0:128]} | slice | bytes 1245184 | tf_op jit(solution)/shard_map/slice | solution.py:347
  76.8 2.2 %collective-permute-start.6 = (bf16[19,128,128]{2,1,0:T(8,128)(2,1)}, bf16[19,128,128]{2,1,0:T(8,128)(2,1)}, u32[]{:S(2)}, u32[]{:S(2)}) collective-permute-start(bf16[19,128,128]{2,1,0:T(8,128)(2,1)} %slice.125), channel_id=1, source_target_pairs={{0,1},{1,2},{2,3},{3,0},{4,5},{5,6},{6,7},{7,4},{8,9},{9,10},{10,1... | collective-permute-start | bytes 1867784 | tf_op jit(solution)/shard_map/ppermute | solution.py:347
  79.0 2.0 %slice.126 = bf16[19,128,128]{2,1,0:T(8,128)(2,1)} slice(bf16[38,128,128]{2,1,0:T(8,128)(2,1)} %collective-permute-done.5.right), slice={[19:38], [0:128], [0:128]} | slice | bytes 1245184 | tf_op jit(solution)/shard_map/slice | solution.py:348
  81.0 4.9 %collective-permute-start.7 = (bf16[19,128,128]{2,1,0:T(8,128)(2,1)}, bf16[19,128,128]{2,1,0:T(8,128)(2,1)}, u32[]{:S(2)}, u32[]{:S(2)}) collective-permute-start(bf16[19,128,128]{2,1,0:T(8,128)(2,1)} %slice.126), channel_id=1, source_target_pairs={{1,0},{2,1},{3,2},{0,3},{5,4},{6,5},{7,6},{4,7},{9,8},{10,9},{11,1... | collective-permute-start | bytes 1867784 | tf_op jit(solution)/shard_map/ppermute | solution.py:348
  85.9 50.3 %collective-permute-done.1 = f32[10,8,128]{2,1,0:T(8,128)S(1)} collective-permute-done((f32[10,8,128]{2,1,0:T(8,128)}, f32[10,8,128]{2,1,0:T(8,128)S(1)}, u32[]{:S(2)}, u32[]{:S(2)}) %collective-permute-start.1) | collective-permute-done | bytes 40992 | tf_op jit(solution)/shard_map/ppermute | solution.py:331
  136.3 4.2 %collective-permute-done = f32[10,8,128]{2,1,0:T(8,128)S(1)} collective-permute-done((f32[10,8,128]{2,1,0:T(8,128)}, f32[10,8,128]{2,1,0:T(8,128)S(1)}, u32[]{:S(2)}, u32[]{:S(2)}) %collective-permute-start) | collective-permute-done | bytes 40992 | tf_op jit(solution)/shard_map/ppermute | solution.py:331
  143.1 3.2 %start.1.local = f32[38,8,128]{2,1,0:T(8,128)S(1)} custom-call(s32[4]{0:T(128)S(1)} %and_select_fusion.2.place, s32[152]{0:T(256)S(1)} %min.12.index, f32[40,8,128]{2,1,0:T(8,128)S(1)} %pad_maximum_fusion.1.frame.begin, bf16[38,128,128]{2,1,0:T(8,128)(2,1)} %pad_maximum_fusion.own, bf16[38,128,128]{2,1,0:T(8,128)(2,1)} %collective-permute-done.4.left, ...), custom_call_target="tpu_custom_call" | custom-call | tf_op jit(solution)/shard_map/start/pallas_call | solution.py:203
  148.9 1.9 %collective-permute-start.8 = (f32[6,8,128]{2,1,0:T(8,128)S(1)}, f32[6,8,128]{2,1,0:T(8,128)S(1)}, u32[]{:S(2)}, u32[]{:S(2)}) collective-permute-start(f32[6,8,128]{2,1,0:T(8,128)S(1)} %get-tuple-element.19), channel_id=1, source_target_pairs={{0,4},{4,8},{8,12},{12,16},{16,20},{20,24},{24,28},{28,32},{32,36}... | collective-permute-start | bytes 73736 | tf_op jit(solution)/shard_map/ppermute | solution.py:331
  150.8 5.8 %collective-permute-start.9 = (f32[6,8,128]{2,1,0:T(8,128)S(1)}, f32[6,8,128]{2,1,0:T(8,128)S(1)}, u32[]{:S(2)}, u32[]{:S(2)}) collective-permute-start(f32[6,8,128]{2,1,0:T(8,128)S(1)} %get-tuple-element.20), channel_id=1, source_target_pairs={{4,0},{8,4},{12,8},{16,12},{20,16},{24,20},{28,24},{32,28},{36,32}... | collective-permute-start | bytes 73736 | tf_op jit(solution)/shard_map/ppermute | solution.py:331
  156.7 2.5 %tracts.1.coupling = f32[4,32,8,128]{3,2,1,0:T(8,128)S(1)} custom-call(bf16[128,72,128]{2,1,0:T(8,128)(2,1)S(1)} %all-to-all-done.refs_0_, bf16[256,2048]{1,0:T(8,128)(2,1)S(1)} %compare_convert_fusion.refs_1_), custom_call_target="tpu_custom_call" | custom-call | tf_op jit(solution)/shard_map/tracts/pallas_call | solution.py:172
  159.2 6.1 %window.1 = (f32[8,4096]{1,0:T(8,128)}, f32[40,128]{1,0:T(8,128)S(1)}, f32[40,128]{1,0:T(8,128)S(1)}, f32[40,128]{1,0:T(8,128)S(1)}) custom-call(s32[4]{0:T(128)S(1)} %and_select_fusion.2.place, s32[152]{0:T(256)S(1)} %min.12.index, f32[2]{0:T(128)S(1)} %add_convert_fusion.flags, s32[1]{0:T(128)} %bitcast.9.offset, f32[40,8,128]{2,1,0:T(8,128)S(1)} %copy-done.2, ...), custom_call_target="tpu_custom_call" | custom-call | tf_op jit(solution)/shard_map/window/pallas_call | solution.py:281
  165.3 4.6 %collective-permute-start.11 = (f32[40,128]{1,0:T(8,128)S(1)}, f32[40,128]{1,0:T(8,128)S(1)}, u32[]{:S(2)}, u32[]{:S(2)}) collective-permute-start(f32[40,128]{1,0:T(8,128)S(1)} %get-tuple-element.24), channel_id=1, source_target_pairs={{4,0},{8,4},{12,8},{16,12},{20,16},{24,20},{28,24},{32,28},{36,32}... | collective-permute-start | bytes 61448 | tf_op jit(solution)/shard_map/ppermute | solution.py:331
  169.9 1.9 %collective-permute-start.10 = (f32[40,128]{1,0:T(8,128)S(1)}, f32[40,128]{1,0:T(8,128)S(1)}, u32[]{:S(2)}, u32[]{:S(2)}) collective-permute-start(f32[40,128]{1,0:T(8,128)S(1)} %get-tuple-element.23), channel_id=1, source_target_pairs={{0,4},{4,8},{8,12},{12,16},{16,20},{20,24},{24,28},{28,32},{32,36}... | collective-permute-start | bytes 61448 | tf_op jit(solution)/shard_map/ppermute | solution.py:331
  171.8 5.3 %collective-permute-done.10 = f32[40,128]{1,0:T(8,128)S(1)} collective-permute-done((f32[40,128]{1,0:T(8,128)S(1)}, f32[40,128]{1,0:T(8,128)S(1)}, u32[]{:S(2)}, u32[]{:S(2)}) %collective-permute-start.10) | collective-permute-done | bytes 20512 | tf_op jit(solution)/shard_map/ppermute | solution.py:331
  (94 shorter events, 18.5 us)
Async XLA Ops:
  1.6 21.8 %collective-permute-start.2 = (bf16[3,128,128]{2,1,0:T(8,128)(2,1)S(1)}, bf16[3,128,128]{2,1,0:T(8,128)(2,1)S(1)}, u32[]{:S(2)}, u32[]{:S(2)}) collective-permute-start(bf16[3,128,128]{2,1,0:T(8,128)(2,1)S(1)} %get-tuple-element.28), channel_id=1, source_target_pairs={{0,4},{4,8},{8,12},{12,16},{16,20},{20,24},{24,28},{28,32},{32,36}... | collective-permute-start | bytes 294920 | tf_op jit(solution)/shard_map/ppermute | solution.py:331
  3.5 19.8 %collective-permute-start.3 = (bf16[3,128,128]{2,1,0:T(8,128)(2,1)S(1)}, bf16[3,128,128]{2,1,0:T(8,128)(2,1)S(1)}, u32[]{:S(2)}, u32[]{:S(2)}) collective-permute-start(bf16[3,128,128]{2,1,0:T(8,128)(2,1)S(1)} %get-tuple-element.27), channel_id=1, source_target_pairs={{4,0},{8,4},{12,8},{16,12},{20,16},{24,20},{28,24},{32,28},{36,32}... | collective-permute-start | bytes 294920 | tf_op jit(solution)/shard_map/ppermute | solution.py:331
  24.0 13.8 %copy-start.20 = (s32[32,4]{0,1:T(4,128)S(1)}, s32[32,4]{0,1:T(4,128)}, u32[]{:S(2)}) copy-start(s32[32,4]{0,1:T(4,128)} %param.21) | copy-start | bytes 1540
  24.0 14.4 %copy-start.16 = (f32[4096]{0:T(1024)S(1)}, f32[4096]{0:T(1024)}, u32[]{:S(2)}) copy-start(f32[4096]{0:T(1024)} %param.17) | copy-start | bytes 49156
  24.0 15.7 %copy-start.12 = (bf16[32,1,128,128]{3,2,1,0:T(8,128)(2,1)S(1)}, bf16[32,1,128,128]{3,2,1,0:T(8,128)(2,1)}, u32[]{:S(2)}) copy-start(bf16[32,1,128,128]{3,2,1,0:T(8,128)(2,1)} %param.20) | copy-start | bytes 3145732
  24.0 123.6 %all-to-all-start = ((bf16[128,72,128]{2,1,0:T(8,128)(2,1)}), bf16[128,72,128]{2,1,0:T(8,128)(2,1)S(1)}, u32[]{:S(2)}, u32[]{:S(2)}) async-start(bf16[128,72,128]{2,1,0:T(8,128)(2,1)} %bitcast.33), calls=%async_computation | async-start | bytes 4718592 | tf_op jit(solution)/shard_map/all_to_all | solution.py:341
  41.8 16.4 %copy-start.21 = (f32[8]{0:T(128)S(1)}, f32[8]{0:T(128)}, u32[]{:S(2)}) copy-start(f32[8]{0:T(128)} %param.18) | copy-start | bytes 100
  41.8 16.4 %copy-start.22 = (f32[8]{0:T(128)S(1)}, f32[8]{0:T(128)}, u32[]{:S(2)}) copy-start(f32[8]{0:T(128)} %param.19) | copy-start | bytes 100
  41.8 33.0 %collective-permute-start.4 = (bf16[38,128,128]{2,1,0:T(8,128)(2,1)}, bf16[38,128,128]{2,1,0:T(8,128)(2,1)}, u32[]{:S(2)}, u32[]{:S(2)}) collective-permute-start(bf16[38,128,128]{2,1,0:T(8,128)(2,1)} %pad_maximum_fusion.own), channel_id=1, source_target_pairs={{0,1},{1,2},{2,3},{3,0},{4,5},{5,6},{6,7},{7,4},{8,9},{9,10},{10,1... | collective-permute-start | bytes 3735560 | tf_op jit(solution)/shard_map/ppermute | solution.py:345
  45.4 33.6 %collective-permute-start.5 = (bf16[38,128,128]{2,1,0:T(8,128)(2,1)}, bf16[38,128,128]{2,1,0:T(8,128)(2,1)}, u32[]{:S(2)}, u32[]{:S(2)}) collective-permute-start(bf16[38,128,128]{2,1,0:T(8,128)(2,1)} %pad_maximum_fusion.own), channel_id=1, source_target_pairs={{1,0},{2,1},{3,2},{0,3},{5,4},{6,5},{7,6},{4,7},{9,8},{10,9},{11,1... | collective-permute-start | bytes 3735560 | tf_op jit(solution)/shard_map/ppermute | solution.py:346
  50.5 85.7 %collective-permute-start.1 = (f32[10,8,128]{2,1,0:T(8,128)}, f32[10,8,128]{2,1,0:T(8,128)S(1)}, u32[]{:S(2)}, u32[]{:S(2)}) collective-permute-start(f32[10,8,128]{2,1,0:T(8,128)} %pad_maximum_fusion.4), channel_id=1, source_target_pairs={{4,0},{8,4},{12,8},{16,12},{20,16},{24,20},{28,24},{32,28},{36,32}... | collective-permute-start | bytes 122888 | tf_op jit(solution)/shard_map/ppermute | solution.py:331
  55.9 84.6 %collective-permute-start = (f32[10,8,128]{2,1,0:T(8,128)}, f32[10,8,128]{2,1,0:T(8,128)S(1)}, u32[]{:S(2)}, u32[]{:S(2)}) collective-permute-start(f32[10,8,128]{2,1,0:T(8,128)} %pad_maximum_fusion.3), channel_id=1, source_target_pairs={{0,4},{4,8},{8,12},{12,16},{16,20},{20,24},{24,28},{28,32},{32,36}... | collective-permute-start | bytes 122888 | tf_op jit(solution)/shard_map/ppermute | solution.py:331
  58.4 82.2 %copy-start.17 = (s32[32,4]{0,1:T(4,128)S(1)}, s32[32,4]{0,1:T(4,128)}, u32[]{:S(2)}) copy-start(s32[32,4]{0,1:T(4,128)} %get-tuple-element.35) | copy-start | bytes 1540
  76.8 66.3 %collective-permute-start.6 = (bf16[19,128,128]{2,1,0:T(8,128)(2,1)}, bf16[19,128,128]{2,1,0:T(8,128)(2,1)}, u32[]{:S(2)}, u32[]{:S(2)}) collective-permute-start(bf16[19,128,128]{2,1,0:T(8,128)(2,1)} %slice.125), channel_id=1, source_target_pairs={{0,1},{1,2},{2,3},{3,0},{4,5},{5,6},{6,7},{7,4},{8,9},{9,10},{10,1... | collective-permute-start | bytes 1867784 | tf_op jit(solution)/shard_map/ppermute | solution.py:347
  81.0 62.0 %collective-permute-start.7 = (bf16[19,128,128]{2,1,0:T(8,128)(2,1)}, bf16[19,128,128]{2,1,0:T(8,128)(2,1)}, u32[]{:S(2)}, u32[]{:S(2)}) collective-permute-start(bf16[19,128,128]{2,1,0:T(8,128)(2,1)} %slice.126), channel_id=1, source_target_pairs={{1,0},{2,1},{3,2},{0,3},{5,4},{6,5},{7,6},{4,7},{9,8},{10,9},{11,1... | collective-permute-start | bytes 1867784 | tf_op jit(solution)/shard_map/ppermute | solution.py:348
  136.2 10.1 %copy-start.14 = (f32[10,8,128]{2,1,0:T(8,128)}, f32[10,8,128]{2,1,0:T(8,128)S(1)}, u32[]{:S(2)}) copy-start(f32[10,8,128]{2,1,0:T(8,128)S(1)} %collective-permute-done.1) | copy-start | bytes 122884
  147.6 9.0 %slice-start = ((f32[10,8,128]{2,1,0:T(8,128)}), f32[3,8,128]{2,1,0:T(8,128)S(1)}, s32[]{:S(2)}) async-start(f32[10,8,128]{2,1,0:T(8,128)} %copy-done.14), calls=%async_computation.1 | async-start | bytes 24576 | tf_op jit(solution)/shard_map/slice | solution.py:366
  147.6 9.0 %slice-start.1 = ((f32[10,8,128]{2,1,0:T(8,128)}), f32[3,8,128]{2,1,0:T(8,128)S(1)}, s32[]{:S(2)}) async-start(f32[10,8,128]{2,1,0:T(8,128)} %copy-done.15), calls=%async_computation.2 | async-start | bytes 24576 | tf_op jit(solution)/shard_map/slice | solution.py:366
  148.9 10.3 %collective-permute-start.8 = (f32[6,8,128]{2,1,0:T(8,128)S(1)}, f32[6,8,128]{2,1,0:T(8,128)S(1)}, u32[]{:S(2)}, u32[]{:S(2)}) collective-permute-start(f32[6,8,128]{2,1,0:T(8,128)S(1)} %get-tuple-element.19), channel_id=1, source_target_pairs={{0,4},{4,8},{8,12},{12,16},{16,20},{20,24},{24,28},{28,32},{32,36}... | collective-permute-start | bytes 73736 | tf_op jit(solution)/shard_map/ppermute | solution.py:331
  150.8 8.4 %collective-permute-start.9 = (f32[6,8,128]{2,1,0:T(8,128)S(1)}, f32[6,8,128]{2,1,0:T(8,128)S(1)}, u32[]{:S(2)}, u32[]{:S(2)}) collective-permute-start(f32[6,8,128]{2,1,0:T(8,128)S(1)} %get-tuple-element.20), channel_id=1, source_target_pairs={{4,0},{8,4},{12,8},{16,12},{20,16},{24,20},{28,24},{32,28},{36,32}... | collective-permute-start | bytes 73736 | tf_op jit(solution)/shard_map/ppermute | solution.py:331
  159.2 17.9 %copy-start.18 = (f32[8,128]{1,0:T(8,128)S(1)}, f32[8,128]{1,0:T(8,128)}, u32[]{:S(2)}) copy-start(f32[8,128]{1,0:T(8,128)} %param.29) | copy-start | bytes 12292
  159.2 17.9 %copy-start.19 = (f32[8,128]{1,0:T(8,128)S(1)}, f32[8,128]{1,0:T(8,128)}, u32[]{:S(2)}) copy-start(f32[8,128]{1,0:T(8,128)} %param.28) | copy-start | bytes 12292
  165.3 6.5 %collective-permute-start.11 = (f32[40,128]{1,0:T(8,128)S(1)}, f32[40,128]{1,0:T(8,128)S(1)}, u32[]{:S(2)}, u32[]{:S(2)}) collective-permute-start(f32[40,128]{1,0:T(8,128)S(1)} %get-tuple-element.24), channel_id=1, source_target_pairs={{4,0},{8,4},{12,8},{16,12},{20,16},{24,20},{28,24},{32,28},{36,32}... | collective-permute-start | bytes 61448 | tf_op jit(solution)/shard_map/ppermute | solution.py:331
  169.9 7.2 %collective-permute-start.10 = (f32[40,128]{1,0:T(8,128)S(1)}, f32[40,128]{1,0:T(8,128)S(1)}, u32[]{:S(2)}, u32[]{:S(2)}) collective-permute-start(f32[40,128]{1,0:T(8,128)S(1)} %get-tuple-element.23), channel_id=1, source_target_pairs={{0,4},{4,8},{8,12},{12,16},{16,20},{20,24},{24,28},{28,32},{32,36}... | collective-permute-start | bytes 61448 | tf_op jit(solution)/shard_map/ppermute | solution.py:331
  (14 other events, 21.2 us)

commit v4 on v3

--- a/solution.py
+++ b/solution.py
@@ -10,21 +10,21 @@
 TR = 8
 EDGE = STEPS - 1
 PAIRS = [(s, i) for s in range(EDGE) for i in range(EDGE - s)]
+SHIFTS = (0, 3, 1, 2)
 F32 = jnp.float32
 BF16 = jnp.bfloat16
 
 SMEM = pl.BlockSpec(memory_space=pltpu.SMEM)
 VMEM = pl.BlockSpec(memory_space=pltpu.VMEM)
 HBM = pl.BlockSpec(memory_space=pltpu.HBM)
-PARAMS = pltpu.CompilerParams(vmem_limit_bytes=48 * 1024 * 1024)
+PARAMS = pltpu.CompilerParams(vmem_limit_bytes=16 * 1024 * 1024)
 
 
 def pack_kernel(
     target, source, delay, block, weight, history, out,
-    to_s, source_s, delay_s, block_s, weight_s, rates, tiles, names, count, from_s, sems,
+    to_s, source_s, delay_s, block_s, weight_s, rates, tiles, names, count, from_s, rank_s, sems,
 ):
     patches = names.shape[0]
-    per = 2 * STEPS + 1
     nblk = rates.shape[0] // 7
     pairs = (
         (target, to_s),
@@ -55,30 +55,31 @@
         name = (block_s[i] + 1).astype(F32)
         names[to, pl.ds(rank, 1), :] = jnp.full((1, BLOCK), name)
         from_s[i] = (delay_s[i] - 1) * nblk + source_s[i]
-        to_s[i] = to * per + rank
+        rank_s[i] = rank
         return carry
 
     lax.fori_loop(0, to_s.shape[0], place, 0, unroll=8)
     for move in moves[4:]:
         move.wait()
-    out_moves = []
+    sends = []
     for part in range(2):
         steps = (2 * part, 2 * part + 1)
 
         def tract(i, carry):
-            start, slot, scale = from_s[i], to_s[i], weight_s[i]
+            start, to, rank, scale = from_s[i], to_s[i], rank_s[i], weight_s[i]
             for step in steps:
                 rows = rates[start - step * nblk].astype(F32)
-                tiles[slot + 2 * step] = (rows * scale).astype(BF16)
+                tiles[to, 2 * step + rank] = (rows * scale).astype(BF16)
             return carry
 
         lax.fori_loop(0, to_s.shape[0], tract, 0, unroll=8)
         if part:
-            for p in range(patches):
-                tiles[p * per + per - 1] = names[p].astype(BF16)
-    move = pltpu.make_async_copy(tiles, out, sems.at[6])
-    move.start()
-    move.wait()
+            tiles[:, 2 * STEPS] = names[...].astype(BF16)
+        at = pl.ds(STEPS * part, STEPS + part)
+        sends.append(pltpu.make_async_copy(tiles.at[:, at], out.at[:, at], sems.at[6 + part]))
+        sends[-1].start()
+    for move in sends:
+        move.wait()
 
 
 def pack(target, source, delay, block, weight, history, patches):
@@ -86,10 +87,12 @@
     lags, trials, verts = history.shape
     history = history.reshape(lags, trials, verts // BLOCK, BLOCK).transpose(0, 2, 1, 3)
     history = history.reshape(-1, trials, BLOCK)
-    shape = (patches * (2 * STEPS + 1), TR, BLOCK)
+    shape = (patches, 2 * STEPS + 1, TR, BLOCK)
+    operands = (target, source, delay, block, weight, history)
+    operands = [pltpu.with_memory_space_constraint(x, pltpu.HBM) for x in operands]
     return pl.pallas_call(
         pack_kernel,
-        out_shape=jax.ShapeDtypeStruct(shape, BF16),
+        out_shape=pltpu.HBM(shape, BF16),
         in_specs=[HBM] * 6,
         out_specs=HBM,
         scratch_shapes=[pltpu.SMEM((count,), jnp.int32)] * 4
@@ -100,11 +103,12 @@
             pltpu.VMEM((patches, TR, BLOCK), F32),
             pltpu.SMEM((patches,), jnp.int32),
             pltpu.SMEM((count,), jnp.int32),
-            pltpu.SemaphoreType.DMA((7,)),
+            pltpu.SMEM((count,), jnp.int32),
+            pltpu.SemaphoreType.DMA((8,)),
         ],
         compiler_params=PARAMS,
         name="pack",
-    )(target, source, delay, block, weight, history)
+    )(*operands)
 
 
 def find_spots(names, spread, patches):
@@ -126,18 +130,12 @@
     return (spot.astype(jnp.int32) - 1) * TR + trial
 
 
-def tract_kernel(nblk, here, spread, *rest):
-    outs, (got, names, picks, sems) = rest[:-4], rest[-4:]
+def tract_kernel(nblk, got, spread, *rest):
+    outs, (names, picks) = rest[:-2], rest[-2:]
     edges = len(outs) == 2
     steps = EDGE if edges else STEPS
     patches = got.shape[0]
     width = 2 * TR
-    moves = []
-    for n in range(steps + 1):
-        at = pl.ds((n - 1) * width if n else STEPS * width, width if n else TR)
-        moves.append(pltpu.make_async_copy(here.at[:, at], got.at[:, at], sems.at[n]))
-        moves[-1].start()
-    moves[0].wait()
     ids = got[:, STEPS * width : STEPS * width + TR, :].astype(F32)
     names[...] = ids.reshape(patches * TR, BLOCK)
     spot = find_spots(names, spread, patches)
@@ -146,7 +144,6 @@
         line = jnp.where(line < EDGE * TR, line, line + (nblk - 2 * EDGE) * TR)
     picks[...] = jnp.where(line == spot, 1.0, 0.0).astype(BF16)
     for s in range(steps):
-        moves[s + 1].wait()
         sent = got[:, s * width : (s + 1) * width, :].reshape(patches * width, BLOCK)
         total = jnp.dot(picks[...], sent, preferred_element_type=F32)
         if not edges:
@@ -172,55 +169,85 @@
     return pl.pallas_call(
         kernel,
         out_shape=[jax.ShapeDtypeStruct(shape, F32) for shape in shapes],
-        in_specs=[HBM, VMEM],
+        in_specs=[VMEM] * 2,
         out_specs=[VMEM] * len(shapes),
         scratch_shapes=[
-            pltpu.VMEM(got.shape, BF16),
             pltpu.VMEM((patches * TR, BLOCK), F32),
             pltpu.VMEM(((2 * EDGE if edges else nblk) * TR, patches * width), BF16),
-            pltpu.SemaphoreType.DMA((STEPS + 1,)),
         ],
         compiler_params=PARAMS,
         name="edges" if edges else "tracts",
     )(got, spread)
 
 
-def local_block(j, place, index, frame, own, left, right, far0, far1):
-    rows = [frame[index[4 * j + place[shift]]] for shift in (0, 3, 1, 2)]
+def local_block(j, place, index, frame, tiles):
+    rows = [frame[index[4 * j + place[shift]]] for shift in SHIFTS]
     rows = jnp.concatenate(rows, axis=1).astype(BF16)
+    return jnp.dot(rows, tiles[j], preferred_element_type=F32)
+
+
+def start_kernel(
+    place, index, offset, frame, owner, own, left, right, far0, far1,
+    out, tiles, kept, hits, sems,
+):
     half = far0.shape[0]
-    distant = far0[j] if j < half else far1[j - half]
-    tiles = jnp.concatenate([own[j], left[j], right[j], distant], axis=0)
-    return jnp.dot(rows, tiles, preferred_element_type=F32)
-
-
-def start_kernel(place, index, frame, own, left, right, far0, far1, out):
-    for j in range(own.shape[0]):
-        out[j] = local_block(j, place, index, frame, own, left, right, far0, far1)
-
-
-def start_local(place, index, frame, tiles):
+    ext = own.shape[0]
+    moves = []
+    for n, tile in enumerate((own, left, right)):
+        at = pl.ds(n * BLOCK, BLOCK)
+        moves.append(pltpu.make_async_copy(tile, tiles.at[:, at], sems.at[n]))
+    at = pl.ds(3 * BLOCK, BLOCK)
+    moves.append(pltpu.make_async_copy(far0, tiles.at[pl.ds(0, half), at], sems.at[3]))
+    moves.append(pltpu.make_async_copy(far1, tiles.at[pl.ds(half, ext - half), at], sems.at[4]))
+    for move in moves:
+        move.start()
+    voxels = hits.shape[0]
+    for c in range(0, hits.shape[1], CHUNK):
+        name = owner[:, c : c + CHUNK] - offset[0]
+        hit = lax.broadcasted_iota(jnp.int32, (voxels, CHUNK), 0) == name
+        hits[:, c : c + CHUNK] = jnp.where(hit, 1.0, 0.0).astype(BF16)
+    keep = pltpu.make_async_copy(hits, kept, sems.at[5])
+    keep.start()
+    for move in moves:
+        move.wait()
+    for j in range(ext):
+        out[j] = local_block(j, place, index, frame, tiles)
+    keep.wait()
+
+
+def start_local(place, index, offset, frame, owner, pieces, voxels):
+    ext = pieces[0].shape[0]
+    pieces = [pltpu.with_memory_space_constraint(x, pltpu.HBM) for x in pieces]
     return pl.pallas_call(
         start_kernel,
-        out_shape=jax.ShapeDtypeStruct((tiles[0].shape[0], TR, BLOCK), F32),
-        in_specs=[SMEM] * 2 + [VMEM] * 6,
-        out_specs=VMEM,
+        out_shape=[
+            jax.ShapeDtypeStruct((ext, TR, BLOCK), F32),
+            pltpu.VMEM((ext, 4 * BLOCK, BLOCK), BF16),
+            pltpu.HBM((voxels, owner.shape[1]), BF16),
+        ],
+        in_specs=[SMEM] * 3 + [VMEM] * 2 + [HBM] * 5,
+        out_specs=[VMEM] * 2 + [HBM],
+        scratch_shapes=[
+            pltpu.VMEM((voxels, owner.shape[1]), BF16),
+            pltpu.SemaphoreType.DMA((6,)),
+        ],
         compiler_params=PARAMS,
         name="start",
-    )(place, index, frame, *tiles)
+    )(place, index, offset, frame, owner, *pieces)
 
 
 CHUNK = 512
 
 
 def window_kernel(
-    place, index, flags, offset, begin, local, coupling, below, above,
-    own, left, right, far0, far1, drive, slope, strength, owner,
-    rate, mine, to_left, to_right, frame, sums, parts,
+    place, index, flags, begin, local, coupling, below, above,
+    tiles, drive, slope, strength, kept,
+    rate, mine, to_left, to_right, frame, sums, parts, hits, sem,
 ):
-    ext = own.shape[0]
+    ext = tiles.shape[0]
     nblk = ext - 2 * EDGE
-    tiles = (own, left, right, far0, far1)
+    fetch = pltpu.make_async_copy(kept, hits, sem)
+    fetch.start()
     frame[...] = begin[...]
     steep = jnp.broadcast_to(slope[...], (TR, BLOCK))
     strong = jnp.broadcast_to(strength[...], (TR, BLOCK))
@@ -228,7 +255,7 @@
         blocks = range(step, ext - step)
         if step > 0:
             for j in blocks:
-                sums[j] = local_block(j, place, index, frame, *tiles)
+                sums[j] = local_block(j, place, index, frame, tiles)
         for j in blocks:
             if j < EDGE:
                 tracts = below[PAIRS.index((step, j - step))]
@@ -254,12 +281,11 @@
                     rate[:, at] = fresh
     voxels = 3 * mine.shape[1]
     rows = 2 * TR * STEPS
+    fetch.wait()
     parts[rows:] = jnp.ones_like(parts[rows:])
     total = jnp.zeros((rows + 2 * TR, voxels), F32)
     for c in range(0, nblk * BLOCK, CHUNK):
-        name = owner[:, c : c + CHUNK] - offset[0]
-        hit = lax.broadcasted_iota(jnp.int32, (voxels, CHUNK), 0) == name
-        hit = jnp.where(hit, 1.0, 0.0).astype(BF16)
+        hit = hits[:, c : c + CHUNK]
         total = total + lax.dot_general(
             parts[:, c : c + CHUNK], hit, (((1,), (1,)), ((), ())), preferred_element_type=F32
         )
@@ -273,10 +299,10 @@
 
 
 def window(
-    place, index, flags, offset, begin, local, coupling, below, above, tiles,
-    drive, slope, strength, owner, voxels,
+    place, index, flags, begin, local, coupling, below, above, tiles,
+    drive, slope, strength, hits, voxels,
 ):
-    ext = tiles[0].shape[0]
+    ext = tiles.shape[0]
     nblk = ext - 2 * EDGE
     return pl.pallas_call(
         window_kernel,
@@ -284,18 +310,20 @@
             jax.ShapeDtypeStruct((TR, nblk * BLOCK), F32),
             *[jax.ShapeDtypeStruct(((STEPS + 1) * TR, voxels), F32)] * 3,
         ],
-        in_specs=[SMEM] * 4 + [VMEM] * 14,
+        in_specs=[SMEM] * 3 + [VMEM] * 9 + [HBM],
         out_specs=[VMEM] * 4,
         scratch_shapes=[
             pltpu.VMEM((ext + 2, TR, BLOCK), F32),
             pltpu.VMEM((ext, TR, BLOCK), F32),
             pltpu.VMEM((2 * TR * (STEPS + 1), nblk * BLOCK), BF16),
+            pltpu.VMEM(hits.shape, BF16),
+            pltpu.SemaphoreType.DMA,
         ],
         compiler_params=PARAMS,
         name="window",
     )(
-        place, index, flags, offset, begin, local, coupling, below, above, *tiles,
-        drive, slope, strength, owner,
+        place, index, flags, begin, local, coupling, below, above, tiles,
+        drive, slope, strength, pltpu.with_memory_space_constraint(hits, pltpu.HBM),
     )
 
 
@@ -335,7 +363,7 @@
     send = pack(
         tract_target[:, 0], tract_source, tract_delay, tract_block, tract_weight, history, patches
     )
-    send, before, after = lax.optimization_barrier((send, before, after))
+    send, _, _ = lax.optimization_barrier((send, before, after))
     rows = (2 * STEPS + 1) * TR
     send = send.reshape(patches, rows, BLOCK)
     got = lax.all_to_all(send, "patch", split_axis=0, concat_axis=0, tiled=True)
@@ -346,7 +374,7 @@
     right = lax.ppermute(own, "trial", counter)
     far0 = lax.ppermute(left[:half], "trial", clock)
     far1 = lax.ppermute(right[half:], "trial", counter)
-    tiles = (own, left, right, far0, far1)
+    pieces = (own, left, right, far0, far1)
 
     near = EDGE + 1
     blocks = activity.reshape(TR, nblk, BLOCK)
@@ -376,7 +404,8 @@
     place = (here + jnp.arange(group, dtype=jnp.int32)) % group
     flags = jnp.stack([patch > 0, patch < patches - 1]).astype(F32)
     offset = ((patch - 1) * voxels_here).reshape(1)
-    local = start_local(place, index, begin, tiles)
+    owner = voxel_owner.reshape(1, verts)
+    local, tiles, hits = start_local(place, index, offset, begin, owner, pieces, 3 * voxels_here)
 
     got, local = lax.optimization_barrier((got, local))
     first, last = tract_sums(got, nblk, True)
@@ -386,7 +415,6 @@
         place,
         index,
         flags,
-        offset,
         begin,
         local,
         coupling,
@@ -396,7 +424,7 @@
         drive_ext,
         slope[:, None],
         strength[:, None],
-        voxel_owner.reshape(1, verts),
+        hits,
         voxels_here,
     )
     below, above = sides(to_left, to_right)

time: 179 us -> 174 us (0.972)
  waiting for transfers between devices: 76.2 us -> 71.6 us
  starting transfers between devices: 61.1 us -> 64.1 us
  local copies, waits for them, and re-layouts: 16.9 us -> 14.1 us
    ppermute x8, waiting for transfers between devices: 59.8 us -> 56.2 us  [sides(): return (lax.ppermute(high, 'patch', up), lax.ppermute(low, 'patch', down))]
    unnamed x46 -> x32, local copies, waits for them, and re-layouts: 7.75 us -> 4.25 us
    ppermute x8, starting transfers between devices: 33.1 us -> 36.2 us  [sides(): return (lax.ppermute(high, 'patch', up), lax.ppermute(low, 'patch', down))]
    pallas_call x2, Pallas kernels: 6.24 us -> 8.85 us  [the longest x1 4.91 us: start_local(): pl.pallas_call(start_kernel, out_shape=[jax.ShapeDtypeStruct((ext, TR, BL...]
  transfers between devices with their start and end apart: 13 -> 13, of which waited for: 4 -> 3; matrix products, arithmetic and copies ran while one was open for 8% -> 8% of each run, Pallas kernels for 5% -> 6%
where the time goes in v4:
time: 174 us; the launch traced here: 173 us
  waiting for transfers between devices  71.6 us (41%)
  starting transfers between devices  64.1 us (37%)
  Pallas kernels  16.7 us (10%)
  local copies, waits for them, and re-layouts  14.1 us (8%)
  other arithmetic  6.01 us (3%)
    ppermute x8, waiting for transfers between devices, sides(): return (lax.ppermute(high, 'patch', up), lax.ppermute(low, 'patch', down))  56.2 us
    ppermute x8, starting transfers between devices, sides(): return (lax.ppermute(high, 'patch', up), lax.ppermute(low, 'patch', down))  36.2 us
    ppermute x1, waiting for transfers between devices, shards(): left = lax.ppermute(own, 'trial', clock)  15.3 us
    all_to_all x1, starting transfers between devices, shards(): got = lax.all_to_all(send, 'patch', split_axis=0, concat_axis=0, tiled=True)  13.6 us
    pallas_call x1, Pallas kernels, window(): pl.pallas_call(window_kernel, out_shape=[jax.ShapeDtypeStruct((TR, nblk *...  5.68 us
    pallas_call x1, Pallas kernels, start_local(): pl.pallas_call(start_kernel, out_shape=[jax.ShapeDtypeStruct((ext, TR, BL...  4.91 us
    ppermute x1, starting transfers between devices, shards(): far1 = lax.ppermute(right[half:], 'trial', counter)  4.85 us
    unnamed x32, local copies, waits for them, and re-layouts  4.25 us
  transfers between devices with their start and end apart: 13, of which 3 were waited for; matrix products, arithmetic and copies ran while one was open for 8% of the time, Pallas kernels for 6%

profile of v4, /device:TPU:24, one launch (start us, length us, event | category | flops | bytes accessed | tf_op | source)
XLA Modules:
  0.0 173.5 jit_solution(9934322029668806388)
XLA Ops:
  1.6 1.9 %collective-permute-start.2 = (bf16[3,128,128]{2,1,0:T(8,128)(2,1)S(1)}, bf16[3,128,128]{2,1,0:T(8,128)(2,1)S(1)}, u32[]{:S(2)}, u32[]{:S(2)}) collective-permute-start(bf16[3,128,128]{2,1,0:T(8,128)(2,1)S(1)} %get-tuple-element.30), channel_id=1, source_target_pairs={{0,4},{4,8},{8,12},{12,16},{16,20},{20,24},{24,28},{28,32},{32,36}... | collective-permute-start | bytes 294920 | tf_op jit(solution)/shard_map/ppermute | solution.py:359
  3.5 11.0 %collective-permute-start.3 = (bf16[3,128,128]{2,1,0:T(8,128)(2,1)S(1)}, bf16[3,128,128]{2,1,0:T(8,128)(2,1)S(1)}, u32[]{:S(2)}, u32[]{:S(2)}) collective-permute-start(bf16[3,128,128]{2,1,0:T(8,128)(2,1)S(1)} %get-tuple-element.29), channel_id=1, source_target_pairs={{4,0},{8,4},{12,8},{16,12},{20,16},{24,20},{28,24},{32,28},{36,32}... | collective-permute-start | bytes 294920 | tf_op jit(solution)/shard_map/ppermute | solution.py:359
  14.5 3.9 %pack.1 = bf16[128,9,8,128]{3,2,1,0:T(8,128)(2,1)} custom-call(s32[128]{0:T(128)} %bitcast.45, s32[128]{0:T(128)} %source.1, s32[128]{0:T(128)} %delay.1, s32[128]{0:T(128)} %block.1, f32[128]{0:T(128)} %weight.1, bf16[224,8,128]{2,1,0:T(8,128)(2,1)} %bitcast.37), custom_call_target="tpu_custom_call" | custom-call | tf_op jit(solution)/shard_map/pack/pallas_call | solution.py:93
  19.2 13.6 %all-to-all-start = ((bf16[128,72,128]{2,1,0:T(8,128)(2,1)}), bf16[128,72,128]{2,1,0:T(8,128)(2,1)S(1)}, u32[]{:S(2)}, u32[]{:S(2)}) async-start(bf16[128,72,128]{2,1,0:T(8,128)(2,1)} %bitcast.34), calls=%async_computation | async-start | bytes 4718592 | tf_op jit(solution)/shard_map/all_to_all | solution.py:369
  34.8 2.1 %pad_maximum_fusion.own = bf16[38,128,128]{2,1,0:T(8,128)(2,1)} fusion(bf16[3,128,128]{2,1,0:T(8,128)(2,1)} %copy-done.8, bf16[32,128,128]{2,1,0:T(8,128)(2,1)S(1)} %bitcast.36, bf16[3,128,128]{2,1,0:T(8,128)(2,1)S(1)} %collective-permute-done.2), kind=kLoop, calls=%fused_computation.1 | loop fusion | flops 1245184 | bytes 2490368 | tf_op jit(solution)/shard_map/concatenate | solution.py:371
  36.9 3.5 %collective-permute-start.4 = (bf16[38,128,128]{2,1,0:T(8,128)(2,1)}, bf16[38,128,128]{2,1,0:T(8,128)(2,1)}, u32[]{:S(2)}, u32[]{:S(2)}) collective-permute-start(bf16[38,128,128]{2,1,0:T(8,128)(2,1)} %pad_maximum_fusion.own), channel_id=1, source_target_pairs={{0,1},{1,2},{2,3},{3,0},{4,5},{5,6},{6,7},{7,4},{8,9},{9,10},{10,1... | collective-permute-start | bytes 3735560 | tf_op jit(solution)/shard_map/ppermute | solution.py:373
  40.4 3.7 %collective-permute-start.5 = (bf16[38,128,128]{2,1,0:T(8,128)(2,1)}, bf16[38,128,128]{2,1,0:T(8,128)(2,1)}, u32[]{:S(2)}, u32[]{:S(2)}) collective-permute-start(bf16[38,128,128]{2,1,0:T(8,128)(2,1)} %pad_maximum_fusion.own), channel_id=1, source_target_pairs={{1,0},{2,1},{3,2},{0,3},{5,4},{6,5},{7,6},{4,7},{9,8},{10,9},{11,1... | collective-permute-start | bytes 3735560 | tf_op jit(solution)/shard_map/ppermute | solution.py:374
  44.9 1.9 %collective-permute-start = (f32[10,8,128]{2,1,0:T(8,128)S(1)}, f32[10,8,128]{2,1,0:T(8,128)}, u32[]{:S(2)}, u32[]{:S(2)}) collective-permute-start(f32[10,8,128]{2,1,0:T(8,128)S(1)} %pad_maximum_fusion.3), channel_id=1, source_target_pairs={{0,4},{4,8},{8,12},{12,16},{16,20},{20,24},{24,28},{28,32},{32,36}... | collective-permute-start | bytes 122888 | tf_op jit(solution)/shard_map/ppermute | solution.py:359
  48.2 5.7 %collective-permute-start.1 = (f32[10,8,128]{2,1,0:T(8,128)}, f32[10,8,128]{2,1,0:T(8,128)S(1)}, u32[]{:S(2)}, u32[]{:S(2)}) collective-permute-start(f32[10,8,128]{2,1,0:T(8,128)} %pad_maximum_fusion.4), channel_id=1, source_target_pairs={{4,0},{8,4},{12,8},{16,12},{20,16},{24,20},{28,24},{32,28},{36,32}... | collective-permute-start | bytes 122888 | tf_op jit(solution)/shard_map/ppermute | solution.py:359
  54.5 15.3 %collective-permute-done.4.left = bf16[38,128,128]{2,1,0:T(8,128)(2,1)} collective-permute-done((bf16[38,128,128]{2,1,0:T(8,128)(2,1)}, bf16[38,128,128]{2,1,0:T(8,128)(2,1)}, u32[]{:S(2)}, u32[]{:S(2)}) %collective-permute-start.4) | collective-permute-done | bytes 1245216 | tf_op jit(solution)/shard_map/ppermute | solution.py:373
  69.8 2.0 %slice.125 = bf16[19,128,128]{2,1,0:T(8,128)(2,1)} slice(bf16[38,128,128]{2,1,0:T(8,128)(2,1)} %collective-permute-done.4.left), slice={[0:19], [0:128], [0:128]} | slice | bytes 1245184 | tf_op jit(solution)/shard_map/slice | solution.py:375
  71.8 2.2 %collective-permute-start.6 = (bf16[19,128,128]{2,1,0:T(8,128)(2,1)}, bf16[19,128,128]{2,1,0:T(8,128)(2,1)}, u32[]{:S(2)}, u32[]{:S(2)}) collective-permute-start(bf16[19,128,128]{2,1,0:T(8,128)(2,1)} %slice.125), channel_id=1, source_target_pairs={{0,1},{1,2},{2,3},{3,0},{4,5},{5,6},{6,7},{7,4},{8,9},{9,10},{10,1... | collective-permute-start | bytes 1867784 | tf_op jit(solution)/shard_map/ppermute | solution.py:375
  74.0 2.0 %slice.126 = bf16[19,128,128]{2,1,0:T(8,128)(2,1)} slice(bf16[38,128,128]{2,1,0:T(8,128)(2,1)} %collective-permute-done.5.right), slice={[19:38], [0:128], [0:128]} | slice | bytes 1245184 | tf_op jit(solution)/shard_map/slice | solution.py:376
  76.0 4.9 %collective-permute-start.7 = (bf16[19,128,128]{2,1,0:T(8,128)(2,1)}, bf16[19,128,128]{2,1,0:T(8,128)(2,1)}, u32[]{:S(2)}, u32[]{:S(2)}) collective-permute-start(bf16[19,128,128]{2,1,0:T(8,128)(2,1)} %slice.126), channel_id=1, source_target_pairs={{1,0},{2,1},{3,2},{0,3},{5,4},{6,5},{7,6},{4,7},{9,8},{10,9},{11,1... | collective-permute-start | bytes 1867784 | tf_op jit(solution)/shard_map/ppermute | solution.py:376
  80.8 54.8 %collective-permute-done = f32[10,8,128]{2,1,0:T(8,128)} collective-permute-done((f32[10,8,128]{2,1,0:T(8,128)S(1)}, f32[10,8,128]{2,1,0:T(8,128)}, u32[]{:S(2)}, u32[]{:S(2)}) %collective-permute-start) | collective-permute-done | bytes 40992 | tf_op jit(solution)/shard_map/ppermute | solution.py:359
  139.2 4.9 %start.1 = (f32[38,8,128]{2,1,0:T(8,128)S(1)}, bf16[38,512,128]{2,1,0:T(8,128)(2,1)S(1)}, bf16[384,4096]{1,0:T(8,128)(2,1)}) custom-call(s32[4]{0:T(128)S(1)} %and_select_fusion.2.place, s32[152]{0:T(256)S(1)} %min.12.index, s32[1]{0:T(128)} %bitcast.18.offset, f32[40,8,128]{2,1,0:T(8,128)S(1)} %pad_maximum_fusion.1.frame.begin, s32[1,4096]{1,0:T(1,128)S(1)} %bitcast.33, ...), custom_call_target="tpu_custom_call" | custom-call | tf_op jit(solution)/shard_map/start/pallas_call | solution.py:221
  144.1 2.2 %copy-done = bf16[38,512,128]{2,1,0:T(8,128)(2,1)} copy-done((bf16[38,512,128]{2,1,0:T(8,128)(2,1)}, bf16[38,512,128]{2,1,0:T(8,128)(2,1)S(1)}, u32[]{:S(2)}) %copy-start) | copy-done | bytes 4980760
  148.4 2.2 %collective-permute-start.8 = (f32[6,8,128]{2,1,0:T(8,128)S(1)}, f32[6,8,128]{2,1,0:T(8,128)S(1)}, u32[]{:S(2)}, u32[]{:S(2)}) collective-permute-start(f32[6,8,128]{2,1,0:T(8,128)S(1)} %get-tuple-element.19), channel_id=1, source_target_pairs={{0,4},{4,8},{8,12},{12,16},{16,20},{20,24},{24,28},{28,32},{32,36}... | collective-permute-start | bytes 73736 | tf_op jit(solution)/shard_map/ppermute | solution.py:359
  150.6 5.8 %collective-permute-start.9 = (f32[6,8,128]{2,1,0:T(8,128)S(1)}, f32[6,8,128]{2,1,0:T(8,128)S(1)}, u32[]{:S(2)}, u32[]{:S(2)}) collective-permute-start(f32[6,8,128]{2,1,0:T(8,128)S(1)} %get-tuple-element.20), channel_id=1, source_target_pairs={{4,0},{8,4},{12,8},{16,12},{20,16},{24,20},{28,24},{32,28},{36,32}... | collective-permute-start | bytes 73736 | tf_op jit(solution)/shard_map/ppermute | solution.py:359
  156.4 1.5 tracts.1.coupling
  158.0 5.7 %window.1 = (f32[8,4096]{1,0:T(8,128)}, f32[40,128]{1,0:T(8,128)S(1)}, f32[40,128]{1,0:T(8,128)S(1)}, f32[40,128]{1,0:T(8,128)S(1)}) custom-call(s32[4]{0:T(128)S(1)} %and_select_fusion.2.place, s32[152]{0:T(256)S(1)} %min.12.index, f32[2]{0:T(128)S(1)} %add_convert_fusion.flags, f32[40,8,128]{2,1,0:T(8,128)S(1)} %copy-done.3, f32[38,8,128]{2,1,0:T(8,128)S(1)} %copy-done.5, ...), custom_call_target="tpu_custom_call" | custom-call | tf_op jit(solution)/shard_map/window/pallas_call | solution.py:307
  163.7 1.9 %collective-permute-start.10 = (f32[40,128]{1,0:T(8,128)S(1)}, f32[40,128]{1,0:T(8,128)S(1)}, u32[]{:S(2)}, u32[]{:S(2)}) collective-permute-start(f32[40,128]{1,0:T(8,128)S(1)} %get-tuple-element.25), channel_id=1, source_target_pairs={{0,4},{4,8},{8,12},{12,16},{16,20},{20,24},{24,28},{28,32},{32,36}... | collective-permute-start | bytes 61448 | tf_op jit(solution)/shard_map/ppermute | solution.py:359
  165.6 5.8 %collective-permute-start.11 = (f32[40,128]{1,0:T(8,128)S(1)}, f32[40,128]{1,0:T(8,128)S(1)}, u32[]{:S(2)}, u32[]{:S(2)}) collective-permute-start(f32[40,128]{1,0:T(8,128)S(1)} %get-tuple-element.26), channel_id=1, source_target_pairs={{4,0},{8,4},{12,8},{16,12},{20,16},{24,20},{28,24},{32,28},{36,32}... | collective-permute-start | bytes 61448 | tf_op jit(solution)/shard_map/ppermute | solution.py:359
  171.4 1.4 collective-permute-done.11
  (78 shorter events, 12.5 us)
Async XLA Ops:
  1.6 16.9 %collective-permute-start.2 = (bf16[3,128,128]{2,1,0:T(8,128)(2,1)S(1)}, bf16[3,128,128]{2,1,0:T(8,128)(2,1)S(1)}, u32[]{:S(2)}, u32[]{:S(2)}) collective-permute-start(bf16[3,128,128]{2,1,0:T(8,128)(2,1)S(1)} %get-tuple-element.30), channel_id=1, source_target_pairs={{0,4},{4,8},{8,12},{12,16},{16,20},{20,24},{24,28},{28,32},{32,36}... | collective-permute-start | bytes 294920 | tf_op jit(solution)/shard_map/ppermute | solution.py:359
  3.5 15.0 %collective-permute-start.3 = (bf16[3,128,128]{2,1,0:T(8,128)(2,1)S(1)}, bf16[3,128,128]{2,1,0:T(8,128)(2,1)S(1)}, u32[]{:S(2)}, u32[]{:S(2)}) collective-permute-start(bf16[3,128,128]{2,1,0:T(8,128)(2,1)S(1)} %get-tuple-element.29), channel_id=1, source_target_pairs={{4,0},{8,4},{12,8},{16,12},{20,16},{24,20},{28,24},{32,28},{36,32}... | collective-permute-start | bytes 294920 | tf_op jit(solution)/shard_map/ppermute | solution.py:359
  18.5 14.3 %copy-start.13 = (s32[32,4]{0,1:T(4,128)S(1)}, s32[32,4]{0,1:T(4,128)}, u32[]{:S(2)}) copy-start(s32[32,4]{0,1:T(4,128)} %param.21) | copy-start | bytes 1540
  18.5 14.9 %copy-start.9 = (f32[4096]{0:T(1024)S(1)}, f32[4096]{0:T(1024)}, u32[]{:S(2)}) copy-start(f32[4096]{0:T(1024)} %param.17) | copy-start | bytes 49156
  18.6 16.2 %copy-start.7 = (bf16[32,1,128,128]{3,2,1,0:T(8,128)(2,1)S(1)}, bf16[32,1,128,128]{3,2,1,0:T(8,128)(2,1)}, u32[]{:S(2)}) copy-start(bf16[32,1,128,128]{3,2,1,0:T(8,128)(2,1)} %param.20) | copy-start | bytes 3145732
  19.2 128.5 %all-to-all-start = ((bf16[128,72,128]{2,1,0:T(8,128)(2,1)}), bf16[128,72,128]{2,1,0:T(8,128)(2,1)S(1)}, u32[]{:S(2)}, u32[]{:S(2)}) async-start(bf16[128,72,128]{2,1,0:T(8,128)(2,1)} %bitcast.34), calls=%async_computation | async-start | bytes 4718592 | tf_op jit(solution)/shard_map/all_to_all | solution.py:369
  36.9 17.5 %copy-start.14 = (f32[8]{0:T(128)S(1)}, f32[8]{0:T(128)}, u32[]{:S(2)}) copy-start(f32[8]{0:T(128)} %param.18) | copy-start | bytes 100
  36.9 17.6 %copy-start.15 = (f32[8]{0:T(128)S(1)}, f32[8]{0:T(128)}, u32[]{:S(2)}) copy-start(f32[8]{0:T(128)} %param.19) | copy-start | bytes 100
  36.9 33.0 %collective-permute-start.4 = (bf16[38,128,128]{2,1,0:T(8,128)(2,1)}, bf16[38,128,128]{2,1,0:T(8,128)(2,1)}, u32[]{:S(2)}, u32[]{:S(2)}) collective-permute-start(bf16[38,128,128]{2,1,0:T(8,128)(2,1)} %pad_maximum_fusion.own), channel_id=1, source_target_pairs={{0,1},{1,2},{2,3},{3,0},{4,5},{5,6},{6,7},{7,4},{8,9},{9,10},{10,1... | collective-permute-start | bytes 3735560 | tf_op jit(solution)/shard_map/ppermute | solution.py:373
  40.4 33.6 %collective-permute-start.5 = (bf16[38,128,128]{2,1,0:T(8,128)(2,1)}, bf16[38,128,128]{2,1,0:T(8,128)(2,1)}, u32[]{:S(2)}, u32[]{:S(2)}) collective-permute-start(bf16[38,128,128]{2,1,0:T(8,128)(2,1)} %pad_maximum_fusion.own), channel_id=1, source_target_pairs={{1,0},{2,1},{3,2},{0,3},{5,4},{6,5},{7,6},{4,7},{9,8},{10,9},{11,1... | collective-permute-start | bytes 3735560 | tf_op jit(solution)/shard_map/ppermute | solution.py:374
  44.9 90.7 %collective-permute-start = (f32[10,8,128]{2,1,0:T(8,128)S(1)}, f32[10,8,128]{2,1,0:T(8,128)}, u32[]{:S(2)}, u32[]{:S(2)}) collective-permute-start(f32[10,8,128]{2,1,0:T(8,128)S(1)} %pad_maximum_fusion.3), channel_id=1, source_target_pairs={{0,4},{4,8},{8,12},{12,16},{16,20},{20,24},{24,28},{28,32},{32,36}... | collective-permute-start | bytes 122888 | tf_op jit(solution)/shard_map/ppermute | solution.py:359
  48.2 88.2 %collective-permute-start.1 = (f32[10,8,128]{2,1,0:T(8,128)}, f32[10,8,128]{2,1,0:T(8,128)S(1)}, u32[]{:S(2)}, u32[]{:S(2)}) collective-permute-start(f32[10,8,128]{2,1,0:T(8,128)} %pad_maximum_fusion.4), channel_id=1, source_target_pairs={{4,0},{8,4},{12,8},{16,12},{20,16},{24,20},{28,24},{32,28},{36,32}... | collective-permute-start | bytes 122888 | tf_op jit(solution)/shard_map/ppermute | solution.py:359
  54.5 82.0 %copy-start.10 = (s32[32,4]{0,1:T(4,128)S(1)}, s32[32,4]{0,1:T(4,128)}, u32[]{:S(2)}) copy-start(s32[32,4]{0,1:T(4,128)} %get-tuple-element.37) | copy-start | bytes 1540
  54.5 84.7 %copy-start.6 = (s32[4096]{0:T(1024)S(1)}, s32[4096]{0:T(1024)}, u32[]{:S(2)}) copy-start(s32[4096]{0:T(1024)} %param.27) | copy-start | bytes 49156
  71.8 67.3 %collective-permute-start.6 = (bf16[19,128,128]{2,1,0:T(8,128)(2,1)}, bf16[19,128,128]{2,1,0:T(8,128)(2,1)}, u32[]{:S(2)}, u32[]{:S(2)}) collective-permute-start(bf16[19,128,128]{2,1,0:T(8,128)(2,1)} %slice.125), channel_id=1, source_target_pairs={{0,1},{1,2},{2,3},{3,0},{4,5},{5,6},{6,7},{7,4},{8,9},{9,10},{10,1... | collective-permute-start | bytes 1867784 | tf_op jit(solution)/shard_map/ppermute | solution.py:375
  76.0 63.2 %collective-permute-start.7 = (bf16[19,128,128]{2,1,0:T(8,128)(2,1)}, bf16[19,128,128]{2,1,0:T(8,128)(2,1)}, u32[]{:S(2)}, u32[]{:S(2)}) collective-permute-start(bf16[19,128,128]{2,1,0:T(8,128)(2,1)} %slice.126), channel_id=1, source_target_pairs={{1,0},{2,1},{3,2},{0,3},{5,4},{6,5},{7,6},{4,7},{9,8},{10,9},{11,1... | collective-permute-start | bytes 1867784 | tf_op jit(solution)/shard_map/ppermute | solution.py:376
  144.1 2.3 %copy-start = (bf16[38,512,128]{2,1,0:T(8,128)(2,1)}, bf16[38,512,128]{2,1,0:T(8,128)(2,1)S(1)}, u32[]{:S(2)}) copy-start(bf16[38,512,128]{2,1,0:T(8,128)(2,1)S(1)} %get-tuple-element.21.tiles) | copy-start | bytes 14942212
  147.7 10.3 %copy-start.1 = (bf16[38,512,128]{2,1,0:T(8,128)(2,1)S(1)}, bf16[38,512,128]{2,1,0:T(8,128)(2,1)}, u32[]{:S(2)}) copy-start(bf16[38,512,128]{2,1,0:T(8,128)(2,1)} %copy-done) | copy-start | bytes 14942212
  148.4 9.5 %collective-permute-start.8 = (f32[6,8,128]{2,1,0:T(8,128)S(1)}, f32[6,8,128]{2,1,0:T(8,128)S(1)}, u32[]{:S(2)}, u32[]{:S(2)}) collective-permute-start(f32[6,8,128]{2,1,0:T(8,128)S(1)} %get-tuple-element.19), channel_id=1, source_target_pairs={{0,4},{4,8},{8,12},{12,16},{16,20},{20,24},{24,28},{28,32},{32,36}... | collective-permute-start | bytes 73736 | tf_op jit(solution)/shard_map/ppermute | solution.py:359
  150.6 7.4 %collective-permute-start.9 = (f32[6,8,128]{2,1,0:T(8,128)S(1)}, f32[6,8,128]{2,1,0:T(8,128)S(1)}, u32[]{:S(2)}, u32[]{:S(2)}) collective-permute-start(f32[6,8,128]{2,1,0:T(8,128)S(1)} %get-tuple-element.20), channel_id=1, source_target_pairs={{4,0},{8,4},{12,8},{16,12},{20,16},{24,20},{28,24},{32,28},{36,32}... | collective-permute-start | bytes 73736 | tf_op jit(solution)/shard_map/ppermute | solution.py:359
  158.0 14.9 %copy-start.11 = (f32[8,128]{1,0:T(8,128)S(1)}, f32[8,128]{1,0:T(8,128)}, u32[]{:S(2)}) copy-start(f32[8,128]{1,0:T(8,128)} %param.29) | copy-start | bytes 12292
  158.0 14.9 %copy-start.12 = (f32[8,128]{1,0:T(8,128)S(1)}, f32[8,128]{1,0:T(8,128)}, u32[]{:S(2)}) copy-start(f32[8,128]{1,0:T(8,128)} %param.28) | copy-start | bytes 12292
  163.7 7.7 %collective-permute-start.10 = (f32[40,128]{1,0:T(8,128)S(1)}, f32[40,128]{1,0:T(8,128)S(1)}, u32[]{:S(2)}, u32[]{:S(2)}) collective-permute-start(f32[40,128]{1,0:T(8,128)S(1)} %get-tuple-element.25), channel_id=1, source_target_pairs={{0,4},{4,8},{8,12},{12,16},{16,20},{20,24},{24,28},{28,32},{32,36}... | collective-permute-start | bytes 61448 | tf_op jit(solution)/shard_map/ppermute | solution.py:359
  165.6 7.2 %collective-permute-start.11 = (f32[40,128]{1,0:T(8,128)S(1)}, f32[40,128]{1,0:T(8,128)S(1)}, u32[]{:S(2)}, u32[]{:S(2)}) collective-permute-start(f32[40,128]{1,0:T(8,128)S(1)} %get-tuple-element.26), channel_id=1, source_target_pairs={{4,0},{8,4},{12,8},{16,12},{20,16},{24,20},{28,24},{32,28},{36,32}... | collective-permute-start | bytes 61448 | tf_op jit(solution)/shard_map/ppermute | solution.py:359
  (5 other events, 5.2 us)

commit v5 on v4

--- a/solution.py
+++ b/solution.py
@@ -130,9 +130,13 @@
     return (spot.astype(jnp.int32) - 1) * TR + trial
 
 
-def tract_kernel(nblk, got, spread, *rest):
-    outs, (names, picks) = rest[:-2], rest[-2:]
-    edges = len(outs) == 2
+def tract_kernel(nblk, edges, got, spread, *rest):
+    if edges:
+        *outs, names, picks = rest
+    else:
+        tiles, *outs, kept, names, picks, sem = rest
+        load = pltpu.make_async_copy(tiles, kept, sem)
+        load.start()
     steps = EDGE if edges else STEPS
     patches = got.shape[0]
     width = 2 * TR
@@ -153,42 +157,56 @@
             n = PAIRS.index((s, i))
             outs[0][n] = total[i * TR : (i + 1) * TR]
             outs[1][n] = total[(EDGE + s + i) * TR : (EDGE + s + i + 1) * TR]
-
-
-def tract_sums(got, nblk, edges):
+    if not edges:
+        load.wait()
+
+
+def tract_sums(got, nblk, tiles=None):
+    edges = tiles is None
     patches = got.shape[0]
     width = 2 * TR
     column = jnp.arange(patches * width, dtype=jnp.int32)[None, :]
     line = jnp.arange(2 * patches, dtype=jnp.int32)[:, None]
     spread = (column // TR == (line % patches) * 2 + line // patches).astype(BF16)
+    operands, in_specs = [got, spread], [VMEM, VMEM]
+    scratch = [
+        pltpu.VMEM((patches * TR, BLOCK), F32),
+        pltpu.VMEM(((2 * EDGE if edges else nblk) * TR, patches * width), BF16),
+    ]
+    if edges:
+        outs = [jax.ShapeDtypeStruct((len(PAIRS), TR, BLOCK), F32)] * 2
+    else:
+        outs = [
+            jax.ShapeDtypeStruct((STEPS, nblk, TR, BLOCK), F32),
+            pltpu.VMEM(tiles.shape, BF16),
+        ]
+        operands.append(pltpu.with_memory_space_constraint(tiles, pltpu.HBM))
+        in_specs.append(HBM)
+        scratch.append(pltpu.SemaphoreType.DMA)
 
     def kernel(*refs):
-        tract_kernel(nblk, *refs)
-
-    shapes = [(len(PAIRS), TR, BLOCK)] * 2 if edges else [(STEPS, nblk, TR, BLOCK)]
+        tract_kernel(nblk, edges, *refs)
+
     return pl.pallas_call(
         kernel,
-        out_shape=[jax.ShapeDtypeStruct(shape, F32) for shape in shapes],
-        in_specs=[VMEM] * 2,
-        out_specs=[VMEM] * len(shapes),
-        scratch_shapes=[
-            pltpu.VMEM((patches * TR, BLOCK), F32),
-            pltpu.VMEM(((2 * EDGE if edges else nblk) * TR, patches * width), BF16),
-        ],
+        out_shape=outs,
+        in_specs=in_specs,
+        out_specs=[VMEM] * 2,
+        scratch_shapes=scratch,
         compiler_params=PARAMS,
         name="edges" if edges else "tracts",
-    )(got, spread)
-
-
-def local_block(j, place, index, frame, tiles):
-    rows = [frame[index[4 * j + place[shift]]] for shift in SHIFTS]
+    )(*operands)
+
+
+def local_block(at, place, index, frame, tiles):
+    rows = [frame[at(place[shift])] for shift in SHIFTS]
     rows = jnp.concatenate(rows, axis=1).astype(BF16)
-    return jnp.dot(rows, tiles[j], preferred_element_type=F32)
+    return jnp.dot(rows, tiles, preferred_element_type=F32)
 
 
 def start_kernel(
-    place, index, offset, frame, owner, own, left, right, far0, far1,
-    out, tiles, kept, hits, sems,
+    place, index, offset, activity, owner, own, left, right, far0, far1,
+    out, joined, kept, tiles, hits, sems, frame,
 ):
     half = far0.shape[0]
     ext = own.shape[0]
@@ -208,77 +226,119 @@
         hits[:, c : c + CHUNK] = jnp.where(hit, 1.0, 0.0).astype(BF16)
     keep = pltpu.make_async_copy(hits, kept, sems.at[5])
     keep.start()
+    for b in range(ext - 2 * EDGE):
+        frame[b] = activity[:, b * BLOCK : (b + 1) * BLOCK]
     for move in moves:
         move.wait()
-    for j in range(ext):
-        out[j] = local_block(j, place, index, frame, tiles)
+    store = pltpu.make_async_copy(tiles, joined, sems.at[0])
+    store.start()
+    for n in range(out.shape[0]):
+        out[n] = local_block(
+            lambda k: index[4 * (n + 1) + k] - 1, place, index, frame, tiles[n + 1 + EDGE]
+        )
     keep.wait()
-
-
-def start_local(place, index, offset, frame, owner, pieces, voxels):
+    store.wait()
+
+
+def start_local(place, index, offset, activity, owner, pieces, voxels):
     ext = pieces[0].shape[0]
+    nblk = ext - 2 * EDGE
     pieces = [pltpu.with_memory_space_constraint(x, pltpu.HBM) for x in pieces]
     return pl.pallas_call(
         start_kernel,
         out_shape=[
-            jax.ShapeDtypeStruct((ext, TR, BLOCK), F32),
-            pltpu.VMEM((ext, 4 * BLOCK, BLOCK), BF16),
+            jax.ShapeDtypeStruct((nblk - 2, TR, BLOCK), F32),
+            pltpu.HBM((ext, 4 * BLOCK, BLOCK), BF16),
             pltpu.HBM((voxels, owner.shape[1]), BF16),
         ],
         in_specs=[SMEM] * 3 + [VMEM] * 2 + [HBM] * 5,
-        out_specs=[VMEM] * 2 + [HBM],
+        out_specs=[VMEM, HBM, HBM],
         scratch_shapes=[
+            pltpu.VMEM((ext, 4 * BLOCK, BLOCK), BF16),
             pltpu.VMEM((voxels, owner.shape[1]), BF16),
             pltpu.SemaphoreType.DMA((6,)),
+            pltpu.VMEM((nblk, TR, BLOCK), F32),
         ],
         compiler_params=PARAMS,
         name="start",
-    )(place, index, offset, frame, owner, *pieces)
+    )(place, index, offset, activity, owner, *pieces)
 
 
 CHUNK = 512
 
 
 def window_kernel(
-    place, index, flags, begin, local, coupling, below, above,
+    place, index, flags, activity, before, after, local, coupling, below, above,
     tiles, drive, slope, strength, kept,
-    rate, mine, to_left, to_right, frame, sums, parts, hits, sem,
+    rate, mine, to_left, to_right, frame, sums, parts, hits, names, outer, sems,
 ):
     ext = tiles.shape[0]
     nblk = ext - 2 * EDGE
-    fetch = pltpu.make_async_copy(kept, hits, sem)
+    near = EDGE + 1
+    fetch = pltpu.make_async_copy(kept, hits, sems.at[0])
     fetch.start()
-    frame[...] = begin[...]
+    names[...] = jnp.zeros_like(names)
+    for i in range(EDGE):
+        name = before[near + EDGE + i].astype(jnp.int32) - (nblk - near + 1)
+        names[i : i + 1] = jnp.clip(name, 0, ext + 1)[:1]
+        name = after[near + EDGE + i].astype(jnp.int32) + (nblk + EDGE)
+        names[EDGE + i : EDGE + i + 1] = jnp.clip(name, 0, ext + 1)[:1]
+    read = pltpu.make_async_copy(names, outer, sems.at[1])
+    read.start()
+    frame[:near] = before[:near]
+    frame[near + nblk :] = after[:near]
+    for b in range(nblk):
+        frame[near + b] = activity[:, b * BLOCK : (b + 1) * BLOCK]
     steep = jnp.broadcast_to(slope[...], (TR, BLOCK))
     strong = jnp.broadcast_to(strength[...], (TR, BLOCK))
-    for step in range(STEPS):
-        blocks = range(step, ext - step)
-        if step > 0:
-            for j in blocks:
-                sums[j] = local_block(j, place, index, frame, tiles)
-        for j in blocks:
-            if j < EDGE:
-                tracts = below[PAIRS.index((step, j - step))]
-            elif j >= nblk + EDGE:
-                tracts = above[PAIRS.index((step, j - nblk - EDGE))]
-            else:
-                tracts = coupling[step, j - EDGE]
-            near = local[j] if step == 0 else sums[j]
-            pre = steep * (near + strong * tracts + drive[j])
-            old = frame[j + 1]
-            fresh = old + 0.5 * (jax.nn.sigmoid(pre) - old)
-            if j < EDGE:
-                fresh = fresh * flags[0]
-            elif j >= nblk + EDGE:
-                fresh = fresh * flags[1]
-            frame[j + 1] = fresh
-            if EDGE <= j < nblk + EDGE:
-                at = slice((j - EDGE) * BLOCK, (j - EDGE + 1) * BLOCK)
-                top = fresh.astype(BF16).astype(F32)
-                pair = jnp.concatenate([top, fresh - top], axis=0)
-                parts[2 * TR * step : 2 * TR * (step + 1), at] = pair.astype(BF16)
-                if step == STEPS - 1:
-                    rate[:, at] = fresh
+
+    def gather(j):
+        if j < EDGE:
+            at = lambda k: outer[j, k]
+        elif j >= nblk + EDGE:
+            at = lambda k: outer[j - nblk, k]
+        else:
+            at = lambda k: index[4 * (j - EDGE) + k] + EDGE
+        sums[j] = local_block(at, place, index, frame, tiles[j])
+
+    def advance(step, j):
+        b = j - EDGE
+        if b < 0:
+            tracts, input_ = below[PAIRS.index((step, j - step))], before[near + j]
+        elif b >= nblk:
+            tracts, input_ = above[PAIRS.index((step, b - nblk))], after[near + b - nblk]
+        else:
+            tracts, input_ = coupling[step, b], drive[:, b * BLOCK : (b + 1) * BLOCK]
+        summed = local[b - 1] if step == 0 and 0 < b < nblk - 1 else sums[j]
+        pre = steep * (summed + strong * tracts + input_)
+        old = frame[j + 1]
+        fresh = old + 0.5 * (jax.nn.sigmoid(pre) - old)
+        if b < 0:
+            fresh = fresh * flags[0]
+        elif b >= nblk:
+            fresh = fresh * flags[1]
+        frame[j + 1] = fresh
+        if 0 <= b < nblk:
+            at = slice(b * BLOCK, (b + 1) * BLOCK)
+            top = fresh.astype(BF16).astype(F32)
+            pair = jnp.concatenate([top, fresh - top], axis=0)
+            parts[2 * TR * step : 2 * TR * (step + 1), at] = pair.astype(BF16)
+            if step == STEPS - 1:
+                rate[:, at] = fresh
+
+    inner = range(EDGE + 2, nblk + EDGE - 2)
+    for j in inner:
+        advance(0, j)
+    read.wait()
+    for j in (*range(near), *range(ext - near, ext)):
+        gather(j)
+    for j in (*range(EDGE + 2), *range(nblk + EDGE - 2, ext)):
+        advance(0, j)
+    for step in range(1, STEPS):
+        for j in range(step, ext - step):
+            gather(j)
+        for j in range(step, ext - step):
+            advance(step, j)
     voxels = 3 * mine.shape[1]
     rows = 2 * TR * STEPS
     fetch.wait()
@@ -299,7 +359,7 @@
 
 
 def window(
-    place, index, flags, begin, local, coupling, below, above, tiles,
+    place, index, flags, activity, before, after, local, coupling, below, above, tiles,
     drive, slope, strength, hits, voxels,
 ):
     ext = tiles.shape[0]
@@ -310,19 +370,21 @@
             jax.ShapeDtypeStruct((TR, nblk * BLOCK), F32),
             *[jax.ShapeDtypeStruct(((STEPS + 1) * TR, voxels), F32)] * 3,
         ],
-        in_specs=[SMEM] * 3 + [VMEM] * 9 + [HBM],
+        in_specs=[SMEM] * 3 + [VMEM] * 11 + [HBM],
         out_specs=[VMEM] * 4,
         scratch_shapes=[
             pltpu.VMEM((ext + 2, TR, BLOCK), F32),
             pltpu.VMEM((ext, TR, BLOCK), F32),
             pltpu.VMEM((2 * TR * (STEPS + 1), nblk * BLOCK), BF16),
             pltpu.VMEM(hits.shape, BF16),
-            pltpu.SemaphoreType.DMA,
+            pltpu.VMEM((TR, BLOCK), jnp.int32),
+            pltpu.SMEM((TR, BLOCK), jnp.int32),
+            pltpu.SemaphoreType.DMA((2,)),
         ],
         compiler_params=PARAMS,
         name="window",
     )(
-        place, index, flags, begin, local, coupling, below, above, tiles,
+        place, index, flags, activity, before, after, local, coupling, below, above, tiles,
         drive, slope, strength, pltpu.with_memory_space_constraint(hits, pltpu.HBM),
     )
 
@@ -390,38 +452,33 @@
         edge(slice(0, near), slice(0, EDGE)),
         edge(slice(nblk - near, nblk), slice(nblk - EDGE, nblk)),
     )
-    begin = jnp.concatenate([before[:near], blocks.transpose(1, 0, 2), after[:near]], axis=0)
-    drive_ext = jnp.concatenate([before[near : near + EDGE], extra, after[near : near + EDGE]])
-    index = jnp.concatenate(
-        [
-            before[near + EDGE :, 0, :4].astype(jnp.int32) - (nblk - near + 1),
-            kernel_index + EDGE,
-            after[near + EDGE :, 0, :4].astype(jnp.int32) + (nblk + EDGE),
-        ]
-    )
-    index = jnp.clip(index, 0, nblk + 2 * near - 1).reshape(-1)
+    index = kernel_index.reshape(-1)
     here = lax.axis_index("trial").astype(jnp.int32)
     place = (here + jnp.arange(group, dtype=jnp.int32)) % group
     flags = jnp.stack([patch > 0, patch < patches - 1]).astype(F32)
     offset = ((patch - 1) * voxels_here).reshape(1)
     owner = voxel_owner.reshape(1, verts)
-    local, tiles, hits = start_local(place, index, offset, begin, owner, pieces, 3 * voxels_here)
+    local, tiles, hits = start_local(
+        place, index, offset, activity, owner, pieces, 3 * voxels_here
+    )
 
     got, local = lax.optimization_barrier((got, local))
-    first, last = tract_sums(got, nblk, True)
+    first, last = tract_sums(got, nblk)
     below, above = sides(first, last)
-    [coupling] = tract_sums(got, nblk, False)
+    coupling, tiles = tract_sums(got, nblk, tiles)
     rate, mine, to_left, to_right = window(
         place,
         index,
         flags,
-        begin,
+        activity,
+        before,
+        after,
         local,
         coupling,
         below,
         above,
         tiles,
-        drive_ext,
+        drive.reshape(1, verts),
         slope[:, None],
         strength[:, None],
         hits,

time: 174 us -> 173 us (level)
  waiting for transfers between devices: 71.6 us -> 68.6 us
  Pallas kernels: 16.7 us -> 19.2 us
  local copies, waits for them, and re-layouts: 14.1 us -> 11.8 us
    ppermute x8, waiting for transfers between devices: 56.2 us -> 1.47 us  [sides(): return (lax.ppermute(high, 'patch', up), lax.ppermute(low, 'patch', down))]
    all_to_all x1, waiting for transfers between devices: 0.01 us -> 40.5 us  [shards(): got = lax.all_to_all(send, 'patch', split_axis=0, concat_axis=0, tiled=True)]
    ppermute x1, waiting for transfers between devices: 0.01 us -> 7.44 us  [shards(): far0 = lax.ppermute(left[:half], 'trial', clock)]
    pallas_call x3, Pallas kernels: 7.11 us -> 10.3 us  [the longest x1 6.38 us: start_local(): pl.pallas_call(start_kernel, out_shape=[jax.ShapeDtypeStruct((nblk - 2, T...]
    ppermute x1, waiting for transfers between devices: 0.01 us -> 3.16 us  [shards(): far1 = lax.ppermute(right[half:], 'trial', counter)]
    unnamed x32 -> x39, local copies, waits for them, and re-layouts: 4.25 us -> 3.39 us
  transfers between devices with their start and end apart: 13 -> 13, of which waited for: 3 -> 5; matrix products, arithmetic and copies ran while one was open for 8% -> 8% of each run, Pallas kernels for 6% -> 8%
where the time goes in v5:
time: 173 us; the launch traced here: 171 us
  waiting for transfers between devices  68.6 us (40%)
  starting transfers between devices  63.7 us (37%)
  Pallas kernels  19.2 us (11%)
  local copies, waits for them, and re-layouts  11.8 us (7%)
  other arithmetic  6.68 us (4%)
    all_to_all x1, waiting for transfers between devices, shards(): got = lax.all_to_all(send, 'patch', split_axis=0, concat_axis=0, tiled=True)  40.5 us
    ppermute x8, starting transfers between devices, sides(): return (lax.ppermute(high, 'patch', up), lax.ppermute(low, 'patch', down))  35.9 us
    ppermute x1, waiting for transfers between devices, shards(): left = lax.ppermute(own, 'trial', clock)  16 us
    all_to_all x1, starting transfers between devices, shards(): got = lax.all_to_all(send, 'patch', split_axis=0, concat_axis=0, tiled=True)  13.7 us
    ppermute x1, waiting for transfers between devices, shards(): far0 = lax.ppermute(left[:half], 'trial', clock)  7.44 us
    pallas_call x1, Pallas kernels, start_local(): pl.pallas_call(start_kernel, out_shape=[jax.ShapeDtypeStruct((nblk - 2, T...  6.38 us
    pallas_call x1, Pallas kernels, window(): pl.pallas_call(window_kernel, out_shape=[jax.ShapeDtypeStruct((TR, nblk *...  5.01 us
    ppermute x1, starting transfers between devices, shards(): far1 = lax.ppermute(right[half:], 'trial', counter)  4.85 us
  transfers between devices with their start and end apart: 13, of which 5 were waited for; matrix products, arithmetic and copies ran while one was open for 8% of the time, Pallas kernels for 8%

profile of v5, /device:TPU:24, one launch (start us, length us, event | category | flops | bytes accessed | tf_op | source)
XLA Modules:
  0.0 171.0 jit_solution(6219588424603338908)
XLA Ops:
  1.6 1.9 %collective-permute-start.2 = (bf16[3,128,128]{2,1,0:T(8,128)(2,1)S(1)}, bf16[3,128,128]{2,1,0:T(8,128)(2,1)S(1)}, u32[]{:S(2)}, u32[]{:S(2)}) collective-permute-start(bf16[3,128,128]{2,1,0:T(8,128)(2,1)S(1)} %get-tuple-element.34), channel_id=1, source_target_pairs={{0,4},{4,8},{8,12},{12,16},{16,20},{20,24},{24,28},{28,32},{32,36}... | collective-permute-start | bytes 294920 | tf_op jit(solution)/shard_map/ppermute | solution.py:421
  3.5 11.0 %collective-permute-start.3 = (bf16[3,128,128]{2,1,0:T(8,128)(2,1)S(1)}, bf16[3,128,128]{2,1,0:T(8,128)(2,1)S(1)}, u32[]{:S(2)}, u32[]{:S(2)}) collective-permute-start(bf16[3,128,128]{2,1,0:T(8,128)(2,1)S(1)} %get-tuple-element.33), channel_id=1, source_target_pairs={{4,0},{8,4},{12,8},{16,12},{20,16},{24,20},{28,24},{32,28},{36,32}... | collective-permute-start | bytes 294920 | tf_op jit(solution)/shard_map/ppermute | solution.py:421
  14.5 3.9 %pack.1 = bf16[128,9,8,128]{3,2,1,0:T(8,128)(2,1)} custom-call(s32[128]{0:T(128)} %bitcast.38, s32[128]{0:T(128)} %source.1, s32[128]{0:T(128)} %delay.1, s32[128]{0:T(128)} %block.1, f32[128]{0:T(128)} %weight.1, bf16[224,8,128]{2,1,0:T(8,128)(2,1)} %bitcast.35), custom_call_target="tpu_custom_call" | custom-call | tf_op jit(solution)/shard_map/pack/pallas_call | solution.py:93
  19.1 13.7 %all-to-all-start = ((bf16[128,72,128]{2,1,0:T(8,128)(2,1)}), bf16[128,72,128]{2,1,0:T(8,128)(2,1)S(1)}, u32[]{:S(2)}, u32[]{:S(2)}) async-start(bf16[128,72,128]{2,1,0:T(8,128)(2,1)} %bitcast.32), calls=%async_computation | async-start | bytes 4718592 | tf_op jit(solution)/shard_map/all_to_all | solution.py:431
  32.8 2.2 %pad_maximum_fusion.own = bf16[38,128,128]{2,1,0:T(8,128)(2,1)} fusion(bf16[3,128,128]{2,1,0:T(8,128)(2,1)} %copy-done.14, bf16[32,128,128]{2,1,0:T(8,128)(2,1)S(1)} %bitcast.34, bf16[3,128,128]{2,1,0:T(8,128)(2,1)} %copy-done.13), kind=kLoop, calls=%fused_computation.1 | loop fusion | flops 1245184 | bytes 2490368 | tf_op jit(solution)/shard_map/concatenate | solution.py:433
  35.0 3.4 %collective-permute-start.4 = (bf16[38,128,128]{2,1,0:T(8,128)(2,1)}, bf16[38,128,128]{2,1,0:T(8,128)(2,1)}, u32[]{:S(2)}, u32[]{:S(2)}) collective-permute-start(bf16[38,128,128]{2,1,0:T(8,128)(2,1)} %pad_maximum_fusion.own), channel_id=1, source_target_pairs={{0,1},{1,2},{2,3},{3,0},{4,5},{5,6},{6,7},{7,4},{8,9},{9,10},{10,1... | collective-permute-start | bytes 3735560 | tf_op jit(solution)/shard_map/ppermute | solution.py:435
  38.4 3.7 %collective-permute-start.5 = (bf16[38,128,128]{2,1,0:T(8,128)(2,1)}, bf16[38,128,128]{2,1,0:T(8,128)(2,1)}, u32[]{:S(2)}, u32[]{:S(2)}) collective-permute-start(bf16[38,128,128]{2,1,0:T(8,128)(2,1)} %pad_maximum_fusion.own), channel_id=1, source_target_pairs={{1,0},{2,1},{3,2},{0,3},{5,4},{6,5},{7,6},{4,7},{9,8},{10,9},{11,1... | collective-permute-start | bytes 3735560 | tf_op jit(solution)/shard_map/ppermute | solution.py:436
  42.9 1.9 %collective-permute-start = (f32[10,8,128]{2,1,0:T(8,128)}, f32[10,8,128]{2,1,0:T(8,128)}, u32[]{:S(2)}, u32[]{:S(2)}) collective-permute-start(f32[10,8,128]{2,1,0:T(8,128)} %pad_maximum_fusion.1), channel_id=1, source_target_pairs={{0,4},{4,8},{8,12},{12,16},{16,20},{20,24},{24,28},{28,32},{32,36}... | collective-permute-start | bytes 122888 | tf_op jit(solution)/shard_map/ppermute | solution.py:421
  45.5 5.7 %collective-permute-start.1 = (f32[10,8,128]{2,1,0:T(8,128)}, f32[10,8,128]{2,1,0:T(8,128)}, u32[]{:S(2)}, u32[]{:S(2)}) collective-permute-start(f32[10,8,128]{2,1,0:T(8,128)} %pad_maximum_fusion.2), channel_id=1, source_target_pairs={{4,0},{8,4},{12,8},{16,12},{20,16},{24,20},{28,24},{32,28},{36,32}... | collective-permute-start | bytes 122888 | tf_op jit(solution)/shard_map/ppermute | solution.py:421
  51.9 16.0 %collective-permute-done.4.left = bf16[38,128,128]{2,1,0:T(8,128)(2,1)} collective-permute-done((bf16[38,128,128]{2,1,0:T(8,128)(2,1)}, bf16[38,128,128]{2,1,0:T(8,128)(2,1)}, u32[]{:S(2)}, u32[]{:S(2)}) %collective-permute-start.4) | collective-permute-done | bytes 1245216 | tf_op jit(solution)/shard_map/ppermute | solution.py:435
  67.8 2.0 %slice.97 = bf16[19,128,128]{2,1,0:T(8,128)(2,1)} slice(bf16[38,128,128]{2,1,0:T(8,128)(2,1)} %collective-permute-done.4.left), slice={[0:19], [0:128], [0:128]} | slice | bytes 1245184 | tf_op jit(solution)/shard_map/slice | solution.py:437
  69.8 2.2 %collective-permute-start.6 = (bf16[19,128,128]{2,1,0:T(8,128)(2,1)}, bf16[19,128,128]{2,1,0:T(8,128)(2,1)}, u32[]{:S(2)}, u32[]{:S(2)}) collective-permute-start(bf16[19,128,128]{2,1,0:T(8,128)(2,1)} %slice.97), channel_id=1, source_target_pairs={{0,1},{1,2},{2,3},{3,0},{4,5},{5,6},{6,7},{7,4},{8,9},{9,10},{10,1... | collective-permute-start | bytes 1867784 | tf_op jit(solution)/shard_map/ppermute | solution.py:437
  72.0 2.0 %slice.98 = bf16[19,128,128]{2,1,0:T(8,128)(2,1)} slice(bf16[38,128,128]{2,1,0:T(8,128)(2,1)} %collective-permute-done.5.right), slice={[19:38], [0:128], [0:128]} | slice | bytes 1245184 | tf_op jit(solution)/shard_map/slice | solution.py:438
  74.0 4.9 %collective-permute-start.7 = (bf16[19,128,128]{2,1,0:T(8,128)(2,1)}, bf16[19,128,128]{2,1,0:T(8,128)(2,1)}, u32[]{:S(2)}, u32[]{:S(2)}) collective-permute-start(bf16[19,128,128]{2,1,0:T(8,128)(2,1)} %slice.98), channel_id=1, source_target_pairs={{1,0},{2,1},{3,2},{0,3},{5,4},{6,5},{7,6},{4,7},{9,8},{10,9},{11,1... | collective-permute-start | bytes 1867784 | tf_op jit(solution)/shard_map/ppermute | solution.py:438
  81.0 7.4 %collective-permute-done.6.far0 = bf16[19,128,128]{2,1,0:T(8,128)(2,1)} collective-permute-done((bf16[19,128,128]{2,1,0:T(8,128)(2,1)}, bf16[19,128,128]{2,1,0:T(8,128)(2,1)}, u32[]{:S(2)}, u32[]{:S(2)}) %collective-permute-start.6) | collective-permute-done | bytes 622624 | tf_op jit(solution)/shard_map/ppermute | solution.py:437
  88.5 3.2 %collective-permute-done.7.far1 = bf16[19,128,128]{2,1,0:T(8,128)(2,1)} collective-permute-done((bf16[19,128,128]{2,1,0:T(8,128)(2,1)}, bf16[19,128,128]{2,1,0:T(8,128)(2,1)}, u32[]{:S(2)}, u32[]{:S(2)}) %collective-permute-start.7) | collective-permute-done | bytes 622624 | tf_op jit(solution)/shard_map/ppermute | solution.py:438
  93.6 6.4 %start.1 = (f32[30,8,128]{2,1,0:T(8,128)S(1)}, bf16[38,512,128]{2,1,0:T(8,128)(2,1)}, bf16[384,4096]{1,0:T(8,128)(2,1)}) custom-call(s32[4]{0:T(128)S(1)} %copy-done.9, s32[128]{0:T(128)S(1)} %copy-done.7, s32[1]{0:T(128)} %bitcast.15.offset, f32[8,4096]{1,0:T(8,128)S(1)} %copy-done, s32[1,4096]{1,0:T(1,128)S(1)} %bitcast.31, ...), custom_call_target="tpu_custom_call" | custom-call | tf_op jit(solution)/shard_map/start/pallas_call | solution.py:247
  100.6 40.5 %all-to-all-done.refs_0_ = bf16[128,72,128]{2,1,0:T(8,128)(2,1)S(1)} async-done(((bf16[128,72,128]{2,1,0:T(8,128)(2,1)}), bf16[128,72,128]{2,1,0:T(8,128)(2,1)S(1)}, u32[]{:S(2)}, u32[]{:S(2)}) %all-to-all-start) | async-done | bytes 2359328 | tf_op jit(solution)/shard_map/all_to_all | solution.py:431
  142.4 1.9 %collective-permute-start.8 = (f32[6,8,128]{2,1,0:T(8,128)}, f32[6,8,128]{2,1,0:T(8,128)}, u32[]{:S(2)}, u32[]{:S(2)}) collective-permute-start(f32[6,8,128]{2,1,0:T(8,128)} %get-tuple-element.23), channel_id=1, source_target_pairs={{0,4},{4,8},{8,12},{12,16},{16,20},{20,24},{24,28},{28,32},{32,36}... | collective-permute-start | bytes 73736 | tf_op jit(solution)/shard_map/ppermute | solution.py:421
  144.4 5.8 %collective-permute-start.9 = (f32[6,8,128]{2,1,0:T(8,128)}, f32[6,8,128]{2,1,0:T(8,128)}, u32[]{:S(2)}, u32[]{:S(2)}) collective-permute-start(f32[6,8,128]{2,1,0:T(8,128)} %get-tuple-element.24), channel_id=1, source_target_pairs={{4,0},{8,4},{12,8},{16,12},{20,16},{24,20},{28,24},{32,28},{36,32}... | collective-permute-start | bytes 73736 | tf_op jit(solution)/shard_map/ppermute | solution.py:421
  153.4 2.7 %tracts.1 = (f32[4,32,8,128]{3,2,1,0:T(8,128)S(1)}, bf16[38,512,128]{2,1,0:T(8,128)(2,1)S(1)}) custom-call(bf16[128,72,128]{2,1,0:T(8,128)(2,1)S(1)} %all-to-all-done.refs_0_, bf16[256,2048]{1,0:T(8,128)(2,1)S(1)} %compare_convert_fusion.refs_1_, bf16[38,512,128]{2,1,0:T(8,128)(2,1)} %get-tuple-element.21.refs_2_), custom_call_target="tpu_custom_call" | custom-call | tf_op jit(solution)/shard_map/tracts/pallas_call | solution.py:190
  156.2 5.0 %window.1 = (f32[8,4096]{1,0:T(8,128)}, f32[40,128]{1,0:T(8,128)S(1)}, f32[40,128]{1,0:T(8,128)S(1)}, f32[40,128]{1,0:T(8,128)S(1)}) custom-call(s32[4]{0:T(128)S(1)} %copy-done.10, s32[128]{0:T(128)S(1)} %copy-done.8, f32[2]{0:T(128)S(1)} %copy-done.11, f32[8,4096]{1,0:T(8,128)S(1)} %copy-done, f32[10,8,128]{2,1,0:T(8,128)} %collective-permute-done.before, ...), custom_call_target="tpu_custom_call" | custom-call | tf_op jit(solution)/shard_map/window/pallas_call | solution.py:367
  161.2 1.9 %collective-permute-start.10 = (f32[40,128]{1,0:T(8,128)S(1)}, f32[40,128]{1,0:T(8,128)S(1)}, u32[]{:S(2)}, u32[]{:S(2)}) collective-permute-start(f32[40,128]{1,0:T(8,128)S(1)} %get-tuple-element.29), channel_id=1, source_target_pairs={{0,4},{4,8},{8,12},{12,16},{16,20},{20,24},{24,28},{28,32},{32,36}... | collective-permute-start | bytes 61448 | tf_op jit(solution)/shard_map/ppermute | solution.py:421
  163.1 5.8 %collective-permute-start.11 = (f32[40,128]{1,0:T(8,128)S(1)}, f32[40,128]{1,0:T(8,128)S(1)}, u32[]{:S(2)}, u32[]{:S(2)}) collective-permute-start(f32[40,128]{1,0:T(8,128)S(1)} %get-tuple-element.30), channel_id=1, source_target_pairs={{4,0},{8,4},{12,8},{16,12},{20,16},{24,20},{28,24},{32,28},{36,32}... | collective-permute-start | bytes 61448 | tf_op jit(solution)/shard_map/ppermute | solution.py:421
  (72 shorter events, 15.1 us)
Async XLA Ops:
  1.6 16.9 %collective-permute-start.2 = (bf16[3,128,128]{2,1,0:T(8,128)(2,1)S(1)}, bf16[3,128,128]{2,1,0:T(8,128)(2,1)S(1)}, u32[]{:S(2)}, u32[]{:S(2)}) collective-permute-start(bf16[3,128,128]{2,1,0:T(8,128)(2,1)S(1)} %get-tuple-element.34), channel_id=1, source_target_pairs={{0,4},{4,8},{8,12},{12,16},{16,20},{20,24},{24,28},{28,32},{32,36}... | collective-permute-start | bytes 294920 | tf_op jit(solution)/shard_map/ppermute | solution.py:421
  3.5 15.0 %collective-permute-start.3 = (bf16[3,128,128]{2,1,0:T(8,128)(2,1)S(1)}, bf16[3,128,128]{2,1,0:T(8,128)(2,1)S(1)}, u32[]{:S(2)}, u32[]{:S(2)}) collective-permute-start(bf16[3,128,128]{2,1,0:T(8,128)(2,1)S(1)} %get-tuple-element.33), channel_id=1, source_target_pairs={{4,0},{8,4},{12,8},{16,12},{20,16},{24,20},{28,24},{32,28},{36,32}... | collective-permute-start | bytes 294920 | tf_op jit(solution)/shard_map/ppermute | solution.py:421
  18.5 14.3 %copy-start.12 = (bf16[32,1,128,128]{3,2,1,0:T(8,128)(2,1)S(1)}, bf16[32,1,128,128]{3,2,1,0:T(8,128)(2,1)}, u32[]{:S(2)}) copy-start(bf16[32,1,128,128]{3,2,1,0:T(8,128)(2,1)} %param.20) | copy-start | bytes 3145732
  19.1 122.0 %all-to-all-start = ((bf16[128,72,128]{2,1,0:T(8,128)(2,1)}), bf16[128,72,128]{2,1,0:T(8,128)(2,1)S(1)}, u32[]{:S(2)}, u32[]{:S(2)}) async-start(bf16[128,72,128]{2,1,0:T(8,128)(2,1)} %bitcast.32), calls=%async_computation | async-start | bytes 4718592 | tf_op jit(solution)/shard_map/all_to_all | solution.py:431
  32.8 9.3 %copy-start.15 = (s32[32,4]{0,1:T(4,128)S(1)}, s32[32,4]{0,1:T(4,128)}, u32[]{:S(2)}) copy-start(s32[32,4]{0,1:T(4,128)} %param.21) | copy-start | bytes 1540
  32.8 9.4 %copy-start.3 = (f32[4096]{0:T(1024)S(1)}, f32[4096]{0:T(1024)}, u32[]{:S(2)}) copy-start(f32[4096]{0:T(1024)} %param.17) | copy-start | bytes 49156
  32.8 9.4 %copy-start = (f32[8,4096]{1,0:T(8,128)S(1)}, f32[8,4096]{1,0:T(8,128)}, u32[]{:S(2)}) copy-start(f32[8,4096]{1,0:T(8,128)} %activity.3) | copy-start | bytes 393220
  35.0 32.8 %collective-permute-start.4 = (bf16[38,128,128]{2,1,0:T(8,128)(2,1)}, bf16[38,128,128]{2,1,0:T(8,128)(2,1)}, u32[]{:S(2)}, u32[]{:S(2)}) collective-permute-start(bf16[38,128,128]{2,1,0:T(8,128)(2,1)} %pad_maximum_fusion.own), channel_id=1, source_target_pairs={{0,1},{1,2},{2,3},{3,0},{4,5},{5,6},{6,7},{7,4},{8,9},{9,10},{10,1... | collective-permute-start | bytes 3735560 | tf_op jit(solution)/shard_map/ppermute | solution.py:435
  38.4 33.6 %collective-permute-start.5 = (bf16[38,128,128]{2,1,0:T(8,128)(2,1)}, bf16[38,128,128]{2,1,0:T(8,128)(2,1)}, u32[]{:S(2)}, u32[]{:S(2)}) collective-permute-start(bf16[38,128,128]{2,1,0:T(8,128)(2,1)} %pad_maximum_fusion.own), channel_id=1, source_target_pairs={{1,0},{2,1},{3,2},{0,3},{5,4},{6,5},{7,6},{4,7},{9,8},{10,9},{11,1... | collective-permute-start | bytes 3735560 | tf_op jit(solution)/shard_map/ppermute | solution.py:436
  42.9 113.2 %collective-permute-start = (f32[10,8,128]{2,1,0:T(8,128)}, f32[10,8,128]{2,1,0:T(8,128)}, u32[]{:S(2)}, u32[]{:S(2)}) collective-permute-start(f32[10,8,128]{2,1,0:T(8,128)} %pad_maximum_fusion.1), channel_id=1, source_target_pairs={{0,4},{4,8},{8,12},{12,16},{16,20},{20,24},{24,28},{28,32},{32,36}... | collective-permute-start | bytes 122888 | tf_op jit(solution)/shard_map/ppermute | solution.py:421
  45.5 110.5 %collective-permute-start.1 = (f32[10,8,128]{2,1,0:T(8,128)}, f32[10,8,128]{2,1,0:T(8,128)}, u32[]{:S(2)}, u32[]{:S(2)}) collective-permute-start(f32[10,8,128]{2,1,0:T(8,128)} %pad_maximum_fusion.2), channel_id=1, source_target_pairs={{4,0},{8,4},{12,8},{16,12},{20,16},{24,20},{28,24},{32,28},{36,32}... | collective-permute-start | bytes 122888 | tf_op jit(solution)/shard_map/ppermute | solution.py:421
  51.9 27.5 %copy-start.16 = (s32[32,4]{0,1:T(4,128)S(1)}, s32[32,4]{0,1:T(4,128)}, u32[]{:S(2)}) copy-start(s32[32,4]{0,1:T(4,128)} %param.21) | copy-start | bytes 1540
  69.8 18.7 %collective-permute-start.6 = (bf16[19,128,128]{2,1,0:T(8,128)(2,1)}, bf16[19,128,128]{2,1,0:T(8,128)(2,1)}, u32[]{:S(2)}, u32[]{:S(2)}) collective-permute-start(bf16[19,128,128]{2,1,0:T(8,128)(2,1)} %slice.97), channel_id=1, source_target_pairs={{0,1},{1,2},{2,3},{3,0},{4,5},{5,6},{6,7},{7,4},{8,9},{9,10},{10,1... | collective-permute-start | bytes 1867784 | tf_op jit(solution)/shard_map/ppermute | solution.py:437
  74.0 17.6 %collective-permute-start.7 = (bf16[19,128,128]{2,1,0:T(8,128)(2,1)}, bf16[19,128,128]{2,1,0:T(8,128)(2,1)}, u32[]{:S(2)}, u32[]{:S(2)}) collective-permute-start(bf16[19,128,128]{2,1,0:T(8,128)(2,1)} %slice.98), channel_id=1, source_target_pairs={{1,0},{2,1},{3,2},{0,3},{5,4},{6,5},{7,6},{4,7},{9,8},{10,9},{11,1... | collective-permute-start | bytes 1867784 | tf_op jit(solution)/shard_map/ppermute | solution.py:438
  142.4 13.6 %collective-permute-start.8 = (f32[6,8,128]{2,1,0:T(8,128)}, f32[6,8,128]{2,1,0:T(8,128)}, u32[]{:S(2)}, u32[]{:S(2)}) collective-permute-start(f32[6,8,128]{2,1,0:T(8,128)} %get-tuple-element.23), channel_id=1, source_target_pairs={{0,4},{4,8},{8,12},{12,16},{16,20},{20,24},{24,28},{28,32},{32,36}... | collective-permute-start | bytes 73736 | tf_op jit(solution)/shard_map/ppermute | solution.py:421
  144.4 11.7 %collective-permute-start.9 = (f32[6,8,128]{2,1,0:T(8,128)}, f32[6,8,128]{2,1,0:T(8,128)}, u32[]{:S(2)}, u32[]{:S(2)}) collective-permute-start(f32[6,8,128]{2,1,0:T(8,128)} %get-tuple-element.24), channel_id=1, source_target_pairs={{4,0},{8,4},{12,8},{16,12},{20,16},{24,20},{28,24},{32,28},{36,32}... | collective-permute-start | bytes 73736 | tf_op jit(solution)/shard_map/ppermute | solution.py:421
  153.4 2.8 %copy-start.5 = (f32[8,1]{1,0:T(8,128)S(1)}, f32[8,1]{1,0:T(8,128)}, u32[]{:S(2)}) copy-start(f32[8,1]{1,0:T(8,128)} %copy.31.strength) | copy-start | bytes 100
  153.4 2.8 %copy-start.8 = (s32[128]{0:T(128)S(1)}, s32[128]{0:T(128)}, u32[]{:S(2)}) copy-start(s32[128]{0:T(128)} %reshape.145.index) | copy-start | bytes 1540
  153.4 2.8 %copy-start.10 = (s32[4]{0:T(128)S(1)}, s32[4]{0:T(128)}, u32[]{:S(2)}) copy-start(s32[4]{0:T(128)} %and_select_fusion.2.place) | copy-start | bytes 52
  153.4 2.8 %copy-start.11 = (f32[2]{0:T(128)S(1)}, f32[2]{0:T(128)}, u32[]{:S(2)}) copy-start(f32[2]{0:T(128)} %add_convert_fusion.flags) | copy-start | bytes 28
  156.2 14.2 %copy-start.17 = (f32[8,128]{1,0:T(8,128)S(1)}, f32[8,128]{1,0:T(8,128)}, u32[]{:S(2)}) copy-start(f32[8,128]{1,0:T(8,128)} %param.29) | copy-start | bytes 12292
  156.2 14.2 %copy-start.18 = (f32[8,128]{1,0:T(8,128)S(1)}, f32[8,128]{1,0:T(8,128)}, u32[]{:S(2)}) copy-start(f32[8,128]{1,0:T(8,128)} %param.28) | copy-start | bytes 12292
  161.2 7.7 %collective-permute-start.10 = (f32[40,128]{1,0:T(8,128)S(1)}, f32[40,128]{1,0:T(8,128)S(1)}, u32[]{:S(2)}, u32[]{:S(2)}) collective-permute-start(f32[40,128]{1,0:T(8,128)S(1)} %get-tuple-element.29), channel_id=1, source_target_pairs={{0,4},{4,8},{8,12},{12,16},{16,20},{20,24},{24,28},{28,32},{32,36}... | collective-permute-start | bytes 61448 | tf_op jit(solution)/shard_map/ppermute | solution.py:421
  163.1 7.2 %collective-permute-start.11 = (f32[40,128]{1,0:T(8,128)S(1)}, f32[40,128]{1,0:T(8,128)S(1)}, u32[]{:S(2)}, u32[]{:S(2)}) collective-permute-start(f32[40,128]{1,0:T(8,128)S(1)} %get-tuple-element.30), channel_id=1, source_target_pairs={{4,0},{8,4},{12,8},{16,12},{20,16},{24,20},{28,24},{32,28},{36,32}... | collective-permute-start | bytes 61448 | tf_op jit(solution)/shard_map/ppermute | solution.py:421
  (8 other events, 9.5 us)

commit v6 on v5

--- a/solution.py
+++ b/solution.py
@@ -174,7 +174,7 @@
         pltpu.VMEM(((2 * EDGE if edges else nblk) * TR, patches * width), BF16),
     ]
     if edges:
-        outs = [jax.ShapeDtypeStruct((len(PAIRS), TR, BLOCK), F32)] * 2
+        outs = [pltpu.VMEM((len(PAIRS), TR, BLOCK), F32)] * 2
     else:
         outs = [
             jax.ShapeDtypeStruct((STEPS, nblk, TR, BLOCK), F32),
@@ -268,8 +268,8 @@
 
 
 def window_kernel(
-    place, index, flags, activity, before, after, local, coupling, below, above,
-    tiles, drive, slope, strength, kept,
+    patches, place, index, offset, slope, strength, activity, before, after, local, coupling, below, above,
+    tiles, drive, kept,
     rate, mine, to_left, to_right, frame, sums, parts, hits, names, outer, sems,
 ):
     ext = tiles.shape[0]
@@ -289,8 +289,13 @@
     frame[near + nblk :] = after[:near]
     for b in range(nblk):
         frame[near + b] = activity[:, b * BLOCK : (b + 1) * BLOCK]
-    steep = jnp.broadcast_to(slope[...], (TR, BLOCK))
-    strong = jnp.broadcast_to(strength[...], (TR, BLOCK))
+    trial = lax.broadcasted_iota(jnp.int32, (TR, BLOCK), 0)
+    steep, strong = jnp.zeros((TR, BLOCK), F32), jnp.zeros((TR, BLOCK), F32)
+    for t in range(TR):
+        steep = jnp.where(trial == t, slope[t], steep)
+        strong = jnp.where(trial == t, strength[t], strong)
+    is_first = offset[0] < 0
+    is_last = offset[0] >= (patches - 2) * mine.shape[1]
 
     def gather(j):
         if j < EDGE:
@@ -314,9 +319,9 @@
         old = frame[j + 1]
         fresh = old + 0.5 * (jax.nn.sigmoid(pre) - old)
         if b < 0:
-            fresh = fresh * flags[0]
+            fresh = jnp.where(is_first, 0.0, fresh)
         elif b >= nblk:
-            fresh = fresh * flags[1]
+            fresh = jnp.where(is_last, 0.0, fresh)
         frame[j + 1] = fresh
         if 0 <= b < nblk:
             at = slice(b * BLOCK, (b + 1) * BLOCK)
@@ -359,18 +364,22 @@
 
 
 def window(
-    place, index, flags, activity, before, after, local, coupling, below, above, tiles,
-    drive, slope, strength, hits, voxels,
+    place, index, offset, slope, strength, activity, before, after, local, coupling, below, above,
+    tiles, drive, hits, voxels, patches,
 ):
     ext = tiles.shape[0]
     nblk = ext - 2 * EDGE
+
+    def kernel(*refs):
+        window_kernel(patches, *refs)
+
     return pl.pallas_call(
-        window_kernel,
+        kernel,
         out_shape=[
             jax.ShapeDtypeStruct((TR, nblk * BLOCK), F32),
             *[jax.ShapeDtypeStruct(((STEPS + 1) * TR, voxels), F32)] * 3,
         ],
-        in_specs=[SMEM] * 3 + [VMEM] * 11 + [HBM],
+        in_specs=[SMEM] * 5 + [VMEM] * 9 + [HBM],
         out_specs=[VMEM] * 4,
         scratch_shapes=[
             pltpu.VMEM((ext + 2, TR, BLOCK), F32),
@@ -384,8 +393,8 @@
         compiler_params=PARAMS,
         name="window",
     )(
-        place, index, flags, activity, before, after, local, coupling, below, above, tiles,
-        drive, slope, strength, pltpu.with_memory_space_constraint(hits, pltpu.HBM),
+        place, index, offset, slope, strength, activity, before, after, local, coupling, below,
+        above, tiles, drive, pltpu.with_memory_space_constraint(hits, pltpu.HBM),
     )
 
 
@@ -455,7 +464,6 @@
     index = kernel_index.reshape(-1)
     here = lax.axis_index("trial").astype(jnp.int32)
     place = (here + jnp.arange(group, dtype=jnp.int32)) % group
-    flags = jnp.stack([patch > 0, patch < patches - 1]).astype(F32)
     offset = ((patch - 1) * voxels_here).reshape(1)
     owner = voxel_owner.reshape(1, verts)
     local, tiles, hits = start_local(
@@ -469,7 +477,9 @@
     rate, mine, to_left, to_right = window(
         place,
         index,
-        flags,
+        offset,
+        slope,
+        strength,
         activity,
         before,
         after,
@@ -479,10 +489,9 @@
         above,
         tiles,
         drive.reshape(1, verts),
-        slope[:, None],
-        strength[:, None],
         hits,
         voxels_here,
+        patches,
     )
     below, above = sides(to_left, to_right)
     total = mine + below + above

time: 173 us -> 170 us (0.983)
  waiting for transfers between devices: 68.6 us -> 66 us
    broadcast_in_dim x2 -> x0, local copies, waits for them, and re-layouts: 2.64 us -> none  [the longest x1 1.32 us: shards(): strength[:, None]]
    ppermute x1, waiting for transfers between devices: 7.44 us -> 4.89 us  [shards(): far0 = lax.ppermute(left[:half], 'trial', clock)]
    unnamed x39 -> x35, local copies, waits for them, and re-layouts: 3.39 us -> 4.75 us
where the time goes in v6:
time: 170 us; the launch traced here: 167 us
  waiting for transfers between devices  66 us (39%)
  starting transfers between devices  63.7 us (37%)
  Pallas kernels  18.6 us (11%)
  local copies, waits for them, and re-layouts  11.2 us (7%)
  other arithmetic  6.68 us (4%)
    all_to_all x1, waiting for transfers between devices, shards(): got = lax.all_to_all(send, 'patch', split_axis=0, concat_axis=0, tiled=True)  40.5 us
    ppermute x8, starting transfers between devices, sides(): return (lax.ppermute(high, 'patch', up), lax.ppermute(low, 'patch', down))  35.9 us
    ppermute x1, waiting for transfers between devices, shards(): left = lax.ppermute(own, 'trial', clock)  16 us
    all_to_all x1, starting transfers between devices, shards(): got = lax.all_to_all(send, 'patch', split_axis=0, concat_axis=0, tiled=True)  13.7 us
    pallas_call x1, Pallas kernels, start_local(): pl.pallas_call(start_kernel, out_shape=[jax.ShapeDtypeStruct((nblk - 2, T...  6.36 us
    pallas_call x1, Pallas kernels, window(): pl.pallas_call(kernel, out_shape=[jax.ShapeDtypeStruct((TR, nblk * BLOCK)...  5.02 us
    ppermute x1, waiting for transfers between devices, shards(): far0 = lax.ppermute(left[:half], 'trial', clock)  4.89 us
    ppermute x1, starting transfers between devices, shards(): far1 = lax.ppermute(right[half:], 'trial', counter)  4.85 us
  transfers between devices with their start and end apart: 13, of which 5 were waited for; matrix products, arithmetic and copies ran while one was open for 8% of the time, Pallas kernels for 8%

profile of v6, /device:TPU:24, one launch (start us, length us, event | category | flops | bytes accessed | tf_op | source)
XLA Modules:
  0.0 167.2 jit_solution(3367719264869328569)
XLA Ops:
  1.6 1.9 %collective-permute-start.2 = (bf16[3,128,128]{2,1,0:T(8,128)(2,1)S(1)}, bf16[3,128,128]{2,1,0:T(8,128)(2,1)S(1)}, u32[]{:S(2)}, u32[]{:S(2)}) collective-permute-start(bf16[3,128,128]{2,1,0:T(8,128)(2,1)S(1)} %get-tuple-element.34), channel_id=1, source_target_pairs={{0,4},{4,8},{8,12},{12,16},{16,20},{20,24},{24,28},{28,32},{32,36}... | collective-permute-start | bytes 294920 | tf_op jit(solution)/shard_map/ppermute | solution.py:430
  3.5 11.0 %collective-permute-start.3 = (bf16[3,128,128]{2,1,0:T(8,128)(2,1)S(1)}, bf16[3,128,128]{2,1,0:T(8,128)(2,1)S(1)}, u32[]{:S(2)}, u32[]{:S(2)}) collective-permute-start(bf16[3,128,128]{2,1,0:T(8,128)(2,1)S(1)} %get-tuple-element.33), channel_id=1, source_target_pairs={{4,0},{8,4},{12,8},{16,12},{20,16},{24,20},{28,24},{32,28},{36,32}... | collective-permute-start | bytes 294920 | tf_op jit(solution)/shard_map/ppermute | solution.py:430
  14.5 3.9 %pack.1 = bf16[128,9,8,128]{3,2,1,0:T(8,128)(2,1)} custom-call(s32[128]{0:T(128)} %bitcast.32, s32[128]{0:T(128)} %source.1, s32[128]{0:T(128)} %delay.1, s32[128]{0:T(128)} %block.1, f32[128]{0:T(128)} %weight.1, bf16[224,8,128]{2,1,0:T(8,128)(2,1)} %bitcast.31), custom_call_target="tpu_custom_call" | custom-call | tf_op jit(solution)/shard_map/pack/pallas_call | solution.py:93
  19.2 13.7 %all-to-all-start = ((bf16[128,72,128]{2,1,0:T(8,128)(2,1)}), bf16[128,72,128]{2,1,0:T(8,128)(2,1)S(1)}, u32[]{:S(2)}, u32[]{:S(2)}) async-start(bf16[128,72,128]{2,1,0:T(8,128)(2,1)} %bitcast.28), calls=%async_computation | async-start | bytes 4718592 | tf_op jit(solution)/shard_map/all_to_all | solution.py:440
  32.9 2.2 %pad_maximum_fusion.own = bf16[38,128,128]{2,1,0:T(8,128)(2,1)} fusion(bf16[3,128,128]{2,1,0:T(8,128)(2,1)} %copy-done.13, bf16[32,128,128]{2,1,0:T(8,128)(2,1)S(1)} %bitcast.30, bf16[3,128,128]{2,1,0:T(8,128)(2,1)} %copy-done.12), kind=kLoop, calls=%fused_computation.1 | loop fusion | flops 1245184 | bytes 2490368 | tf_op jit(solution)/shard_map/concatenate | solution.py:442
  35.0 3.4 %collective-permute-start.4 = (bf16[38,128,128]{2,1,0:T(8,128)(2,1)}, bf16[38,128,128]{2,1,0:T(8,128)(2,1)}, u32[]{:S(2)}, u32[]{:S(2)}) collective-permute-start(bf16[38,128,128]{2,1,0:T(8,128)(2,1)} %pad_maximum_fusion.own), channel_id=1, source_target_pairs={{0,1},{1,2},{2,3},{3,0},{4,5},{5,6},{6,7},{7,4},{8,9},{9,10},{10,1... | collective-permute-start | bytes 3735560 | tf_op jit(solution)/shard_map/ppermute | solution.py:444
  38.4 3.7 %collective-permute-start.5 = (bf16[38,128,128]{2,1,0:T(8,128)(2,1)}, bf16[38,128,128]{2,1,0:T(8,128)(2,1)}, u32[]{:S(2)}, u32[]{:S(2)}) collective-permute-start(bf16[38,128,128]{2,1,0:T(8,128)(2,1)} %pad_maximum_fusion.own), channel_id=1, source_target_pairs={{1,0},{2,1},{3,2},{0,3},{5,4},{6,5},{7,6},{4,7},{9,8},{10,9},{11,1... | collective-permute-start | bytes 3735560 | tf_op jit(solution)/shard_map/ppermute | solution.py:445
  42.9 1.9 %collective-permute-start = (f32[10,8,128]{2,1,0:T(8,128)}, f32[10,8,128]{2,1,0:T(8,128)}, u32[]{:S(2)}, u32[]{:S(2)}) collective-permute-start(f32[10,8,128]{2,1,0:T(8,128)} %pad_maximum_fusion.1), channel_id=1, source_target_pairs={{0,4},{4,8},{8,12},{12,16},{16,20},{20,24},{24,28},{28,32},{32,36}... | collective-permute-start | bytes 122888 | tf_op jit(solution)/shard_map/ppermute | solution.py:430
  45.5 5.7 %collective-permute-start.1 = (f32[10,8,128]{2,1,0:T(8,128)}, f32[10,8,128]{2,1,0:T(8,128)}, u32[]{:S(2)}, u32[]{:S(2)}) collective-permute-start(f32[10,8,128]{2,1,0:T(8,128)} %pad_maximum_fusion.2), channel_id=1, source_target_pairs={{4,0},{8,4},{12,8},{16,12},{20,16},{24,20},{28,24},{32,28},{36,32}... | collective-permute-start | bytes 122888 | tf_op jit(solution)/shard_map/ppermute | solution.py:430
  51.9 16.0 %collective-permute-done.4.left = bf16[38,128,128]{2,1,0:T(8,128)(2,1)} collective-permute-done((bf16[38,128,128]{2,1,0:T(8,128)(2,1)}, bf16[38,128,128]{2,1,0:T(8,128)(2,1)}, u32[]{:S(2)}, u32[]{:S(2)}) %collective-permute-start.4) | collective-permute-done | bytes 1245216 | tf_op jit(solution)/shard_map/ppermute | solution.py:444
  67.9 2.0 %slice.97 = bf16[19,128,128]{2,1,0:T(8,128)(2,1)} slice(bf16[38,128,128]{2,1,0:T(8,128)(2,1)} %collective-permute-done.4.left), slice={[0:19], [0:128], [0:128]} | slice | bytes 1245184 | tf_op jit(solution)/shard_map/slice | solution.py:446
  69.8 2.2 %collective-permute-start.6 = (bf16[19,128,128]{2,1,0:T(8,128)(2,1)}, bf16[19,128,128]{2,1,0:T(8,128)(2,1)}, u32[]{:S(2)}, u32[]{:S(2)}) collective-permute-start(bf16[19,128,128]{2,1,0:T(8,128)(2,1)} %slice.97), channel_id=1, source_target_pairs={{0,1},{1,2},{2,3},{3,0},{4,5},{5,6},{6,7},{7,4},{8,9},{9,10},{10,1... | collective-permute-start | bytes 1867784 | tf_op jit(solution)/shard_map/ppermute | solution.py:446
  72.0 2.0 %slice.98 = bf16[19,128,128]{2,1,0:T(8,128)(2,1)} slice(bf16[38,128,128]{2,1,0:T(8,128)(2,1)} %collective-permute-done.5.right), slice={[19:38], [0:128], [0:128]} | slice | bytes 1245184 | tf_op jit(solution)/shard_map/slice | solution.py:447
  74.0 4.9 %collective-permute-start.7 = (bf16[19,128,128]{2,1,0:T(8,128)(2,1)}, bf16[19,128,128]{2,1,0:T(8,128)(2,1)}, u32[]{:S(2)}, u32[]{:S(2)}) collective-permute-start(bf16[19,128,128]{2,1,0:T(8,128)(2,1)} %slice.98), channel_id=1, source_target_pairs={{1,0},{2,1},{3,2},{0,3},{5,4},{6,5},{7,6},{4,7},{9,8},{10,9},{11,1... | collective-permute-start | bytes 1867784 | tf_op jit(solution)/shard_map/ppermute | solution.py:447
  83.6 4.9 %collective-permute-done.6.far0 = bf16[19,128,128]{2,1,0:T(8,128)(2,1)} collective-permute-done((bf16[19,128,128]{2,1,0:T(8,128)(2,1)}, bf16[19,128,128]{2,1,0:T(8,128)(2,1)}, u32[]{:S(2)}, u32[]{:S(2)}) %collective-permute-start.6) | collective-permute-done | bytes 622624 | tf_op jit(solution)/shard_map/ppermute | solution.py:446
  88.5 3.2 %collective-permute-done.7.far1 = bf16[19,128,128]{2,1,0:T(8,128)(2,1)} collective-permute-done((bf16[19,128,128]{2,1,0:T(8,128)(2,1)}, bf16[19,128,128]{2,1,0:T(8,128)(2,1)}, u32[]{:S(2)}, u32[]{:S(2)}) %collective-permute-start.7) | collective-permute-done | bytes 622624 | tf_op jit(solution)/shard_map/ppermute | solution.py:447
  93.7 6.4 %start.1 = (f32[30,8,128]{2,1,0:T(8,128)S(1)}, bf16[38,512,128]{2,1,0:T(8,128)(2,1)}, bf16[384,4096]{1,0:T(8,128)(2,1)}) custom-call(s32[4]{0:T(128)S(1)} %copy-done.7, s32[128]{0:T(128)S(1)} %copy-done.5, s32[1]{0:T(128)} %bitcast.offset.refs_2_, f32[8,4096]{1,0:T(8,128)S(1)} %copy-done, s32[1,4096]{1,0:T(1,128)S(1)} %bitcast.27, ...), custom_call_target="tpu_custom_call" | custom-call | tf_op jit(solution)/shard_map/start/pallas_call | solution.py:247
  100.7 40.5 %all-to-all-done.refs_0_ = bf16[128,72,128]{2,1,0:T(8,128)(2,1)S(1)} async-done(((bf16[128,72,128]{2,1,0:T(8,128)(2,1)}), bf16[128,72,128]{2,1,0:T(8,128)(2,1)S(1)}, u32[]{:S(2)}, u32[]{:S(2)}) %all-to-all-start) | async-done | bytes 2359328 | tf_op jit(solution)/shard_map/all_to_all | solution.py:440
  141.9 1.9 %collective-permute-start.8 = (f32[6,8,128]{2,1,0:T(8,128)S(1)}, f32[6,8,128]{2,1,0:T(8,128)S(1)}, u32[]{:S(2)}, u32[]{:S(2)}) collective-permute-start(f32[6,8,128]{2,1,0:T(8,128)S(1)} %get-tuple-element.23), channel_id=1, source_target_pairs={{0,4},{4,8},{8,12},{12,16},{16,20},{20,24},{24,28},{28,32},{32,36}... | collective-permute-start | bytes 73736 | tf_op jit(solution)/shard_map/ppermute | solution.py:430
  143.8 5.8 %collective-permute-start.9 = (f32[6,8,128]{2,1,0:T(8,128)S(1)}, f32[6,8,128]{2,1,0:T(8,128)S(1)}, u32[]{:S(2)}, u32[]{:S(2)}) collective-permute-start(f32[6,8,128]{2,1,0:T(8,128)S(1)} %get-tuple-element.24), channel_id=1, source_target_pairs={{4,0},{8,4},{12,8},{16,12},{20,16},{24,20},{28,24},{32,28},{36,32}... | collective-permute-start | bytes 73736 | tf_op jit(solution)/shard_map/ppermute | solution.py:430
  149.6 2.7 %tracts.1 = (f32[4,32,8,128]{3,2,1,0:T(8,128)S(1)}, bf16[38,512,128]{2,1,0:T(8,128)(2,1)S(1)}) custom-call(bf16[128,72,128]{2,1,0:T(8,128)(2,1)S(1)} %all-to-all-done.refs_0_, bf16[256,2048]{1,0:T(8,128)(2,1)S(1)} %compare_convert_fusion.refs_1_, bf16[38,512,128]{2,1,0:T(8,128)(2,1)} %get-tuple-element.21.refs_2_), custom_call_target="tpu_custom_call" | custom-call | tf_op jit(solution)/shard_map/tracts/pallas_call | solution.py:190
  152.4 5.0 %window.1 = (f32[8,4096]{1,0:T(8,128)}, f32[40,128]{1,0:T(8,128)S(1)}, f32[40,128]{1,0:T(8,128)S(1)}, f32[40,128]{1,0:T(8,128)S(1)}) custom-call(s32[4]{0:T(128)S(1)} %copy-done.8, s32[128]{0:T(128)S(1)} %copy-done.6, s32[1]{0:T(128)} %bitcast.offset.refs_2_, f32[8]{0:T(128)S(1)} %copy-done.9, f32[8]{0:T(128)S(1)} %copy-done.10, f32[8,4096]{1,0:T(8,128)S(1)} %copy-done, ...), custom_call_target="tpu_custom_call" | custom-call | tf_op jit(solution)/shard_map/window/pallas_call | solution.py:376
  157.4 1.9 %collective-permute-start.10 = (f32[40,128]{1,0:T(8,128)S(1)}, f32[40,128]{1,0:T(8,128)S(1)}, u32[]{:S(2)}, u32[]{:S(2)}) collective-permute-start(f32[40,128]{1,0:T(8,128)S(1)} %get-tuple-element.29), channel_id=1, source_target_pairs={{0,4},{4,8},{8,12},{12,16},{16,20},{20,24},{24,28},{28,32},{32,36}... | collective-permute-start | bytes 61448 | tf_op jit(solution)/shard_map/ppermute | solution.py:430
  159.4 5.8 %collective-permute-start.11 = (f32[40,128]{1,0:T(8,128)S(1)}, f32[40,128]{1,0:T(8,128)S(1)}, u32[]{:S(2)}, u32[]{:S(2)}) collective-permute-start(f32[40,128]{1,0:T(8,128)S(1)} %get-tuple-element.30), channel_id=1, source_target_pairs={{4,0},{8,4},{12,8},{16,12},{20,16},{24,20},{28,24},{32,28},{36,32}... | collective-permute-start | bytes 61448 | tf_op jit(solution)/shard_map/ppermute | solution.py:430
  (65 shorter events, 13.9 us)
Async XLA Ops:
  1.6 16.9 %collective-permute-start.2 = (bf16[3,128,128]{2,1,0:T(8,128)(2,1)S(1)}, bf16[3,128,128]{2,1,0:T(8,128)(2,1)S(1)}, u32[]{:S(2)}, u32[]{:S(2)}) collective-permute-start(bf16[3,128,128]{2,1,0:T(8,128)(2,1)S(1)} %get-tuple-element.34), channel_id=1, source_target_pairs={{0,4},{4,8},{8,12},{12,16},{16,20},{20,24},{24,28},{28,32},{32,36}... | collective-permute-start | bytes 294920 | tf_op jit(solution)/shard_map/ppermute | solution.py:430
  3.5 15.0 %collective-permute-start.3 = (bf16[3,128,128]{2,1,0:T(8,128)(2,1)S(1)}, bf16[3,128,128]{2,1,0:T(8,128)(2,1)S(1)}, u32[]{:S(2)}, u32[]{:S(2)}) collective-permute-start(bf16[3,128,128]{2,1,0:T(8,128)(2,1)S(1)} %get-tuple-element.33), channel_id=1, source_target_pairs={{4,0},{8,4},{12,8},{16,12},{20,16},{24,20},{28,24},{32,28},{36,32}... | collective-permute-start | bytes 294920 | tf_op jit(solution)/shard_map/ppermute | solution.py:430
  18.5 14.3 %copy-start.11 = (bf16[32,1,128,128]{3,2,1,0:T(8,128)(2,1)S(1)}, bf16[32,1,128,128]{3,2,1,0:T(8,128)(2,1)}, u32[]{:S(2)}) copy-start(bf16[32,1,128,128]{3,2,1,0:T(8,128)(2,1)} %param.20) | copy-start | bytes 3145732
  19.2 122.0 %all-to-all-start = ((bf16[128,72,128]{2,1,0:T(8,128)(2,1)}), bf16[128,72,128]{2,1,0:T(8,128)(2,1)S(1)}, u32[]{:S(2)}, u32[]{:S(2)}) async-start(bf16[128,72,128]{2,1,0:T(8,128)(2,1)} %bitcast.28), calls=%async_computation | async-start | bytes 4718592 | tf_op jit(solution)/shard_map/all_to_all | solution.py:440
  32.8 9.3 %copy-start.14 = (s32[32,4]{0,1:T(4,128)S(1)}, s32[32,4]{0,1:T(4,128)}, u32[]{:S(2)}) copy-start(s32[32,4]{0,1:T(4,128)} %param.21) | copy-start | bytes 1540
  32.8 9.4 %copy-start.3 = (f32[4096]{0:T(1024)S(1)}, f32[4096]{0:T(1024)}, u32[]{:S(2)}) copy-start(f32[4096]{0:T(1024)} %param.17) | copy-start | bytes 49156
  32.8 9.4 %copy-start = (f32[8,4096]{1,0:T(8,128)S(1)}, f32[8,4096]{1,0:T(8,128)}, u32[]{:S(2)}) copy-start(f32[8,4096]{1,0:T(8,128)} %refs_5_.1) | copy-start | bytes 393220
  35.0 32.8 %collective-permute-start.4 = (bf16[38,128,128]{2,1,0:T(8,128)(2,1)}, bf16[38,128,128]{2,1,0:T(8,128)(2,1)}, u32[]{:S(2)}, u32[]{:S(2)}) collective-permute-start(bf16[38,128,128]{2,1,0:T(8,128)(2,1)} %pad_maximum_fusion.own), channel_id=1, source_target_pairs={{0,1},{1,2},{2,3},{3,0},{4,5},{5,6},{6,7},{7,4},{8,9},{9,10},{10,1... | collective-permute-start | bytes 3735560 | tf_op jit(solution)/shard_map/ppermute | solution.py:444
  38.4 33.6 %collective-permute-start.5 = (bf16[38,128,128]{2,1,0:T(8,128)(2,1)}, bf16[38,128,128]{2,1,0:T(8,128)(2,1)}, u32[]{:S(2)}, u32[]{:S(2)}) collective-permute-start(bf16[38,128,128]{2,1,0:T(8,128)(2,1)} %pad_maximum_fusion.own), channel_id=1, source_target_pairs={{1,0},{2,1},{3,2},{0,3},{5,4},{6,5},{7,6},{4,7},{9,8},{10,9},{11,1... | collective-permute-start | bytes 3735560 | tf_op jit(solution)/shard_map/ppermute | solution.py:445
  42.9 109.4 %collective-permute-start = (f32[10,8,128]{2,1,0:T(8,128)}, f32[10,8,128]{2,1,0:T(8,128)}, u32[]{:S(2)}, u32[]{:S(2)}) collective-permute-start(f32[10,8,128]{2,1,0:T(8,128)} %pad_maximum_fusion.1), channel_id=1, source_target_pairs={{0,4},{4,8},{8,12},{12,16},{16,20},{20,24},{24,28},{28,32},{32,36}... | collective-permute-start | bytes 122888 | tf_op jit(solution)/shard_map/ppermute | solution.py:430
  45.5 106.8 %collective-permute-start.1 = (f32[10,8,128]{2,1,0:T(8,128)}, f32[10,8,128]{2,1,0:T(8,128)}, u32[]{:S(2)}, u32[]{:S(2)}) collective-permute-start(f32[10,8,128]{2,1,0:T(8,128)} %pad_maximum_fusion.2), channel_id=1, source_target_pairs={{4,0},{8,4},{12,8},{16,12},{20,16},{24,20},{28,24},{32,28},{36,32}... | collective-permute-start | bytes 122888 | tf_op jit(solution)/shard_map/ppermute | solution.py:430
  69.8 18.7 %collective-permute-start.6 = (bf16[19,128,128]{2,1,0:T(8,128)(2,1)}, bf16[19,128,128]{2,1,0:T(8,128)(2,1)}, u32[]{:S(2)}, u32[]{:S(2)}) collective-permute-start(bf16[19,128,128]{2,1,0:T(8,128)(2,1)} %slice.97), channel_id=1, source_target_pairs={{0,1},{1,2},{2,3},{3,0},{4,5},{5,6},{6,7},{7,4},{8,9},{9,10},{10,1... | collective-permute-start | bytes 1867784 | tf_op jit(solution)/shard_map/ppermute | solution.py:446
  74.0 17.6 %collective-permute-start.7 = (bf16[19,128,128]{2,1,0:T(8,128)(2,1)}, bf16[19,128,128]{2,1,0:T(8,128)(2,1)}, u32[]{:S(2)}, u32[]{:S(2)}) collective-permute-start(bf16[19,128,128]{2,1,0:T(8,128)(2,1)} %slice.98), channel_id=1, source_target_pairs={{1,0},{2,1},{3,2},{0,3},{5,4},{6,5},{7,6},{4,7},{9,8},{10,9},{11,1... | collective-permute-start | bytes 1867784 | tf_op jit(solution)/shard_map/ppermute | solution.py:447
  141.9 10.5 %collective-permute-start.8 = (f32[6,8,128]{2,1,0:T(8,128)S(1)}, f32[6,8,128]{2,1,0:T(8,128)S(1)}, u32[]{:S(2)}, u32[]{:S(2)}) collective-permute-start(f32[6,8,128]{2,1,0:T(8,128)S(1)} %get-tuple-element.23), channel_id=1, source_target_pairs={{0,4},{4,8},{8,12},{12,16},{16,20},{20,24},{24,28},{28,32},{32,36}... | collective-permute-start | bytes 73736 | tf_op jit(solution)/shard_map/ppermute | solution.py:430
  143.8 8.5 %collective-permute-start.9 = (f32[6,8,128]{2,1,0:T(8,128)S(1)}, f32[6,8,128]{2,1,0:T(8,128)S(1)}, u32[]{:S(2)}, u32[]{:S(2)}) collective-permute-start(f32[6,8,128]{2,1,0:T(8,128)S(1)} %get-tuple-element.24), channel_id=1, source_target_pairs={{4,0},{8,4},{12,8},{16,12},{20,16},{24,20},{28,24},{32,28},{36,32}... | collective-permute-start | bytes 73736 | tf_op jit(solution)/shard_map/ppermute | solution.py:430
  149.5 2.8 %copy-start.2 = (f32[30,8,128]{2,1,0:T(8,128)S(1)}, f32[30,8,128]{2,1,0:T(8,128)}, u32[]{:S(2)}) copy-start(f32[30,8,128]{2,1,0:T(8,128)} %copy-done.1) | copy-start | bytes 368644
  149.6 2.8 %copy-start.6 = (s32[128]{0:T(128)S(1)}, s32[128]{0:T(128)}, u32[]{:S(2)}) copy-start(s32[128]{0:T(128)} %reshape.145.index.refs_1_) | copy-start | bytes 1540
  149.6 2.8 %copy-start.8 = (s32[4]{0:T(128)S(1)}, s32[4]{0:T(128)}, u32[]{:S(2)}) copy-start(s32[4]{0:T(128)} %and_select_fusion.2.place.refs_0_) | copy-start | bytes 52
  149.6 2.8 %copy-start.9 = (f32[8]{0:T(128)S(1)}, f32[8]{0:T(128)}, u32[]{:S(2)}) copy-start(f32[8]{0:T(128)} %refs_3_.1) | copy-start | bytes 100
  149.6 2.8 %copy-start.10 = (f32[8]{0:T(128)S(1)}, f32[8]{0:T(128)}, u32[]{:S(2)}) copy-start(f32[8]{0:T(128)} %refs_4_.1) | copy-start | bytes 100
  152.4 14.2 %copy-start.15 = (f32[8,128]{1,0:T(8,128)S(1)}, f32[8,128]{1,0:T(8,128)}, u32[]{:S(2)}) copy-start(f32[8,128]{1,0:T(8,128)} %param.29) | copy-start | bytes 12292
  152.4 14.2 %copy-start.16 = (f32[8,128]{1,0:T(8,128)S(1)}, f32[8,128]{1,0:T(8,128)}, u32[]{:S(2)}) copy-start(f32[8,128]{1,0:T(8,128)} %param.28) | copy-start | bytes 12292
  157.4 7.7 %collective-permute-start.10 = (f32[40,128]{1,0:T(8,128)S(1)}, f32[40,128]{1,0:T(8,128)S(1)}, u32[]{:S(2)}, u32[]{:S(2)}) collective-permute-start(f32[40,128]{1,0:T(8,128)S(1)} %get-tuple-element.29), channel_id=1, source_target_pairs={{0,4},{4,8},{8,12},{12,16},{16,20},{20,24},{24,28},{28,32},{32,36}... | collective-permute-start | bytes 61448 | tf_op jit(solution)/shard_map/ppermute | solution.py:430
  159.4 7.2 %collective-permute-start.11 = (f32[40,128]{1,0:T(8,128)S(1)}, f32[40,128]{1,0:T(8,128)S(1)}, u32[]{:S(2)}, u32[]{:S(2)}) collective-permute-start(f32[40,128]{1,0:T(8,128)S(1)} %get-tuple-element.30), channel_id=1, source_target_pairs={{4,0},{8,4},{12,8},{16,12},{20,16},{24,20},{28,24},{32,28},{36,32}... | collective-permute-start | bytes 61448 | tf_op jit(solution)/shard_map/ppermute | solution.py:430
  (6 other events, 4.0 us)

commit v7 on v6

--- a/solution.py
+++ b/solution.py
@@ -132,7 +132,8 @@
 
 def tract_kernel(nblk, edges, got, spread, *rest):
     if edges:
-        *outs, names, picks = rest
+        patch, *outs, names, picks = rest
+        even = patch[0] % 2 == 0
     else:
         tiles, *outs, kept, names, picks, sem = rest
         load = pltpu.make_async_copy(tiles, kept, sem)
@@ -155,13 +156,15 @@
             continue
         for i in range(EDGE - s):
             n = PAIRS.index((s, i))
-            outs[0][n] = total[i * TR : (i + 1) * TR]
-            outs[1][n] = total[(EDGE + s + i) * TR : (EDGE + s + i + 1) * TR]
+            low = total[i * TR : (i + 1) * TR]
+            high = total[(EDGE + s + i) * TR : (EDGE + s + i + 1) * TR]
+            outs[0][n] = jnp.where(even, high, low)
+            outs[1][n] = jnp.where(even, low, high)
     if not edges:
         load.wait()
 
 
-def tract_sums(got, nblk, tiles=None):
+def tract_sums(got, nblk, patch, tiles=None):
     edges = tiles is None
     patches = got.shape[0]
     width = 2 * TR
@@ -175,6 +178,8 @@
     ]
     if edges:
         outs = [pltpu.VMEM((len(PAIRS), TR, BLOCK), F32)] * 2
+        operands.append(patch)
+        in_specs.append(SMEM)
     else:
         outs = [
             jax.ShapeDtypeStruct((STEPS, nblk, TR, BLOCK), F32),
@@ -268,9 +273,9 @@
 
 
 def window_kernel(
-    patches, place, index, offset, slope, strength, activity, before, after, local, coupling, below, above,
+    patches, place, index, patch, slope, strength, activity, before, after, local, coupling, inner_swap, outer_swap,
     tiles, drive, kept,
-    rate, mine, to_left, to_right, frame, sums, parts, hits, names, outer, sems,
+    rate, mine, to_inner, to_outer, frame, sums, parts, hits, names, outer, sems,
 ):
     ext = tiles.shape[0]
     nblk = ext - 2 * EDGE
@@ -294,8 +299,9 @@
     for t in range(TR):
         steep = jnp.where(trial == t, slope[t], steep)
         strong = jnp.where(trial == t, strength[t], strong)
-    is_first = offset[0] < 0
-    is_last = offset[0] >= (patches - 2) * mine.shape[1]
+    is_first = patch[0] == 0
+    is_last = patch[0] == patches - 1
+    even = patch[0] % 2 == 0
 
     def gather(j):
         if j < EDGE:
@@ -309,9 +315,11 @@
     def advance(step, j):
         b = j - EDGE
         if b < 0:
-            tracts, input_ = below[PAIRS.index((step, j - step))], before[near + j]
+            n, input_ = PAIRS.index((step, j - step)), before[near + j]
+            tracts = jnp.where(even, outer_swap[n], inner_swap[n])
         elif b >= nblk:
-            tracts, input_ = above[PAIRS.index((step, b - nblk))], after[near + b - nblk]
+            n, input_ = PAIRS.index((step, b - nblk)), after[near + b - nblk]
+            tracts = jnp.where(even, inner_swap[n], outer_swap[n])
         else:
             tracts, input_ = coupling[step, b], drive[:, b * BLOCK : (b + 1) * BLOCK]
         summed = local[b - 1] if step == 0 and 0 < b < nblk - 1 else sums[j]
@@ -354,17 +362,20 @@
         total = total + lax.dot_general(
             parts[:, c : c + CHUNK], hit, (((1,), (1,)), ((), ())), preferred_element_type=F32
         )
-    for n, out in enumerate((to_left, mine, to_right)):
+    def level_sums(n):
         at = slice(n * mine.shape[1], (n + 1) * mine.shape[1])
-        for step in range(STEPS):
-            high = total[2 * TR * step : 2 * TR * step + TR, at]
-            low = total[2 * TR * step + TR : 2 * TR * (step + 1), at]
-            out[TR * step : TR * (step + 1)] = high + low
-        out[TR * STEPS :] = total[rows : rows + TR, at]
+        pairs = [total[2 * TR * step : 2 * TR * (step + 1), at] for step in range(STEPS)]
+        return [x[:TR] + x[TR:] for x in pairs] + [total[rows : rows + TR, at]]
+
+    for step, (low, own, high) in enumerate(zip(*[level_sums(n) for n in range(3)])):
+        at = slice(TR * step, TR * (step + 1))
+        mine[at] = own
+        to_inner[at] = jnp.where(even, high, low)
+        to_outer[at] = jnp.where(even, low, high)
 
 
 def window(
-    place, index, offset, slope, strength, activity, before, after, local, coupling, below, above,
+    place, index, patch, slope, strength, activity, before, after, local, coupling, below, above,
     tiles, drive, hits, voxels, patches,
 ):
     ext = tiles.shape[0]
@@ -393,7 +404,7 @@
         compiler_params=PARAMS,
         name="window",
     )(
-        place, index, offset, slope, strength, activity, before, after, local, coupling, below,
+        place, index, patch, slope, strength, activity, before, after, local, coupling, below,
         above, tiles, drive, pltpu.with_memory_space_constraint(hits, pltpu.HBM),
     )
 
@@ -420,26 +431,34 @@
     patches = lax.axis_size("patch")
     group = lax.axis_size("trial")
     voxels_here = vaso_signal.shape[1]
-    up = [(i, i + 1) for i in range(patches - 1)]
-    down = [(j, i) for i, j in up]
+    inner = [(i ^ 1, i) for i in range(patches)]
+    outer = [(j, i) for i in range(1, patches - 1, 2) for i, j in ((i, i + 1), (i + 1, i))]
     clock = [(i, (i + 1) % group) for i in range(group)]
     counter = [(j, i) for i, j in clock]
     patch = lax.axis_index("patch").astype(jnp.int32)
 
+    even = patch % 2 == 0
+
+    def swap(to_inner, to_outer):
+        return lax.ppermute(to_inner, "patch", inner), lax.ppermute(to_outer, "patch", outer)
+
     def sides(low, high):
-        return lax.ppermute(high, "patch", up), lax.ppermute(low, "patch", down)
+        a, b = swap(jnp.where(even, high, low), jnp.where(even, low, high))
+        return jnp.where(even, b, a), jnp.where(even, a, b)
 
     raw = kernel.reshape(nblk, BLOCK, BLOCK)
-    before, after = sides(raw[:EDGE], raw[nblk - EDGE :])
+    low, high = raw[:EDGE], raw[nblk - EDGE :]
+    swapped = swap(jnp.where(even, high, low), jnp.where(even, low, high))
     send = pack(
         tract_target[:, 0], tract_source, tract_delay, tract_block, tract_weight, history, patches
     )
-    send, _, _ = lax.optimization_barrier((send, before, after))
+    send, _ = lax.optimization_barrier((send, swapped))
     rows = (2 * STEPS + 1) * TR
     send = send.reshape(patches, rows, BLOCK)
     got = lax.all_to_all(send, "patch", split_axis=0, concat_axis=0, tiled=True)
 
-    own = jnp.concatenate([before, raw, after], axis=0)
+    a, b = swapped
+    own = jnp.concatenate([jnp.where(even, b, a), raw, jnp.where(even, a, b)], axis=0)
     half = own.shape[0] // 2
     left = lax.ppermute(own, "trial", clock)
     right = lax.ppermute(own, "trial", counter)
@@ -471,13 +490,13 @@
     )
 
     got, local = lax.optimization_barrier((got, local))
-    first, last = tract_sums(got, nblk)
-    below, above = sides(first, last)
-    coupling, tiles = tract_sums(got, nblk, tiles)
-    rate, mine, to_left, to_right = window(
+    where = patch.reshape(1)
+    below, above = swap(*tract_sums(got, nblk, where))
+    coupling, tiles = tract_sums(got, nblk, where, tiles)
+    rate, mine, to_inner, to_outer = window(
         place,
         index,
-        offset,
+        where,
         slope,
         strength,
         activity,
@@ -493,7 +512,7 @@
         voxels_here,
         patches,
     )
-    below, above = sides(to_left, to_right)
+    below, above = swap(to_inner, to_outer)
     total = mine + below + above
     floor = jnp.maximum(total[STEPS * TR :], 1.0)
     vaso, flow = vaso_signal, blood_flow

time: 170 us -> 167 us (0.982)
  starting transfers between devices: 63.7 us -> 54.9 us
  waiting for transfers between devices: 66 us -> 72.6 us
    ppermute x8, starting transfers between devices: 35.9 us -> 29.4 us  [the longest x4 20.8 us: swap(): lax.ppermute(to_outer, 'patch', outer)]
    ppermute x8, waiting for transfers between devices: 1.47 us -> 5.78 us  [the longest x4 5.77 us: swap(): lax.ppermute(to_outer, 'patch', outer)]
    select_n x0 -> x4, other arithmetic: none -> 3.32 us  [the longest x1 0.96 us: shards(): swapped = swap(jnp.where(even, high, low), jnp.where(even, low, high))]
    ppermute x1, waiting for transfers between devices: 16 us -> 18.2 us  [shards(): left = lax.ppermute(own, 'trial', clock)]
    concatenate x3 -> x1, other arithmetic: 3.42 us -> 1.19 us  [shards(): jnp.concatenate([jnp.where(even, b, a), raw, jnp.where(even, a, b)], axis=0)]
    all_to_all x1, starting transfers between devices: 13.7 us -> 11.5 us  [shards(): got = lax.all_to_all(send, 'patch', split_axis=0, concat_axis=0, tiled=True)]
    unnamed x35 -> x33, local copies, waits for them, and re-layouts: 4.75 us -> 4.74 us
  transfers between devices with their start and end apart: 13 -> 13, of which waited for: 5 -> 6; matrix products, arithmetic and copies ran while one was open for 8% -> 8% of each run, Pallas kernels for 8% -> 8%
where the time goes in v7:
time: 167 us; the launch traced here: 165 us
  waiting for transfers between devices  72.6 us (43%)
  starting transfers between devices  54.9 us (33%)
  Pallas kernels  18.4 us (11%)
  local copies, waits for them, and re-layouts  10.3 us (6%)
  other arithmetic  7.78 us (5%)
    all_to_all x1, waiting for transfers between devices, shards(): got = lax.all_to_all(send, 'patch', split_axis=0, concat_axis=0, tiled=True)  40.5 us
    ppermute x4, starting transfers between devices, swap(): lax.ppermute(to_outer, 'patch', outer)  20.8 us
    ppermute x1, waiting for transfers between devices, shards(): left = lax.ppermute(own, 'trial', clock)  18.2 us
    all_to_all x1, starting transfers between devices, shards(): got = lax.all_to_all(send, 'patch', split_axis=0, concat_axis=0, tiled=True)  11.5 us
    ppermute x4, starting transfers between devices, swap(): lax.ppermute(to_inner, 'patch', inner)  8.53 us
    pallas_call x1, Pallas kernels, start_local(): pl.pallas_call(start_kernel, out_shape=[jax.ShapeDtypeStruct((nblk - 2, T...  6.38 us
    ppermute x4, waiting for transfers between devices, swap(): lax.ppermute(to_outer, 'patch', outer)  5.77 us
    ppermute x1, waiting for transfers between devices, shards(): far0 = lax.ppermute(left[:half], 'trial', clock)  4.89 us
  transfers between devices with their start and end apart: 13, of which 6 were waited for; matrix products, arithmetic and copies ran while one was open for 8% of the time, Pallas kernels for 8%

profile of v7, /device:TPU:24, one launch (start us, length us, event | category | flops | bytes accessed | tf_op | source)
XLA Modules:
  0.0 165.0 jit_solution(2661394697856172421)
XLA Ops:
  1.6 1.9 %collective-permute-start.2 = (bf16[3,128,128]{2,1,0:T(8,128)(2,1)S(1)}, bf16[3,128,128]{2,1,0:T(8,128)(2,1)S(1)}, u32[]{:S(2)}, u32[]{:S(2)}) collective-permute-start(bf16[3,128,128]{2,1,0:T(8,128)(2,1)S(1)} %get-tuple-element.34), channel_id=1, source_target_pairs={{4,0},{0,4},{12,8},{8,12},{20,16},{16,20},{28,24},{24,28},{36,32},... | collective-permute-start | bytes 294920 | tf_op jit(solution)/shard_map/ppermute | solution.py:443
  3.5 11.7 %collective-permute-start.3 = (bf16[3,128,128]{2,1,0:T(8,128)(2,1)S(1)}, bf16[3,128,128]{2,1,0:T(8,128)(2,1)S(1)}, u32[]{:S(2)}, u32[]{:S(2)}) collective-permute-start(bf16[3,128,128]{2,1,0:T(8,128)(2,1)S(1)} %get-tuple-element.33), channel_id=1, source_target_pairs={{8,4},{4,8},{16,12},{12,16},{24,20},{20,24},{32,28},{28,32},{40,36... | collective-permute-start | bytes 294920 | tf_op jit(solution)/shard_map/ppermute | solution.py:443
  15.2 3.9 %pack.1 = bf16[128,9,8,128]{3,2,1,0:T(8,128)(2,1)} custom-call(s32[128]{0:T(128)} %bitcast.33, s32[128]{0:T(128)} %source.1, s32[128]{0:T(128)} %delay.1, s32[128]{0:T(128)} %block.1, f32[128]{0:T(128)} %weight.1, bf16[224,8,128]{2,1,0:T(8,128)(2,1)} %bitcast.32), custom_call_target="tpu_custom_call" | custom-call | tf_op jit(solution)/shard_map/pack/pallas_call | solution.py:93
  19.8 11.5 %all-to-all-start = ((bf16[128,72,128]{2,1,0:T(8,128)(2,1)}), bf16[128,72,128]{2,1,0:T(8,128)(2,1)S(1)}, u32[]{:S(2)}, u32[]{:S(2)}) async-start(bf16[128,72,128]{2,1,0:T(8,128)(2,1)} %bitcast.29), calls=%async_computation | async-start | bytes 4718592 | tf_op jit(solution)/shard_map/all_to_all | solution.py:458
  33.4 3.4 %collective-permute-start.4 = (bf16[38,128,128]{2,1,0:T(8,128)(2,1)}, bf16[38,128,128]{2,1,0:T(8,128)(2,1)}, u32[]{:S(2)}, u32[]{:S(2)}) collective-permute-start(bf16[38,128,128]{2,1,0:T(8,128)(2,1)} %pad_maximum_fusion.own), channel_id=1, source_target_pairs={{0,1},{1,2},{2,3},{3,0},{4,5},{5,6},{6,7},{7,4},{8,9},{9,10},{10,1... | collective-permute-start | bytes 3735560 | tf_op jit(solution)/shard_map/ppermute | solution.py:463
  36.8 3.7 %collective-permute-start.5 = (bf16[38,128,128]{2,1,0:T(8,128)(2,1)}, bf16[38,128,128]{2,1,0:T(8,128)(2,1)}, u32[]{:S(2)}, u32[]{:S(2)}) collective-permute-start(bf16[38,128,128]{2,1,0:T(8,128)(2,1)} %pad_maximum_fusion.own), channel_id=1, source_target_pairs={{1,0},{2,1},{3,2},{0,3},{5,4},{6,5},{7,6},{4,7},{9,8},{10,9},{11,1... | collective-permute-start | bytes 3735560 | tf_op jit(solution)/shard_map/ppermute | solution.py:464
  41.5 4.0 %collective-permute-start = (f32[10,8,128]{2,1,0:T(8,128)}, f32[10,8,128]{2,1,0:T(8,128)}, u32[]{:S(2)}, u32[]{:S(2)}) collective-permute-start(f32[10,8,128]{2,1,0:T(8,128)} %get-tuple-element.42), channel_id=1, source_target_pairs={{8,4},{4,8},{16,12},{12,16},{24,20},{20,24},{32,28},{28,32},{40,36... | collective-permute-start | bytes 122888 | tf_op jit(solution)/shard_map/ppermute | solution.py:443
  45.5 1.9 %collective-permute-start.1 = (f32[10,8,128]{2,1,0:T(8,128)}, f32[10,8,128]{2,1,0:T(8,128)}, u32[]{:S(2)}, u32[]{:S(2)}) collective-permute-start(f32[10,8,128]{2,1,0:T(8,128)} %get-tuple-element.41), channel_id=1, source_target_pairs={{4,0},{0,4},{12,8},{8,12},{20,16},{16,20},{28,24},{24,28},{36,32},... | collective-permute-start | bytes 122888 | tf_op jit(solution)/shard_map/ppermute | solution.py:443
  48.0 18.2 %collective-permute-done.4.left = bf16[38,128,128]{2,1,0:T(8,128)(2,1)} collective-permute-done((bf16[38,128,128]{2,1,0:T(8,128)(2,1)}, bf16[38,128,128]{2,1,0:T(8,128)(2,1)}, u32[]{:S(2)}, u32[]{:S(2)}) %collective-permute-start.4) | collective-permute-done | bytes 1245216 | tf_op jit(solution)/shard_map/ppermute | solution.py:463
  66.3 2.0 %slice.91 = bf16[19,128,128]{2,1,0:T(8,128)(2,1)} slice(bf16[38,128,128]{2,1,0:T(8,128)(2,1)} %collective-permute-done.4.left), slice={[0:19], [0:128], [0:128]} | slice | bytes 1245184 | tf_op jit(solution)/shard_map/slice | solution.py:465
  68.2 2.2 %collective-permute-start.6 = (bf16[19,128,128]{2,1,0:T(8,128)(2,1)}, bf16[19,128,128]{2,1,0:T(8,128)(2,1)}, u32[]{:S(2)}, u32[]{:S(2)}) collective-permute-start(bf16[19,128,128]{2,1,0:T(8,128)(2,1)} %slice.91), channel_id=1, source_target_pairs={{0,1},{1,2},{2,3},{3,0},{4,5},{5,6},{6,7},{7,4},{8,9},{9,10},{10,1... | collective-permute-start | bytes 1867784 | tf_op jit(solution)/shard_map/ppermute | solution.py:465
  70.4 2.0 %slice.92 = bf16[19,128,128]{2,1,0:T(8,128)(2,1)} slice(bf16[38,128,128]{2,1,0:T(8,128)(2,1)} %collective-permute-done.5.right), slice={[19:38], [0:128], [0:128]} | slice | bytes 1245184 | tf_op jit(solution)/shard_map/slice | solution.py:466
  72.4 4.9 %collective-permute-start.7 = (bf16[19,128,128]{2,1,0:T(8,128)(2,1)}, bf16[19,128,128]{2,1,0:T(8,128)(2,1)}, u32[]{:S(2)}, u32[]{:S(2)}) collective-permute-start(bf16[19,128,128]{2,1,0:T(8,128)(2,1)} %slice.92), channel_id=1, source_target_pairs={{1,0},{2,1},{3,2},{0,3},{5,4},{6,5},{7,6},{4,7},{9,8},{10,9},{11,1... | collective-permute-start | bytes 1867784 | tf_op jit(solution)/shard_map/ppermute | solution.py:466
  82.0 4.9 %collective-permute-done.6.far0 = bf16[19,128,128]{2,1,0:T(8,128)(2,1)} collective-permute-done((bf16[19,128,128]{2,1,0:T(8,128)(2,1)}, bf16[19,128,128]{2,1,0:T(8,128)(2,1)}, u32[]{:S(2)}, u32[]{:S(2)}) %collective-permute-start.6) | collective-permute-done | bytes 622624 | tf_op jit(solution)/shard_map/ppermute | solution.py:465
  86.9 3.2 %collective-permute-done.7.far1 = bf16[19,128,128]{2,1,0:T(8,128)(2,1)} collective-permute-done((bf16[19,128,128]{2,1,0:T(8,128)(2,1)}, bf16[19,128,128]{2,1,0:T(8,128)(2,1)}, u32[]{:S(2)}, u32[]{:S(2)}) %collective-permute-start.7) | collective-permute-done | bytes 622624 | tf_op jit(solution)/shard_map/ppermute | solution.py:466
  92.1 6.4 %start.1 = (f32[30,8,128]{2,1,0:T(8,128)S(1)}, bf16[38,512,128]{2,1,0:T(8,128)(2,1)}, bf16[384,4096]{1,0:T(8,128)(2,1)}) custom-call(s32[4]{0:T(128)S(1)} %copy-done.7, s32[128]{0:T(128)S(1)} %copy-done.5, s32[1]{0:T(128)} %bitcast.14.offset, f32[8,4096]{1,0:T(8,128)S(1)} %copy-done, s32[1,4096]{1,0:T(1,128)S(1)} %bitcast.28, ...), custom_call_target="tpu_custom_call" | custom-call | tf_op jit(solution)/shard_map/start/pallas_call | solution.py:252
  99.1 40.5 %all-to-all-done.refs_0_ = bf16[128,72,128]{2,1,0:T(8,128)(2,1)S(1)} async-done(((bf16[128,72,128]{2,1,0:T(8,128)(2,1)}), bf16[128,72,128]{2,1,0:T(8,128)(2,1)S(1)}, u32[]{:S(2)}, u32[]{:S(2)}) %all-to-all-start) | async-done | bytes 2359328 | tf_op jit(solution)/shard_map/all_to_all | solution.py:458
  140.3 1.9 %collective-permute-start.8 = (f32[6,8,128]{2,1,0:T(8,128)S(1)}, f32[6,8,128]{2,1,0:T(8,128)S(1)}, u32[]{:S(2)}, u32[]{:S(2)}) collective-permute-start(f32[6,8,128]{2,1,0:T(8,128)S(1)} %get-tuple-element.23), channel_id=1, source_target_pairs={{4,0},{0,4},{12,8},{8,12},{20,16},{16,20},{28,24},{24,28},{36,32},... | collective-permute-start | bytes 73736 | tf_op jit(solution)/shard_map/ppermute | solution.py:443
  142.3 1.9 %collective-permute-start.9 = (f32[6,8,128]{2,1,0:T(8,128)S(1)}, f32[6,8,128]{2,1,0:T(8,128)S(1)}, u32[]{:S(2)}, u32[]{:S(2)}) collective-permute-start(f32[6,8,128]{2,1,0:T(8,128)S(1)} %get-tuple-element.24), channel_id=1, source_target_pairs={{8,4},{4,8},{16,12},{12,16},{24,20},{20,24},{32,28},{28,32},{40,36... | collective-permute-start | bytes 73736 | tf_op jit(solution)/shard_map/ppermute | solution.py:443
  145.1 2.7 %tracts.1 = (f32[4,32,8,128]{3,2,1,0:T(8,128)S(1)}, bf16[38,512,128]{2,1,0:T(8,128)(2,1)S(1)}) custom-call(bf16[128,72,128]{2,1,0:T(8,128)(2,1)S(1)} %all-to-all-done.refs_0_, bf16[256,2048]{1,0:T(8,128)(2,1)S(1)} %compare_convert_fusion.refs_1_, bf16[38,512,128]{2,1,0:T(8,128)(2,1)} %get-tuple-element.21.refs_2_), custom_call_target="tpu_custom_call" | custom-call | tf_op jit(solution)/shard_map/tracts/pallas_call | solution.py:195
  149.6 4.8 %window.1 = (f32[8,4096]{1,0:T(8,128)}, f32[40,128]{1,0:T(8,128)S(1)}, f32[40,128]{1,0:T(8,128)S(1)}, f32[40,128]{1,0:T(8,128)S(1)}) custom-call(s32[4]{0:T(128)S(1)} %copy-done.8, s32[128]{0:T(128)S(1)} %copy-done.6, s32[1]{0:T(128)} %bitcast.refs_2_, f32[8]{0:T(128)S(1)} %copy-done.9, f32[8]{0:T(128)S(1)} %copy-done.10, f32[8,4096]{1,0:T(8,128)S(1)} %copy-done, ...), custom_call_target="tpu_custom_call" | custom-call | tf_op jit(solution)/shard_map/window/pallas_call | solution.py:387
  154.3 2.8 %collective-permute-start.10 = (f32[40,128]{1,0:T(8,128)S(1)}, f32[40,128]{1,0:T(8,128)S(1)}, u32[]{:S(2)}, u32[]{:S(2)}) collective-permute-start(f32[40,128]{1,0:T(8,128)S(1)} %get-tuple-element.29), channel_id=1, source_target_pairs={{4,0},{0,4},{12,8},{8,12},{20,16},{16,20},{28,24},{24,28},{36,32},... | collective-permute-start | bytes 61448 | tf_op jit(solution)/shard_map/ppermute | solution.py:443
  157.1 3.2 %collective-permute-start.11 = (f32[40,128]{1,0:T(8,128)S(1)}, f32[40,128]{1,0:T(8,128)S(1)}, u32[]{:S(2)}, u32[]{:S(2)}) collective-permute-start(f32[40,128]{1,0:T(8,128)S(1)} %get-tuple-element.30), channel_id=1, source_target_pairs={{8,4},{4,8},{16,12},{12,16},{24,20},{20,24},{32,28},{28,32},{40,36... | collective-permute-start | bytes 61448 | tf_op jit(solution)/shard_map/ppermute | solution.py:443
  160.3 4.0 %collective-permute-done.11 = f32[40,128]{1,0:T(8,128)S(1)} collective-permute-done((f32[40,128]{1,0:T(8,128)S(1)}, f32[40,128]{1,0:T(8,128)S(1)}, u32[]{:S(2)}, u32[]{:S(2)}) %collective-permute-start.11) | collective-permute-done | bytes 20512 | tf_op jit(solution)/shard_map/ppermute | solution.py:443
  (64 shorter events, 16.5 us)
Async XLA Ops:
  1.6 17.5 %collective-permute-start.2 = (bf16[3,128,128]{2,1,0:T(8,128)(2,1)S(1)}, bf16[3,128,128]{2,1,0:T(8,128)(2,1)S(1)}, u32[]{:S(2)}, u32[]{:S(2)}) collective-permute-start(bf16[3,128,128]{2,1,0:T(8,128)(2,1)S(1)} %get-tuple-element.34), channel_id=1, source_target_pairs={{4,0},{0,4},{12,8},{8,12},{20,16},{16,20},{28,24},{24,28},{36,32},... | collective-permute-start | bytes 294920 | tf_op jit(solution)/shard_map/ppermute | solution.py:443
  3.5 15.6 %collective-permute-start.3 = (bf16[3,128,128]{2,1,0:T(8,128)(2,1)S(1)}, bf16[3,128,128]{2,1,0:T(8,128)(2,1)S(1)}, u32[]{:S(2)}, u32[]{:S(2)}) collective-permute-start(bf16[3,128,128]{2,1,0:T(8,128)(2,1)S(1)} %get-tuple-element.33), channel_id=1, source_target_pairs={{8,4},{4,8},{16,12},{12,16},{24,20},{20,24},{32,28},{28,32},{40,36... | collective-permute-start | bytes 294920 | tf_op jit(solution)/shard_map/ppermute | solution.py:443
  19.8 12.4 %copy-start.11 = (bf16[32,1,128,128]{3,2,1,0:T(8,128)(2,1)S(1)}, bf16[32,1,128,128]{3,2,1,0:T(8,128)(2,1)}, u32[]{:S(2)}) copy-start(bf16[32,1,128,128]{3,2,1,0:T(8,128)(2,1)} %param.20) | copy-start | bytes 3145732
  19.8 119.9 %all-to-all-start = ((bf16[128,72,128]{2,1,0:T(8,128)(2,1)}), bf16[128,72,128]{2,1,0:T(8,128)(2,1)S(1)}, u32[]{:S(2)}, u32[]{:S(2)}) async-start(bf16[128,72,128]{2,1,0:T(8,128)(2,1)} %bitcast.29), calls=%async_computation | async-start | bytes 4718592 | tf_op jit(solution)/shard_map/all_to_all | solution.py:458
  32.2 8.3 %copy-start.13 = (s32[32,4]{0,1:T(4,128)S(1)}, s32[32,4]{0,1:T(4,128)}, u32[]{:S(2)}) copy-start(s32[32,4]{0,1:T(4,128)} %param.21) | copy-start | bytes 1540
  32.2 8.5 %copy-start.3 = (f32[4096]{0:T(1024)S(1)}, f32[4096]{0:T(1024)}, u32[]{:S(2)}) copy-start(f32[4096]{0:T(1024)} %param.17) | copy-start | bytes 49156
  32.2 8.5 %copy-start = (f32[8,4096]{1,0:T(8,128)S(1)}, f32[8,4096]{1,0:T(8,128)}, u32[]{:S(2)}) copy-start(f32[8,4096]{1,0:T(8,128)} %refs_5_.1) | copy-start | bytes 393220
  33.4 32.8 %collective-permute-start.4 = (bf16[38,128,128]{2,1,0:T(8,128)(2,1)}, bf16[38,128,128]{2,1,0:T(8,128)(2,1)}, u32[]{:S(2)}, u32[]{:S(2)}) collective-permute-start(bf16[38,128,128]{2,1,0:T(8,128)(2,1)} %pad_maximum_fusion.own), channel_id=1, source_target_pairs={{0,1},{1,2},{2,3},{3,0},{4,5},{5,6},{6,7},{7,4},{8,9},{9,10},{10,1... | collective-permute-start | bytes 3735560 | tf_op jit(solution)/shard_map/ppermute | solution.py:463
  36.8 33.6 %collective-permute-start.5 = (bf16[38,128,128]{2,1,0:T(8,128)(2,1)}, bf16[38,128,128]{2,1,0:T(8,128)(2,1)}, u32[]{:S(2)}, u32[]{:S(2)}) collective-permute-start(bf16[38,128,128]{2,1,0:T(8,128)(2,1)} %pad_maximum_fusion.own), channel_id=1, source_target_pairs={{1,0},{2,1},{3,2},{0,3},{5,4},{6,5},{7,6},{4,7},{9,8},{10,9},{11,1... | collective-permute-start | bytes 3735560 | tf_op jit(solution)/shard_map/ppermute | solution.py:464
  41.5 102.7 %collective-permute-start = (f32[10,8,128]{2,1,0:T(8,128)}, f32[10,8,128]{2,1,0:T(8,128)}, u32[]{:S(2)}, u32[]{:S(2)}) collective-permute-start(f32[10,8,128]{2,1,0:T(8,128)} %get-tuple-element.42), channel_id=1, source_target_pairs={{8,4},{4,8},{16,12},{12,16},{24,20},{20,24},{32,28},{28,32},{40,36... | collective-permute-start | bytes 122888 | tf_op jit(solution)/shard_map/ppermute | solution.py:443
  45.5 98.7 %collective-permute-start.1 = (f32[10,8,128]{2,1,0:T(8,128)}, f32[10,8,128]{2,1,0:T(8,128)}, u32[]{:S(2)}, u32[]{:S(2)}) collective-permute-start(f32[10,8,128]{2,1,0:T(8,128)} %get-tuple-element.41), channel_id=1, source_target_pairs={{4,0},{0,4},{12,8},{8,12},{20,16},{16,20},{28,24},{24,28},{36,32},... | collective-permute-start | bytes 122888 | tf_op jit(solution)/shard_map/ppermute | solution.py:443
  68.2 18.7 %collective-permute-start.6 = (bf16[19,128,128]{2,1,0:T(8,128)(2,1)}, bf16[19,128,128]{2,1,0:T(8,128)(2,1)}, u32[]{:S(2)}, u32[]{:S(2)}) collective-permute-start(bf16[19,128,128]{2,1,0:T(8,128)(2,1)} %slice.91), channel_id=1, source_target_pairs={{0,1},{1,2},{2,3},{3,0},{4,5},{5,6},{6,7},{7,4},{8,9},{9,10},{10,1... | collective-permute-start | bytes 1867784 | tf_op jit(solution)/shard_map/ppermute | solution.py:465
  72.4 17.6 %collective-permute-start.7 = (bf16[19,128,128]{2,1,0:T(8,128)(2,1)}, bf16[19,128,128]{2,1,0:T(8,128)(2,1)}, u32[]{:S(2)}, u32[]{:S(2)}) collective-permute-start(bf16[19,128,128]{2,1,0:T(8,128)(2,1)} %slice.92), channel_id=1, source_target_pairs={{1,0},{2,1},{3,2},{0,3},{5,4},{6,5},{7,6},{4,7},{9,8},{10,9},{11,1... | collective-permute-start | bytes 1867784 | tf_op jit(solution)/shard_map/ppermute | solution.py:466
  140.3 7.4 %collective-permute-start.8 = (f32[6,8,128]{2,1,0:T(8,128)S(1)}, f32[6,8,128]{2,1,0:T(8,128)S(1)}, u32[]{:S(2)}, u32[]{:S(2)}) collective-permute-start(f32[6,8,128]{2,1,0:T(8,128)S(1)} %get-tuple-element.23), channel_id=1, source_target_pairs={{4,0},{0,4},{12,8},{8,12},{20,16},{16,20},{28,24},{24,28},{36,32},... | collective-permute-start | bytes 73736 | tf_op jit(solution)/shard_map/ppermute | solution.py:443
  142.3 7.3 %collective-permute-start.9 = (f32[6,8,128]{2,1,0:T(8,128)S(1)}, f32[6,8,128]{2,1,0:T(8,128)S(1)}, u32[]{:S(2)}, u32[]{:S(2)}) collective-permute-start(f32[6,8,128]{2,1,0:T(8,128)S(1)} %get-tuple-element.24), channel_id=1, source_target_pairs={{8,4},{4,8},{16,12},{12,16},{24,20},{20,24},{32,28},{28,32},{40,36... | collective-permute-start | bytes 73736 | tf_op jit(solution)/shard_map/ppermute | solution.py:443
  145.0 4.5 %copy-start.2 = (f32[30,8,128]{2,1,0:T(8,128)S(1)}, f32[30,8,128]{2,1,0:T(8,128)}, u32[]{:S(2)}) copy-start(f32[30,8,128]{2,1,0:T(8,128)} %copy-done.1) | copy-start | bytes 368644
  145.0 4.5 %copy-start.6 = (s32[128]{0:T(128)S(1)}, s32[128]{0:T(128)}, u32[]{:S(2)}) copy-start(s32[128]{0:T(128)} %reshape.152.index.refs_1_) | copy-start | bytes 1540
  145.0 4.5 %copy-start.8 = (s32[4]{0:T(128)S(1)}, s32[4]{0:T(128)}, u32[]{:S(2)}) copy-start(s32[4]{0:T(128)} %and_select_fusion.2.place.refs_0_) | copy-start | bytes 52
  145.0 4.5 %copy-start.9 = (f32[8]{0:T(128)S(1)}, f32[8]{0:T(128)}, u32[]{:S(2)}) copy-start(f32[8]{0:T(128)} %refs_3_.1) | copy-start | bytes 100
  145.1 4.5 %copy-start.10 = (f32[8]{0:T(128)S(1)}, f32[8]{0:T(128)}, u32[]{:S(2)}) copy-start(f32[8]{0:T(128)} %refs_4_.1) | copy-start | bytes 100
  149.5 14.8 %copy-start.14 = (f32[8,128]{1,0:T(8,128)S(1)}, f32[8,128]{1,0:T(8,128)}, u32[]{:S(2)}) copy-start(f32[8,128]{1,0:T(8,128)} %param.29) | copy-start | bytes 12292
  149.6 14.8 %copy-start.15 = (f32[8,128]{1,0:T(8,128)S(1)}, f32[8,128]{1,0:T(8,128)}, u32[]{:S(2)}) copy-start(f32[8,128]{1,0:T(8,128)} %param.28) | copy-start | bytes 12292
  154.3 6.0 %collective-permute-start.10 = (f32[40,128]{1,0:T(8,128)S(1)}, f32[40,128]{1,0:T(8,128)S(1)}, u32[]{:S(2)}, u32[]{:S(2)}) collective-permute-start(f32[40,128]{1,0:T(8,128)S(1)} %get-tuple-element.29), channel_id=1, source_target_pairs={{4,0},{0,4},{12,8},{8,12},{20,16},{16,20},{28,24},{24,28},{36,32},... | collective-permute-start | bytes 61448 | tf_op jit(solution)/shard_map/ppermute | solution.py:443
  157.1 7.2 %collective-permute-start.11 = (f32[40,128]{1,0:T(8,128)S(1)}, f32[40,128]{1,0:T(8,128)S(1)}, u32[]{:S(2)}, u32[]{:S(2)}) collective-permute-start(f32[40,128]{1,0:T(8,128)S(1)} %get-tuple-element.30), channel_id=1, source_target_pairs={{8,4},{4,8},{16,12},{12,16},{24,20},{20,24},{32,28},{28,32},{40,36... | collective-permute-start | bytes 61448 | tf_op jit(solution)/shard_map/ppermute | solution.py:443
  (5 other events, 3.3 us)

commit v8 on v7

--- a/solution.py
+++ b/solution.py
@@ -273,13 +273,17 @@
 
 
 def window_kernel(
-    patches, place, index, patch, slope, strength, activity, before, after, local, coupling, inner_swap, outer_swap,
+    patches, place, index, patch, slope, strength, activity, inner_edge, outer_edge, local,
+    coupling, inner_swap, outer_swap,
     tiles, drive, kept,
     rate, mine, to_inner, to_outer, frame, sums, parts, hits, names, outer, sems,
 ):
     ext = tiles.shape[0]
     nblk = ext - 2 * EDGE
     near = EDGE + 1
+    even = patch[0] % 2 == 0
+    before = jnp.where(even, outer_edge[...], inner_edge[...])
+    after = jnp.where(even, inner_edge[...], outer_edge[...])
     fetch = pltpu.make_async_copy(kept, hits, sems.at[0])
     fetch.start()
     names[...] = jnp.zeros_like(names)
@@ -301,7 +305,6 @@
         strong = jnp.where(trial == t, strength[t], strong)
     is_first = patch[0] == 0
     is_last = patch[0] == patches - 1
-    even = patch[0] % 2 == 0
 
     def gather(j):
         if j < EDGE:
@@ -442,10 +445,6 @@
     def swap(to_inner, to_outer):
         return lax.ppermute(to_inner, "patch", inner), lax.ppermute(to_outer, "patch", outer)
 
-    def sides(low, high):
-        a, b = swap(jnp.where(even, high, low), jnp.where(even, low, high))
-        return jnp.where(even, b, a), jnp.where(even, a, b)
-
     raw = kernel.reshape(nblk, BLOCK, BLOCK)
     low, high = raw[:EDGE], raw[nblk - EDGE :]
     swapped = swap(jnp.where(even, high, low), jnp.where(even, low, high))
@@ -476,10 +475,9 @@
         rates = blocks[:, at].transpose(1, 0, 2)
         return jnp.concatenate([rates, extra[inner], names[inner]], axis=0)
 
-    before, after = sides(
-        edge(slice(0, near), slice(0, EDGE)),
-        edge(slice(nblk - near, nblk), slice(nblk - EDGE, nblk)),
-    )
+    low = edge(slice(0, near), slice(0, EDGE))
+    high = edge(slice(nblk - near, nblk), slice(nblk - EDGE, nblk))
+    before, after = swap(jnp.where(even, high, low), jnp.where(even, low, high))
     index = kernel_index.reshape(-1)
     here = lax.axis_index("trial").astype(jnp.int32)
     place = (here + jnp.arange(group, dtype=jnp.int32)) % group

time: 167 us -> 167 us (level)
  transfers between devices with their start and end apart: 13 -> 13, of which waited for: 6 -> 6; matrix products, arithmetic and copies ran while one was open for 8% -> 7% of each run, Pallas kernels for 8% -> 8%
where the time goes in v8:
time: 167 us; the launch traced here: 164 us
  waiting for transfers between devices  72.4 us (43%)
  starting transfers between devices  55.1 us (33%)
  Pallas kernels  18.6 us (11%)
  local copies, waits for them, and re-layouts  10.3 us (6%)
  other arithmetic  6.95 us (4%)
    all_to_all x1, waiting for transfers between devices, shards(): got = lax.all_to_all(send, 'patch', split_axis=0, concat_axis=0, tiled=True)  40.5 us
    ppermute x4, starting transfers between devices, swap(): lax.ppermute(to_outer, 'patch', outer)  21.8 us
    ppermute x1, waiting for transfers between devices, shards(): left = lax.ppermute(own, 'trial', clock)  17.3 us
    all_to_all x1, starting transfers between devices, shards(): got = lax.all_to_all(send, 'patch', split_axis=0, concat_axis=0, tiled=True)  11.5 us
    ppermute x4, starting transfers between devices, swap(): lax.ppermute(to_inner, 'patch', inner)  7.72 us
    ppermute x4, waiting for transfers between devices, swap(): lax.ppermute(to_outer, 'patch', outer)  6.56 us
    pallas_call x1, Pallas kernels, start_local(): pl.pallas_call(start_kernel, out_shape=[jax.ShapeDtypeStruct((nblk - 2, T...  6.39 us
    pallas_call x1, Pallas kernels, window(): pl.pallas_call(kernel, out_shape=[jax.ShapeDtypeStruct((TR, nblk * BLOCK)...  5.04 us
  transfers between devices with their start and end apart: 13, of which 6 were waited for; matrix products, arithmetic and copies ran while one was open for 7% of the time, Pallas kernels for 8%

profile of v8, /device:TPU:24, one launch (start us, length us, event | category | flops | bytes accessed | tf_op | source)
XLA Modules:
  0.0 164.5 jit_solution(13635428253256166701)
XLA Ops:
  1.6 1.9 %collective-permute-start.2 = (bf16[3,128,128]{2,1,0:T(8,128)(2,1)S(1)}, bf16[3,128,128]{2,1,0:T(8,128)(2,1)S(1)}, u32[]{:S(2)}, u32[]{:S(2)}) collective-permute-start(bf16[3,128,128]{2,1,0:T(8,128)(2,1)S(1)} %get-tuple-element.34), channel_id=1, source_target_pairs={{4,0},{0,4},{12,8},{8,12},{20,16},{16,20},{28,24},{24,28},{36,32},... | collective-permute-start | bytes 294920 | tf_op jit(solution)/shard_map/ppermute | solution.py:446
  3.5 11.7 %collective-permute-start.3 = (bf16[3,128,128]{2,1,0:T(8,128)(2,1)S(1)}, bf16[3,128,128]{2,1,0:T(8,128)(2,1)S(1)}, u32[]{:S(2)}, u32[]{:S(2)}) collective-permute-start(bf16[3,128,128]{2,1,0:T(8,128)(2,1)S(1)} %get-tuple-element.33), channel_id=1, source_target_pairs={{8,4},{4,8},{16,12},{12,16},{24,20},{20,24},{32,28},{28,32},{40,36... | collective-permute-start | bytes 294920 | tf_op jit(solution)/shard_map/ppermute | solution.py:446
  15.2 3.9 %pack.1 = bf16[128,9,8,128]{3,2,1,0:T(8,128)(2,1)} custom-call(s32[128]{0:T(128)} %bitcast.33, s32[128]{0:T(128)} %source.1, s32[128]{0:T(128)} %delay.1, s32[128]{0:T(128)} %block.1, f32[128]{0:T(128)} %weight.1, bf16[224,8,128]{2,1,0:T(8,128)(2,1)} %bitcast.32), custom_call_target="tpu_custom_call" | custom-call | tf_op jit(solution)/shard_map/pack/pallas_call | solution.py:93
  19.8 11.5 %all-to-all-start = ((bf16[128,72,128]{2,1,0:T(8,128)(2,1)}), bf16[128,72,128]{2,1,0:T(8,128)(2,1)S(1)}, u32[]{:S(2)}, u32[]{:S(2)}) async-start(bf16[128,72,128]{2,1,0:T(8,128)(2,1)} %bitcast.29), calls=%async_computation | async-start | bytes 4718592 | tf_op jit(solution)/shard_map/all_to_all | solution.py:457
  33.4 3.4 %collective-permute-start.4 = (bf16[38,128,128]{2,1,0:T(8,128)(2,1)}, bf16[38,128,128]{2,1,0:T(8,128)(2,1)}, u32[]{:S(2)}, u32[]{:S(2)}) collective-permute-start(bf16[38,128,128]{2,1,0:T(8,128)(2,1)} %pad_maximum_fusion.own), channel_id=1, source_target_pairs={{0,1},{1,2},{2,3},{3,0},{4,5},{5,6},{6,7},{7,4},{8,9},{9,10},{10,1... | collective-permute-start | bytes 3735560 | tf_op jit(solution)/shard_map/ppermute | solution.py:462
  36.8 3.7 %collective-permute-start.5 = (bf16[38,128,128]{2,1,0:T(8,128)(2,1)}, bf16[38,128,128]{2,1,0:T(8,128)(2,1)}, u32[]{:S(2)}, u32[]{:S(2)}) collective-permute-start(bf16[38,128,128]{2,1,0:T(8,128)(2,1)} %pad_maximum_fusion.own), channel_id=1, source_target_pairs={{1,0},{2,1},{3,2},{0,3},{5,4},{6,5},{7,6},{4,7},{9,8},{10,9},{11,1... | collective-permute-start | bytes 3735560 | tf_op jit(solution)/shard_map/ppermute | solution.py:463
  43.4 5.0 %collective-permute-start.1 = (f32[10,8,128]{2,1,0:T(8,128)}, f32[10,8,128]{2,1,0:T(8,128)}, u32[]{:S(2)}, u32[]{:S(2)}) collective-permute-start(f32[10,8,128]{2,1,0:T(8,128)} %get-tuple-element.39), channel_id=1, source_target_pairs={{8,4},{4,8},{16,12},{12,16},{24,20},{20,24},{32,28},{28,32},{40,36... | collective-permute-start | bytes 122888 | tf_op jit(solution)/shard_map/ppermute | solution.py:446
  48.9 17.3 %collective-permute-done.4.left = bf16[38,128,128]{2,1,0:T(8,128)(2,1)} collective-permute-done((bf16[38,128,128]{2,1,0:T(8,128)(2,1)}, bf16[38,128,128]{2,1,0:T(8,128)(2,1)}, u32[]{:S(2)}, u32[]{:S(2)}) %collective-permute-start.4) | collective-permute-done | bytes 1245216 | tf_op jit(solution)/shard_map/ppermute | solution.py:462
  66.3 2.0 %slice.91 = bf16[19,128,128]{2,1,0:T(8,128)(2,1)} slice(bf16[38,128,128]{2,1,0:T(8,128)(2,1)} %collective-permute-done.4.left), slice={[0:19], [0:128], [0:128]} | slice | bytes 1245184 | tf_op jit(solution)/shard_map/slice | solution.py:464
  68.2 2.2 %collective-permute-start.6 = (bf16[19,128,128]{2,1,0:T(8,128)(2,1)}, bf16[19,128,128]{2,1,0:T(8,128)(2,1)}, u32[]{:S(2)}, u32[]{:S(2)}) collective-permute-start(bf16[19,128,128]{2,1,0:T(8,128)(2,1)} %slice.91), channel_id=1, source_target_pairs={{0,1},{1,2},{2,3},{3,0},{4,5},{5,6},{6,7},{7,4},{8,9},{9,10},{10,1... | collective-permute-start | bytes 1867784 | tf_op jit(solution)/shard_map/ppermute | solution.py:464
  70.4 2.0 %slice.92 = bf16[19,128,128]{2,1,0:T(8,128)(2,1)} slice(bf16[38,128,128]{2,1,0:T(8,128)(2,1)} %collective-permute-done.5.right), slice={[19:38], [0:128], [0:128]} | slice | bytes 1245184 | tf_op jit(solution)/shard_map/slice | solution.py:465
  72.4 4.9 %collective-permute-start.7 = (bf16[19,128,128]{2,1,0:T(8,128)(2,1)}, bf16[19,128,128]{2,1,0:T(8,128)(2,1)}, u32[]{:S(2)}, u32[]{:S(2)}) collective-permute-start(bf16[19,128,128]{2,1,0:T(8,128)(2,1)} %slice.92), channel_id=1, source_target_pairs={{1,0},{2,1},{3,2},{0,3},{5,4},{6,5},{7,6},{4,7},{9,8},{10,9},{11,1... | collective-permute-start | bytes 1867784 | tf_op jit(solution)/shard_map/ppermute | solution.py:465
  82.0 4.9 %collective-permute-done.6.far0 = bf16[19,128,128]{2,1,0:T(8,128)(2,1)} collective-permute-done((bf16[19,128,128]{2,1,0:T(8,128)(2,1)}, bf16[19,128,128]{2,1,0:T(8,128)(2,1)}, u32[]{:S(2)}, u32[]{:S(2)}) %collective-permute-start.6) | collective-permute-done | bytes 622624 | tf_op jit(solution)/shard_map/ppermute | solution.py:464
  86.9 3.2 %collective-permute-done.7.far1 = bf16[19,128,128]{2,1,0:T(8,128)(2,1)} collective-permute-done((bf16[19,128,128]{2,1,0:T(8,128)(2,1)}, bf16[19,128,128]{2,1,0:T(8,128)(2,1)}, u32[]{:S(2)}, u32[]{:S(2)}) %collective-permute-start.7) | collective-permute-done | bytes 622624 | tf_op jit(solution)/shard_map/ppermute | solution.py:465
  92.1 6.4 %start.1 = (f32[30,8,128]{2,1,0:T(8,128)S(1)}, bf16[38,512,128]{2,1,0:T(8,128)(2,1)}, bf16[384,4096]{1,0:T(8,128)(2,1)}) custom-call(s32[4]{0:T(128)S(1)} %copy-done.7, s32[128]{0:T(128)S(1)} %copy-done.5, s32[1]{0:T(128)} %bitcast.14.offset, f32[8,4096]{1,0:T(8,128)S(1)} %copy-done, s32[1,4096]{1,0:T(1,128)S(1)} %bitcast.28, ...), custom_call_target="tpu_custom_call" | custom-call | tf_op jit(solution)/shard_map/start/pallas_call | solution.py:252
  99.2 40.5 %all-to-all-done.refs_0_ = bf16[128,72,128]{2,1,0:T(8,128)(2,1)S(1)} async-done(((bf16[128,72,128]{2,1,0:T(8,128)(2,1)}), bf16[128,72,128]{2,1,0:T(8,128)(2,1)S(1)}, u32[]{:S(2)}, u32[]{:S(2)}) %all-to-all-start) | async-done | bytes 2359328 | tf_op jit(solution)/shard_map/all_to_all | solution.py:457
  140.3 1.9 %collective-permute-start.8 = (f32[6,8,128]{2,1,0:T(8,128)S(1)}, f32[6,8,128]{2,1,0:T(8,128)S(1)}, u32[]{:S(2)}, u32[]{:S(2)}) collective-permute-start(f32[6,8,128]{2,1,0:T(8,128)S(1)} %get-tuple-element.23), channel_id=1, source_target_pairs={{4,0},{0,4},{12,8},{8,12},{20,16},{16,20},{28,24},{24,28},{36,32},... | collective-permute-start | bytes 73736 | tf_op jit(solution)/shard_map/ppermute | solution.py:446
  142.3 1.9 %collective-permute-start.9 = (f32[6,8,128]{2,1,0:T(8,128)S(1)}, f32[6,8,128]{2,1,0:T(8,128)S(1)}, u32[]{:S(2)}, u32[]{:S(2)}) collective-permute-start(f32[6,8,128]{2,1,0:T(8,128)S(1)} %get-tuple-element.24), channel_id=1, source_target_pairs={{8,4},{4,8},{16,12},{12,16},{24,20},{20,24},{32,28},{28,32},{40,36... | collective-permute-start | bytes 73736 | tf_op jit(solution)/shard_map/ppermute | solution.py:446
  144.2 2.7 %tracts.1 = (f32[4,32,8,128]{3,2,1,0:T(8,128)S(1)}, bf16[38,512,128]{2,1,0:T(8,128)(2,1)S(1)}) custom-call(bf16[128,72,128]{2,1,0:T(8,128)(2,1)S(1)} %all-to-all-done.refs_0_, bf16[256,2048]{1,0:T(8,128)(2,1)S(1)} %compare_convert_fusion.refs_1_, bf16[38,512,128]{2,1,0:T(8,128)(2,1)} %get-tuple-element.21.refs_2_), custom_call_target="tpu_custom_call" | custom-call | tf_op jit(solution)/shard_map/tracts/pallas_call | solution.py:195
  147.0 2.6 %collective-permute-done.9.refs_11_ = f32[6,8,128]{2,1,0:T(8,128)S(1)} collective-permute-done((f32[6,8,128]{2,1,0:T(8,128)S(1)}, f32[6,8,128]{2,1,0:T(8,128)S(1)}, u32[]{:S(2)}, u32[]{:S(2)}) %collective-permute-start.9) | collective-permute-done | bytes 24608 | tf_op jit(solution)/shard_map/ppermute | solution.py:446
  149.6 5.0 %window.1 = (f32[8,4096]{1,0:T(8,128)}, f32[40,128]{1,0:T(8,128)S(1)}, f32[40,128]{1,0:T(8,128)S(1)}, f32[40,128]{1,0:T(8,128)S(1)}) custom-call(s32[4]{0:T(128)S(1)} %copy-done.8, s32[128]{0:T(128)S(1)} %copy-done.6, s32[1]{0:T(128)} %bitcast.refs_2_, f32[8]{0:T(128)S(1)} %copy-done.9, f32[8]{0:T(128)S(1)} %copy-done.10, f32[8,4096]{1,0:T(8,128)S(1)} %copy-done, ...), custom_call_target="tpu_custom_call" | custom-call | tf_op jit(solution)/shard_map/window/pallas_call | solution.py:390
  154.6 2.0 %collective-permute-start.10 = (f32[40,128]{1,0:T(8,128)S(1)}, f32[40,128]{1,0:T(8,128)S(1)}, u32[]{:S(2)}, u32[]{:S(2)}) collective-permute-start(f32[40,128]{1,0:T(8,128)S(1)} %get-tuple-element.29), channel_id=1, source_target_pairs={{4,0},{0,4},{12,8},{8,12},{20,16},{16,20},{28,24},{24,28},{36,32},... | collective-permute-start | bytes 61448 | tf_op jit(solution)/shard_map/ppermute | solution.py:446
  156.6 3.2 %collective-permute-start.11 = (f32[40,128]{1,0:T(8,128)S(1)}, f32[40,128]{1,0:T(8,128)S(1)}, u32[]{:S(2)}, u32[]{:S(2)}) collective-permute-start(f32[40,128]{1,0:T(8,128)S(1)} %get-tuple-element.30), channel_id=1, source_target_pairs={{8,4},{4,8},{16,12},{12,16},{24,20},{20,24},{32,28},{28,32},{40,36... | collective-permute-start | bytes 61448 | tf_op jit(solution)/shard_map/ppermute | solution.py:446
  159.8 4.0 %collective-permute-done.11 = f32[40,128]{1,0:T(8,128)S(1)} collective-permute-done((f32[40,128]{1,0:T(8,128)S(1)}, f32[40,128]{1,0:T(8,128)S(1)}, u32[]{:S(2)}, u32[]{:S(2)}) %collective-permute-start.11) | collective-permute-done | bytes 20512 | tf_op jit(solution)/shard_map/ppermute | solution.py:446
  (63 shorter events, 15.9 us)
Async XLA Ops:
  1.6 17.5 %collective-permute-start.2 = (bf16[3,128,128]{2,1,0:T(8,128)(2,1)S(1)}, bf16[3,128,128]{2,1,0:T(8,128)(2,1)S(1)}, u32[]{:S(2)}, u32[]{:S(2)}) collective-permute-start(bf16[3,128,128]{2,1,0:T(8,128)(2,1)S(1)} %get-tuple-element.34), channel_id=1, source_target_pairs={{4,0},{0,4},{12,8},{8,12},{20,16},{16,20},{28,24},{24,28},{36,32},... | collective-permute-start | bytes 294920 | tf_op jit(solution)/shard_map/ppermute | solution.py:446
  3.5 15.6 %collective-permute-start.3 = (bf16[3,128,128]{2,1,0:T(8,128)(2,1)S(1)}, bf16[3,128,128]{2,1,0:T(8,128)(2,1)S(1)}, u32[]{:S(2)}, u32[]{:S(2)}) collective-permute-start(bf16[3,128,128]{2,1,0:T(8,128)(2,1)S(1)} %get-tuple-element.33), channel_id=1, source_target_pairs={{8,4},{4,8},{16,12},{12,16},{24,20},{20,24},{32,28},{28,32},{40,36... | collective-permute-start | bytes 294920 | tf_op jit(solution)/shard_map/ppermute | solution.py:446
  19.8 12.4 %copy-start.11 = (bf16[32,1,128,128]{3,2,1,0:T(8,128)(2,1)S(1)}, bf16[32,1,128,128]{3,2,1,0:T(8,128)(2,1)}, u32[]{:S(2)}) copy-start(bf16[32,1,128,128]{3,2,1,0:T(8,128)(2,1)} %param.20) | copy-start | bytes 3145732
  19.8 119.9 %all-to-all-start = ((bf16[128,72,128]{2,1,0:T(8,128)(2,1)}), bf16[128,72,128]{2,1,0:T(8,128)(2,1)S(1)}, u32[]{:S(2)}, u32[]{:S(2)}) async-start(bf16[128,72,128]{2,1,0:T(8,128)(2,1)} %bitcast.29), calls=%async_computation | async-start | bytes 4718592 | tf_op jit(solution)/shard_map/all_to_all | solution.py:457
  32.2 8.3 %copy-start.13 = (s32[32,4]{0,1:T(4,128)S(1)}, s32[32,4]{0,1:T(4,128)}, u32[]{:S(2)}) copy-start(s32[32,4]{0,1:T(4,128)} %param.21) | copy-start | bytes 1540
  32.2 8.5 %copy-start.3 = (f32[4096]{0:T(1024)S(1)}, f32[4096]{0:T(1024)}, u32[]{:S(2)}) copy-start(f32[4096]{0:T(1024)} %param.17) | copy-start | bytes 49156
  32.2 8.5 %copy-start = (f32[8,4096]{1,0:T(8,128)S(1)}, f32[8,4096]{1,0:T(8,128)}, u32[]{:S(2)}) copy-start(f32[8,4096]{1,0:T(8,128)} %refs_5_.1) | copy-start | bytes 393220
  33.4 32.8 %collective-permute-start.4 = (bf16[38,128,128]{2,1,0:T(8,128)(2,1)}, bf16[38,128,128]{2,1,0:T(8,128)(2,1)}, u32[]{:S(2)}, u32[]{:S(2)}) collective-permute-start(bf16[38,128,128]{2,1,0:T(8,128)(2,1)} %pad_maximum_fusion.own), channel_id=1, source_target_pairs={{0,1},{1,2},{2,3},{3,0},{4,5},{5,6},{6,7},{7,4},{8,9},{9,10},{10,1... | collective-permute-start | bytes 3735560 | tf_op jit(solution)/shard_map/ppermute | solution.py:462
  36.8 33.6 %collective-permute-start.5 = (bf16[38,128,128]{2,1,0:T(8,128)(2,1)}, bf16[38,128,128]{2,1,0:T(8,128)(2,1)}, u32[]{:S(2)}, u32[]{:S(2)}) collective-permute-start(bf16[38,128,128]{2,1,0:T(8,128)(2,1)} %pad_maximum_fusion.own), channel_id=1, source_target_pairs={{1,0},{2,1},{3,2},{0,3},{5,4},{6,5},{7,6},{4,7},{9,8},{10,9},{11,1... | collective-permute-start | bytes 3735560 | tf_op jit(solution)/shard_map/ppermute | solution.py:463
  41.4 105.5 %collective-permute-start = (f32[10,8,128]{2,1,0:T(8,128)}, f32[10,8,128]{2,1,0:T(8,128)}, u32[]{:S(2)}, u32[]{:S(2)}) collective-permute-start(f32[10,8,128]{2,1,0:T(8,128)} %get-tuple-element.40), channel_id=1, source_target_pairs={{4,0},{0,4},{12,8},{8,12},{20,16},{16,20},{28,24},{24,28},{36,32},... | collective-permute-start | bytes 122888 | tf_op jit(solution)/shard_map/ppermute | solution.py:446
  43.4 103.6 %collective-permute-start.1 = (f32[10,8,128]{2,1,0:T(8,128)}, f32[10,8,128]{2,1,0:T(8,128)}, u32[]{:S(2)}, u32[]{:S(2)}) collective-permute-start(f32[10,8,128]{2,1,0:T(8,128)} %get-tuple-element.39), channel_id=1, source_target_pairs={{8,4},{4,8},{16,12},{12,16},{24,20},{20,24},{32,28},{28,32},{40,36... | collective-permute-start | bytes 122888 | tf_op jit(solution)/shard_map/ppermute | solution.py:446
  68.2 18.7 %collective-permute-start.6 = (bf16[19,128,128]{2,1,0:T(8,128)(2,1)}, bf16[19,128,128]{2,1,0:T(8,128)(2,1)}, u32[]{:S(2)}, u32[]{:S(2)}) collective-permute-start(bf16[19,128,128]{2,1,0:T(8,128)(2,1)} %slice.91), channel_id=1, source_target_pairs={{0,1},{1,2},{2,3},{3,0},{4,5},{5,6},{6,7},{7,4},{8,9},{9,10},{10,1... | collective-permute-start | bytes 1867784 | tf_op jit(solution)/shard_map/ppermute | solution.py:464
  72.4 17.6 %collective-permute-start.7 = (bf16[19,128,128]{2,1,0:T(8,128)(2,1)}, bf16[19,128,128]{2,1,0:T(8,128)(2,1)}, u32[]{:S(2)}, u32[]{:S(2)}) collective-permute-start(bf16[19,128,128]{2,1,0:T(8,128)(2,1)} %slice.92), channel_id=1, source_target_pairs={{1,0},{2,1},{3,2},{0,3},{5,4},{6,5},{7,6},{4,7},{9,8},{10,9},{11,1... | collective-permute-start | bytes 1867784 | tf_op jit(solution)/shard_map/ppermute | solution.py:465
  140.3 6.6 %collective-permute-start.8 = (f32[6,8,128]{2,1,0:T(8,128)S(1)}, f32[6,8,128]{2,1,0:T(8,128)S(1)}, u32[]{:S(2)}, u32[]{:S(2)}) collective-permute-start(f32[6,8,128]{2,1,0:T(8,128)S(1)} %get-tuple-element.23), channel_id=1, source_target_pairs={{4,0},{0,4},{12,8},{8,12},{20,16},{16,20},{28,24},{24,28},{36,32},... | collective-permute-start | bytes 73736 | tf_op jit(solution)/shard_map/ppermute | solution.py:446
  142.3 7.3 %collective-permute-start.9 = (f32[6,8,128]{2,1,0:T(8,128)S(1)}, f32[6,8,128]{2,1,0:T(8,128)S(1)}, u32[]{:S(2)}, u32[]{:S(2)}) collective-permute-start(f32[6,8,128]{2,1,0:T(8,128)S(1)} %get-tuple-element.24), channel_id=1, source_target_pairs={{8,4},{4,8},{16,12},{12,16},{24,20},{20,24},{32,28},{28,32},{40,36... | collective-permute-start | bytes 73736 | tf_op jit(solution)/shard_map/ppermute | solution.py:446
  144.2 5.3 %copy-start.2 = (f32[30,8,128]{2,1,0:T(8,128)S(1)}, f32[30,8,128]{2,1,0:T(8,128)}, u32[]{:S(2)}) copy-start(f32[30,8,128]{2,1,0:T(8,128)} %copy-done.1) | copy-start | bytes 368644
  144.2 5.3 %copy-start.6 = (s32[128]{0:T(128)S(1)}, s32[128]{0:T(128)}, u32[]{:S(2)}) copy-start(s32[128]{0:T(128)} %reshape.152.index.refs_1_) | copy-start | bytes 1540
  144.2 5.3 %copy-start.8 = (s32[4]{0:T(128)S(1)}, s32[4]{0:T(128)}, u32[]{:S(2)}) copy-start(s32[4]{0:T(128)} %and_select_fusion.2.place.refs_0_) | copy-start | bytes 52
  144.2 5.3 %copy-start.9 = (f32[8]{0:T(128)S(1)}, f32[8]{0:T(128)}, u32[]{:S(2)}) copy-start(f32[8]{0:T(128)} %refs_3_.1) | copy-start | bytes 100
  144.2 5.3 %copy-start.10 = (f32[8]{0:T(128)S(1)}, f32[8]{0:T(128)}, u32[]{:S(2)}) copy-start(f32[8]{0:T(128)} %refs_4_.1) | copy-start | bytes 100
  149.5 14.3 %copy-start.14 = (f32[8,128]{1,0:T(8,128)S(1)}, f32[8,128]{1,0:T(8,128)}, u32[]{:S(2)}) copy-start(f32[8,128]{1,0:T(8,128)} %param.29) | copy-start | bytes 12292
  149.6 14.3 %copy-start.15 = (f32[8,128]{1,0:T(8,128)S(1)}, f32[8,128]{1,0:T(8,128)}, u32[]{:S(2)}) copy-start(f32[8,128]{1,0:T(8,128)} %param.28) | copy-start | bytes 12292
  154.6 5.2 %collective-permute-start.10 = (f32[40,128]{1,0:T(8,128)S(1)}, f32[40,128]{1,0:T(8,128)S(1)}, u32[]{:S(2)}, u32[]{:S(2)}) collective-permute-start(f32[40,128]{1,0:T(8,128)S(1)} %get-tuple-element.29), channel_id=1, source_target_pairs={{4,0},{0,4},{12,8},{8,12},{20,16},{16,20},{28,24},{24,28},{36,32},... | collective-permute-start | bytes 61448 | tf_op jit(solution)/shard_map/ppermute | solution.py:446
  156.6 7.2 %collective-permute-start.11 = (f32[40,128]{1,0:T(8,128)S(1)}, f32[40,128]{1,0:T(8,128)S(1)}, u32[]{:S(2)}, u32[]{:S(2)}) collective-permute-start(f32[40,128]{1,0:T(8,128)S(1)} %get-tuple-element.30), channel_id=1, source_target_pairs={{8,4},{4,8},{16,12},{12,16},{24,20},{20,24},{32,28},{28,32},{40,36... | collective-permute-start | bytes 61448 | tf_op jit(solution)/shard_map/ppermute | solution.py:446
  (5 other events, 3.3 us)
